TPU v7x, 32 devices: a whole 2x2x4 slice. The times are simulated.
32 devices in a mesh: dp: 8 (over z, y), head: 4 (over x, core).
Axes of the slice: x: 2, y: 2, z: 4, core: 2. Of those that a mesh axis runs over, the one named last changes fastest.
Arguments:
- tokens: bfloat16 [24576, 768], P(('dp', 'head')), may hold values from -15 to 15
- segment_ids: int32 [24576], P('dp'), may hold values from 0 to 189, as said below
- cotangent: bfloat16 [24576, 768], P(('dp', 'head')), may hold values from -6 to 6
- clip_norm: float32 [1], replicated, as said below
- master_qkv: float32 [768, 2304], P('dp'), may hold values from -0.21875 to 0.21875
- master_out: float32 [768, 768], P('dp'), may hold values from -0.875 to 0.875
- master_gu: float32 [768, 6144], P('dp'), may hold values from -0.72168784 to 0.72168784
- master_down: float32 [3072, 768], P('dp'), may hold values from -0.109375 to 0.109375
- master_vec: float32 [6, 768], P(None, 'dp')
- first_qkv: float32 [768, 2304], P('dp')
- first_out: float32 [768, 768], P('dp')
- first_gu: float32 [768, 6144], P('dp')
- first_down: float32 [3072, 768], P('dp')
- first_vec: float32 [6, 768], P(None, 'dp')
- second_qkv: float32 [768, 2304], P('dp'), as said below
- second_out: float32 [768, 768], P('dp'), as said below
- second_gu: float32 [768, 6144], P('dp'), as said below
- second_down: float32 [3072, 768], P('dp'), as said below
- second_vec: float32 [6, 768], P(None, 'dp'), as said below
Outputs:
- output: bfloat16 [24576, 768], P(('dp', 'head'))
- grad_input: float32 [24576, 768], P(('dp', 'head'))
- new_qkv: float32 [768, 2304], P('dp')
- moment1_qkv: float32 [768, 2304], P('dp')
- moment2_qkv: float32 [768, 2304], P('dp')
- copy_qkv: bfloat16 [768, 2304], P('dp')
- new_out: float32 [768, 768], P('dp')
- moment1_out: float32 [768, 768], P('dp')
- moment2_out: float32 [768, 768], P('dp')
- copy_out: bfloat16 [768, 768], P('dp')
- new_gu: float32 [768, 6144], P('dp')
- moment1_gu: float32 [768, 6144], P('dp')
- moment2_gu: float32 [768, 6144], P('dp')
- copy_gu: bfloat16 [768, 6144], P('dp')
- new_down: float32 [3072, 768], P('dp')
- moment1_down: float32 [3072, 768], P('dp')
- moment2_down: float32 [3072, 768], P('dp')
- copy_down: bfloat16 [3072, 768], P('dp')
- new_vec: float32 [6, 768], P(None, 'dp')
- moment1_vec: float32 [6, 768], P(None, 'dp')
- moment2_vec: float32 [6, 768], P(None, 'dp')
- copy_vec: bfloat16 [6, 768], P(None, 'dp')
- grad_norm: float32 [1], replicated
Inputs may be any that keep to these rules, and one draw needn't show every extreme that they name: `segment_ids`: ids never fall; each aligned block of 1024 tokens holds whole sequences of 128, 256 or 512 tokens, and no id appears in two blocks; block k's ids lie within 8 * k to 8 * k + 5. `clip_norm`: Positive. `second_qkv`: Positive. `second_out`: Positive. `second_gu`: Positive. `second_down`: Positive. `second_vec`: Positive.
All inputs are finite; a program needn't handle non-finite values.
Results may differ from a plain program's by a relative error of at most 0.019.
The roundings to bfloat16 on the way count: a program that leaves them out, or rounds other values in their place, can miss the bound.
Values may be sent and summed in bfloat16 or wider, within the bound.
No kernel may reach another device: no remote copies, remote signals or barrier semaphores. Data moves between devices by JAX's collectives and lax.ppermute only.
A program may use at most 192 MiB of HBM per device.

v0:
```python
import jax
import jax.numpy as jnp
import numpy as np
from jax import lax
from jax.sharding import PartitionSpec as P

HEADS = 12
HEAD_DIM = 64
PACK = 1024


SLOPES = [2.0 ** (-(level + 1)) for level in range(8)] + [
    2.0 ** (-(level + 0.5)) for level in range(4)
]
LN_EPS = 1e-05
BETA_ONE = 0.9
BETA_TWO = 0.999
ADAM_EPS = 1e-08
CORR_ONE = 1.0 - 0.9**10
CORR_TWO = 1.0 - 0.999**10
RATE_MAT = 0.05
RATE_VEC = 0.5
DECAY_MAT = 0.01


def layer_norm(hidden, gain_vec, shift_vec):
    center = hidden - jnp.mean(hidden, axis=-1, keepdims=True)
    spread = jnp.mean(center * center, axis=-1, keepdims=True)
    return center * lax.rsqrt(spread + LN_EPS) * gain_vec + shift_vec


def gating(joined):
    half_width = joined.shape[-1] // 2
    return jax.nn.gelu(joined[:, :half_width], approximate=False) * joined[:, half_width:]


def contract_rows(left_rows, right_rows):
    return lax.dot_general(
        left_rows, right_rows, (((0,), (0,)), ((), ())), preferred_element_type=jnp.float32
    )


def times_transposed(left_rows, weight):
    return lax.dot_general(
        left_rows, weight, (((1,), (1,)), ((), ())), preferred_element_type=jnp.float32
    )


def adam_update(master, first_mom, second, grad_term, factor, step_rate, decay_rate):
    clipped = grad_term * factor
    first_new = BETA_ONE * first_mom + (1.0 - BETA_ONE) * clipped
    second_new = BETA_TWO * second + (1.0 - BETA_TWO) * clipped * clipped
    direction = first_new / CORR_ONE / (jnp.sqrt(second_new / CORR_TWO) + ADAM_EPS)
    master_new = master - step_rate * (direction + decay_rate * master)
    return (master_new, first_new, second_new, master_new.astype(jnp.bfloat16))


def pack_scores(queries, keys_part, seg_pack, slopes_local, score_scale):
    scores = (
        jnp.einsum("qhd,khd->hqk", queries, keys_part, preferred_element_type=jnp.float32)
        * score_scale
    )
    positions = jnp.arange(seg_pack.shape[0]).astype(jnp.float32)
    distance = jnp.abs(positions[:, None] - positions[None, :])
    same_seq = seg_pack[:, None] == seg_pack[None, :]
    return jnp.where(
        same_seq[None], scores - slopes_local[:, None, None] * distance[None], -1000000000.0
    )


def body(
    tokens,
    segment_ids,
    cotangent,
    clip_norm,
    master_qkv,
    master_out,
    master_gu,
    master_down,
    master_vec,
    first_qkv,
    first_out,
    first_gu,
    first_down,
    first_vec,
    second_qkv,
    second_out,
    second_gu,
    second_down,
    second_vec,
):
    groups = lax.axis_size("head")
    heads_local = HEADS // groups
    group_width = heads_local * HEAD_DIM
    tok_rows = tokens.shape[0]
    model_width = tokens.shape[1]
    score_scale = HEAD_DIM ** (-0.5)
    low_qkv = master_qkv.astype(jnp.bfloat16)
    low_out = master_out.astype(jnp.bfloat16)
    low_gu = master_gu.astype(jnp.bfloat16)
    low_down = master_down.astype(jnp.bfloat16)
    low_vec = master_vec.astype(jnp.bfloat16)
    full_qkv, full_out, full_gu, full_down, full_vec = (
        lax.all_gather(low_qkv, "dp", axis=0, tiled=True),
        lax.all_gather(low_out, "dp", axis=0, tiled=True),
        lax.all_gather(low_gu, "dp", axis=0, tiled=True),
        lax.all_gather(low_down, "dp", axis=0, tiled=True),
        lax.all_gather(low_vec, "dp", axis=1, tiled=True),
    )
    vectors = full_vec.astype(jnp.float32)
    slopes_local = lax.dynamic_slice_in_dim(
        jnp.asarray(np.array(SLOPES), jnp.float32),
        lax.axis_index("head") * heads_local,
        heads_local,
    )
    joined = jnp.dot(tokens, full_qkv, preferred_element_type=jnp.float32).astype(jnp.bfloat16)
    regrouped = lax.all_to_all(
        joined.reshape(tok_rows, 3, groups, group_width),
        "head",
        split_axis=2,
        concat_axis=0,
        tiled=True,
    )
    group_rows = regrouped.shape[0]
    pack_count = group_rows // PACK
    by_pack = regrouped.reshape(pack_count, PACK, 3, heads_local, HEAD_DIM)
    seg_packs = segment_ids.reshape(pack_count, PACK)

    def forward_pack(pieces):
        pack_block, seg_pack = pieces
        scores = pack_scores(
            pack_block[:, 0], pack_block[:, 1], seg_pack, slopes_local, score_scale
        )
        row_peak = jnp.max(scores, axis=-1, keepdims=True)
        exp_terms = jnp.exp(scores - row_peak)
        row_total = jnp.sum(exp_terms, axis=-1, keepdims=True)
        soft_weights = (exp_terms / row_total).astype(jnp.bfloat16)
        context = jnp.einsum(
            "hqk,khd->qhd", soft_weights, pack_block[:, 2], preferred_element_type=jnp.float32
        )
        return (
            context.astype(jnp.bfloat16).reshape(PACK, group_width),
            (row_peak + jnp.log(row_total))[..., 0],
        )

    context_packs, log_totals = lax.map(forward_pack, (by_pack, seg_packs))
    context_back = lax.all_to_all(
        context_packs.reshape(group_rows, 1, group_width),
        "head",
        split_axis=0,
        concat_axis=1,
        tiled=True,
    )
    context_rows = context_back.reshape(tok_rows, model_width)
    inputs = tokens.astype(jnp.float32)
    attn_out = jnp.dot(context_rows, full_out, preferred_element_type=jnp.float32)
    first_sum = inputs + attn_out + vectors[4]
    normed_one, norm_one_pull = jax.vjp(layer_norm, first_sum, vectors[0], vectors[1])
    normed_low = normed_one.astype(jnp.bfloat16)
    gate_up = jnp.dot(normed_low, full_gu, preferred_element_type=jnp.float32)
    hidden_full, gating_pull = jax.vjp(gating, gate_up)
    hidden_low = hidden_full.astype(jnp.bfloat16)
    ffn_out = jnp.dot(hidden_low, full_down, preferred_element_type=jnp.float32)
    second_sum = normed_one + ffn_out + vectors[5]
    result, norm_two_pull = jax.vjp(layer_norm, second_sum, vectors[2], vectors[3])
    grad_second, grad_gain_two, grad_shift_two = norm_two_pull(cotangent.astype(jnp.float32))
    grad_bias_down = jnp.sum(grad_second, axis=0)
    grad_ffn_low = grad_second.astype(jnp.bfloat16)
    grad_down = contract_rows(hidden_low, grad_ffn_low)
    grad_hidden = times_transposed(grad_ffn_low, full_down)
    (grad_joined_full,) = gating_pull(grad_hidden)
    grad_gate_up = grad_joined_full.astype(jnp.bfloat16)
    grad_gu = contract_rows(normed_low, grad_gate_up)
    grad_normed = grad_second + times_transposed(grad_gate_up, full_gu)
    grad_first, grad_gain_one, grad_shift_one = norm_one_pull(grad_normed)
    grad_bias_out = jnp.sum(grad_first, axis=0)
    grad_attn_low = grad_first.astype(jnp.bfloat16)
    grad_out = contract_rows(context_rows, grad_attn_low)
    grad_context = times_transposed(grad_attn_low, full_out).astype(jnp.bfloat16)
    grad_context_group = lax.all_to_all(
        grad_context.reshape(tok_rows, groups, group_width),
        "head",
        split_axis=1,
        concat_axis=0,
        tiled=True,
    )
    grad_packs = grad_context_group.reshape(pack_count, PACK, heads_local, HEAD_DIM)

    def backward_pack(pieces):
        pack_block, seg_pack, log_total, grad_ctx = pieces
        queries = pack_block[:, 0]
        keys_part = pack_block[:, 1]
        values_part = pack_block[:, 2]
        scores = pack_scores(queries, keys_part, seg_pack, slopes_local, score_scale)
        soft_full = jnp.exp(scores - log_total[..., None])
        grad_soft = jnp.einsum(
            "qhd,khd->hqk", grad_ctx, values_part, preferred_element_type=jnp.float32
        )
        grad_values = jnp.einsum(
            "hqk,qhd->khd",
            soft_full.astype(jnp.bfloat16),
            grad_ctx,
            preferred_element_type=jnp.float32,
        )
        row_inner = jnp.sum(soft_full * grad_soft, axis=-1, keepdims=True)
        grad_scores = (soft_full * (grad_soft - row_inner)).astype(jnp.bfloat16)
        grad_queries = (
            jnp.einsum("hqk,khd->qhd", grad_scores, keys_part, preferred_element_type=jnp.float32)
            * score_scale
        )
        grad_keys = (
            jnp.einsum("hqk,qhd->khd", grad_scores, queries, preferred_element_type=jnp.float32)
            * score_scale
        )
        stacked = jnp.stack((grad_queries, grad_keys, grad_values), axis=1).astype(jnp.bfloat16)
        return stacked.reshape(PACK, 3, group_width)

    grad_blocks = lax.map(backward_pack, (by_pack, seg_packs, log_totals, grad_packs))
    grad_joined = lax.all_to_all(
        grad_blocks.reshape(group_rows, 3, 1, group_width),
        "head",
        split_axis=0,
        concat_axis=2,
        tiled=True,
    )
    grad_joined_rows = grad_joined.reshape(tok_rows, 3 * model_width)
    grad_qkv = contract_rows(tokens, grad_joined_rows)
    grad_input = grad_first + times_transposed(grad_joined_rows, full_qkv)
    grad_vec = jnp.stack(
        (
            grad_gain_one,
            grad_shift_one,
            grad_gain_two,
            grad_shift_two,
            grad_bias_out,
            grad_bias_down,
        )
    )
    shard_qkv, shard_out, shard_gu, shard_down, shard_vec = (
        lax.psum_scatter(grad_qkv, "dp", scatter_dimension=0, tiled=True),
        lax.psum_scatter(grad_out, "dp", scatter_dimension=0, tiled=True),
        lax.psum_scatter(grad_gu, "dp", scatter_dimension=0, tiled=True),
        lax.psum_scatter(grad_down, "dp", scatter_dimension=0, tiled=True),
        lax.psum_scatter(grad_vec, "dp", scatter_dimension=1, tiled=True),
    )
    shards = (
        lax.psum(shard_qkv.astype(jnp.bfloat16), "head").astype(jnp.float32),
        lax.psum(shard_out.astype(jnp.bfloat16), "head").astype(jnp.float32),
        lax.psum(shard_gu.astype(jnp.bfloat16), "head").astype(jnp.float32),
        lax.psum(shard_down.astype(jnp.bfloat16), "head").astype(jnp.float32),
        lax.psum(shard_vec.astype(jnp.bfloat16), "head").astype(jnp.float32),
    )
    squares = jnp.float32(0.0)
    for shard_piece in shards:
        squares = squares + jnp.sum(shard_piece * shard_piece)
    grad_norm = jnp.sqrt(lax.psum(squares, "dp"))
    factor = jnp.minimum(1.0, clip_norm[0] / grad_norm)
    up_qkv = adam_update(master_qkv, first_qkv, second_qkv, shards[0], factor, RATE_MAT, DECAY_MAT)
    up_out = adam_update(master_out, first_out, second_out, shards[1], factor, RATE_MAT, DECAY_MAT)
    up_gu = adam_update(master_gu, first_gu, second_gu, shards[2], factor, RATE_MAT, DECAY_MAT)
    up_down = adam_update(
        master_down, first_down, second_down, shards[3], factor, RATE_MAT, DECAY_MAT
    )
    up_vec = adam_update(master_vec, first_vec, second_vec, shards[4], factor, RATE_VEC, 0.0)
    return (
        result.astype(jnp.bfloat16),
        grad_input,
        up_qkv[0],
        up_qkv[1],
        up_qkv[2],
        up_qkv[3],
        up_out[0],
        up_out[1],
        up_out[2],
        up_out[3],
        up_gu[0],
        up_gu[1],
        up_gu[2],
        up_gu[3],
        up_down[0],
        up_down[1],
        up_down[2],
        up_down[3],
        up_vec[0],
        up_vec[1],
        up_vec[2],
        up_vec[3],
        grad_norm.reshape(1),
    )


def solution(mesh):
    in_specs = (
        P(("dp", "head"), None),
        P("dp"),
        P(("dp", "head"), None),
        P(),
        P("dp", None),
        P("dp", None),
        P("dp", None),
        P("dp", None),
        P(None, "dp"),
        P("dp", None),
        P("dp", None),
        P("dp", None),
        P("dp", None),
        P(None, "dp"),
        P("dp", None),
        P("dp", None),
        P("dp", None),
        P("dp", None),
        P(None, "dp"),
    )
    out_specs = (
        P(("dp", "head"), None),
        P(("dp", "head"), None),
        P("dp", None),
        P("dp", None),
        P("dp", None),
        P("dp", None),
        P("dp", None),
        P("dp", None),
        P("dp", None),
        P("dp", None),
        P("dp", None),
        P("dp", None),
        P("dp", None),
        P("dp", None),
        P("dp", None),
        P("dp", None),
        P("dp", None),
        P("dp", None),
        P(None, "dp"),
        P(None, "dp"),
        P(None, "dp"),
        P(None, "dp"),
        P(),
    )
    return jax.shard_map(body, mesh=mesh, in_specs=in_specs, out_specs=out_specs, check_vma=False)
```

profile of v0, /device:TPU:0, one launch (start us, length us, event | category | flops | bytes accessed | tf_op | source)
XLA Modules:
  0.0 1466.6 jit_solution(240032955310916540)
XLA Ops:
  9.2 69.5 %all-gather.6.cloned.1.call-done = bf16[768,2304]{1,0:T(8,128)(2,1)} async-done(((bf16[96,2304]{1,0:T(8,128)(2,1)}), bf16[768,2304]{1,0:T(8,128)(2,1)}) %all-gather.6.cloned.1.call-update) | async-done | bytes 3538960 | tf_op jit(solution)/shard_map/all_gather | solution.py:104
  102.7 34.4 %all-to-all-done = bf16[768,3,4,192]{0,3,1,2:T(8,128)(2,1)S(1)} async-done(((bf16[768,3,4,192]{0,3,1,2:T(8,128)(2,1)}), bf16[768,3,4,192]{0,3,1,2:T(8,128)(2,1)S(1)}, u32[]{:S(2)}, u32[]{:S(2)}) %all-to-all-start) | async-done | bytes 3538976 | tf_op jit(solution)/shard_map/all_to_all | solution.py:117
  141.6 11.2 reshape.363
  156.5 45.1 %while.22 = (s32[]{:T(128)}, bf16[3,1024,192]{1,2,0:T(8,128)(2,1)}, f32[3,3,1024]{2,1,0:T(4,128)}, bf16[3,1024,3,3,64]{1,4,3,2,0:T(8,128)(2,1)S(1)}, s32[3,1024]{1,0:T(4,128)S(1)}, /*index=5*/f32[3]{0:T(128)}, s32[]{:T(128)}) while((s32[]{:T(128)}, bf16[3,1024,192]{1,2,0:T(8,128)(2,1)}, f32[3,3,1024]{2,1,0:T(4,128)}, ...), condition=%wide.region_3.4_spmd, body=%wide.region_0.3_spmd.sunk | while | flops 865269760 | bytes 63571132 | solution.py:146
  204.1 10.0 reshape.379
  214.7 19.5 %reduce.12 = bf16[3072,192]{1,0:T(8,128)(2,1)} reduce(bf16[3072,1,192]{2,1,0:T(2,128)(2,1)} %reshape.379, bf16[]{:T(256)} %broadcast.241), dimensions={1}, to_apply=%reshape.379.reduce_sub_computation | reduce | bytes 2359298 | tf_op jit(solution)/shard_map/reshape | solution.py:148
  249.7 26.3 %all-gather = bf16[8,96,6]{1,2,0:T(8,128)(2,1)S(1)} all-gather(bf16[1,96,6]{1,2,0:T(8,128)(2,1)S(1)} %convert_bitcast_fusion), channel_id=1, replica_groups=mesh['dp'=8,'head'=4] {'dp'}, dimensions={0}, use_global_device_ids=true | all-gather | bytes 10368 | tf_op jit(solution)/shard_map/all_gather | solution.py:108
  303.2 11.6 fusion.63
  321.6 21.7 %multiply_convert_fusion.1 = (bf16[768,3072]{1,0:T(8,128)(2,1)}, f32[768,3072]{1,0:T(8,128)}) fusion(f32[768,6144]{1,0:T(8,128)S(1)} %fusion.63), kind=kLoop, calls=%fused_computation.51 | loop fusion | flops 155713536 | bytes 33030144 | tf_op jit(solution)/shard_map/convert_element_type | solution.py:162
  343.3 17.1 %all-gather.12.cloned.1.call-done = bf16[3072,768]{1,0:T(8,128)(2,1)} async-done(((bf16[384,768]{1,0:T(8,128)(2,1)}), bf16[3072,768]{1,0:T(8,128)(2,1)}) %all-gather.12.cloned.1.call-update) | async-done | bytes 4718608 | tf_op jit(solution)/shard_map/all_gather | solution.py:107
  375.0 18.9 %fusion.28 = (f32[768,3072]{1,0:T(8,128)}, f32[768,3072]{1,0:T(8,128)}) fusion(f32[768,3072]{1,0:T(8,128)} %get-tuple-element.294, f32[768,6144]{1,0:T(8,128)} %copy-done, bf16[3072,768]{1,0:T(8,128)(2,1)} %all-gather.12.cloned.1.call-done, f32[768,768]{0,1:T(8,128)} %get-tuple-element.292, f32[768]{0:T(1024)S(1)} %negate_multiply_fusion.2), kind=kOutput, calls=%fused_computation.75 | convolution fusion | flops 3662807040 | bytes 54266880 | tf_op jit(solution)/shard_map/dot_general | solution.py:44
  393.9 20.0 %multiply_reduce_fusion.1 = (f32[768]{0:T(1024)}, f32[768]{0:T(1024)}, f32[768]{0:T(1024)}, f32[768,768]{0,1:T(8,128)}) fusion(f32[768,768]{0,1:T(8,128)} %copy-done.3, f32[768]{0:T(1024)S(1)} %fusion.58, f32[768]{0:T(1024)S(1)} %broadcast_multiply_fusion.1, f32[768]{0:T(1024)S(1)} %get-tuple-element.237, ...), kind=kOutput, calls=%fused_computation.87 | convolution fusion | flops 7263089664 | bytes 35410944 | tf_op jit(solution)/shard_map/dot_general | solution.py:44
  428.9 11.2 all-to-all-done.2
  450.7 95.2 %while.23 = (s32[]{:T(128)}, bf16[3,1024,3,192]{1,3,2,0:T(8,128)(2,1)}, bf16[3,1024,3,3,64]{1,4,3,2,0:T(8,128)(2,1)S(1)}, s32[3,1024]{1,0:T(4,128)}, f32[3]{0:T(...) while((s32[]{:T(128)}, bf16[3,1024,3,192]{1,3,2,0:T(8,128)(2,1)}, ...), condition=%wide.region_14.15_spmd, body=%wide.region_12.14_spmd.sunk | while | flops 2055534592 | bytes 141906608 | solution.py:218
  545.9 9.8 copy.165
  555.7 77.5 %all_to_all.60 = bf16[3072,3,1,192]{3,1,2,0:T(4,128)(2,1)} all-to-all(bf16[3072,3,1,192]{3,1,2,0:T(4,128)(2,1)} %bitcast.155), channel_id=1, replica_groups=mesh['dp'=8,'head'=4] {'head'}, dimensions={0} | all-to-all | bytes 7077888 | tf_op jit(solution)/shard_map/all_to_all | solution.py:219
  633.2 10.5 copy.166
  671.2 20.7 %fusion.40 = f32[768,6144]{1,0:T(8,128)} fusion(f32[768,3072]{1,0:T(8,128)} %get-tuple-element.300, f32[768,3072]{1,0:T(8,128)} %get-tuple-element.299, f32[768,768]{0,1:T(8,128)S(1)} %copy-done.4, f32[768]{0:T(1024)S(1)} %copy-done.31, f32[768]{0:T(1024)S(1)} %copy-done.29, f32[768]{0:T(1024)S(1)} %copy-done.27, f32[768]{0:T(1024)S(1)} %copy-done.25), kind=kOutput, calls=%fused_computation.111 | convolution fusion | flops 7260143616 | bytes 40120320 | tf_op jit(solution)/shard_map/dot_general | solution.py:38
  697.4 88.2 %reduce-scatter.16.cloned.1.call-done = f32[96,2304]{1,0:T(8,128)} async-done(((f32[768,2304]{1,0:T(8,128)}), f32[96,2304]{1,0:T(8,128)}) %reduce-scatter.16.cloned.1.call-update) | async-done | bytes 884752
  787.8 164.3 %reduce-scatter.14.cloned.1.call-done = f32[384,768]{1,0:T(8,128)} async-done(((f32[3072,768]{1,0:T(8,128)}), f32[384,768]{1,0:T(8,128)}) %reduce-scatter.14.cloned.1.call-update) | async-done | bytes 1179664 | tf_op jit(solution)/shard_map/reduce_scatter | solution.py:243
  954.3 314.7 %reduce-scatter.12.cloned.1.call-done = f32[96,6144]{1,0:T(8,128)} async-done(((f32[768,6144]{1,0:T(8,128)}), f32[96,6144]{1,0:T(8,128)}) %reduce-scatter.12.cloned.1.call-update) | async-done | bytes 2359312 | tf_op jit(solution)/shard_map/reduce_scatter | solution.py:242
  1280.5 53.2 %reduce-scatter.18.cloned.1.call-done = f32[96,6]{1,0:T(8,128)} async-done(((f32[768,6]{1,0:T(8,128)}), f32[96,6]{1,0:T(8,128)}) %reduce-scatter.18.cloned.1.call-update) | async-done | bytes 2320
  1349.0 46.9 %all-reduce.5.cloned.1.call-done = (bf16[96,2304]{0,1:T(8,128)(2,1)}, bf16[96,768]{1,0:T(8,128)(2,1)}, bf16[96,6144]{1,0:T(8,128)(2,1)}, bf16[384,768]{1,0:T(8,128)(2,1)}) async-done(((bf16[96,2304]{0,1:T(8,128)(2,1)}, bf16[96,768]{1,0:T(8,128)(2,1)}, bf16[96,6144]{1,0:T(8,128)(2,1)}, bf16[384,768]{1,0:T(8,128)(2,1)}), (bf16[96,2304]{0,1:T(8,128)(2,1)}, bf16[96,768]{1,0:T(8,128)(2,1)}, ...) | async-done | bytes 2359312 | tf_op jit(solution)/shard_map/psum | solution.py:247
  1410.4 21.8 %psum.47 = f32[]{:T(128)} all-reduce(f32[]{:T(128)S(6)} %add.231), channel_id=1, replica_groups=mesh['dp'=8,'head'=4] {'dp'}, use_global_device_ids=true, to_apply=%region_36.37 | all-reduce | flops 1 | bytes 8 | tf_op jit(solution)/shard_map/psum | solution.py:256
  (299 shorter events, 366.1 us)
Async XLA Ops:
  7.2 71.5 %all-gather.6.cloned.1.call-start = ((), (), s32[]{:S(2)}) async-start(), calls=%async_computation.9 | async-start | bytes 3981312 | tf_op jit(solution)/shard_map/all_gather | solution.py:104
  92.3 44.9 %all-to-all-start = ((bf16[768,3,4,192]{0,3,1,2:T(8,128)(2,1)}), bf16[768,3,4,192]{0,3,1,2:T(8,128)(2,1)S(1)}, u32[]{:S(2)}, u32[]{:S(2)}) async-start(bf16[768,3,4,192]{0,3,1,2:T(8,128)(2,1)} %copy.130), calls=%async_computation | async-start | bytes 7077888 | tf_op jit(solution)/shard_map/all_to_all | solution.py:117
  96.0 201.7 %all-gather.8.cloned.1.call-start = ((), (), s32[]{:S(2)}) async-start(), calls=%async_computation.10 | async-start | bytes 1327104 | tf_op jit(solution)/shard_map/all_gather | solution.py:105
  97.7 205.5 %all-gather.10.cloned.1.call-start = ((), (), s32[]{:S(2)}) async-start(), calls=%async_computation.11 | async-start | bytes 10616832 | tf_op jit(solution)/shard_map/all_gather | solution.py:106
  201.6 12.5 copy-start.32
  238.5 41.3 %all-to-all-start.1 = ((bf16[4,2,73728]{2,1,0:T(2,128)(2,1)}), bf16[4,2,73728]{2,1,0:T(2,128)(2,1)}, u32[]{:S(2)}, u32[]{:S(2)}) async-start(bf16[4,2,73728]{2,1,0:T(2,128)(2,1)} %reshape.390), calls=%async_computation.1 | async-start | bytes 2359296 | tf_op jit(solution)/shard_map/all_to_all | solution.py:147
  242.8 117.6 %all-gather.12.cloned.1.call-start = ((), (), s32[]{:S(2)}) async-start(), calls=%async_computation.12 | async-start | bytes 5308416 | tf_op jit(solution)/shard_map/all_gather | solution.py:107
  279.7 80.6 %copy-start.30 = (f32[768]{0:T(1024)}, f32[768]{0:T(1024)S(1)}, u32[]{:S(2)}) copy-start(f32[768]{0:T(1024)S(1)} %get-tuple-element.236) | copy-start | bytes 9220
  279.7 134.9 %copy-start.28 = (f32[768]{0:T(1024)}, f32[768]{0:T(1024)S(1)}, u32[]{:S(2)}) copy-start(f32[768]{0:T(1024)S(1)} %get-tuple-element.237) | copy-start | bytes 9220
  300.9 113.7 %copy-start.24 = (f32[768]{0:T(1024)}, f32[768]{0:T(1024)S(1)}, u32[]{:S(2)}) copy-start(f32[768]{0:T(1024)S(1)} %broadcast_multiply_fusion.1) | copy-start | bytes 9220
  303.2 111.4 %copy-start.26 = (f32[768]{0:T(1024)}, f32[768]{0:T(1024)S(1)}, u32[]{:S(2)}) copy-start(f32[768]{0:T(1024)S(1)} %fusion.58) | copy-start | bytes 9220
  375.0 18.9 %copy-start.42 = (f32[768]{0:T(1024)}, f32[768]{0:T(1024)S(1)}, u32[]{:S(2)}) copy-start(f32[768]{0:T(1024)S(1)} %negate_multiply_fusion.2) | copy-start | bytes 9220
  393.9 20.0 %copy-start.37 = (f32[768]{0:T(1024)S(1)}, f32[768]{0:T(1024)}, u32[]{:S(2)}) copy-start(f32[768]{0:T(1024)} %copy-done.36) | copy-start | bytes 9220
  419.9 20.2 %all-to-all-start.2 = ((bf16[768,4,192]{0,2,1:T(8,128)(2,1)}), bf16[768,4,192]{0,2,1:T(8,128)(2,1)}, u32[]{:S(2)}, u32[]{:S(2)}) async-start(bf16[768,4,192]{0,2,1:T(8,128)(2,1)} %bitcast.167), calls=%async_computation.2 | async-start | bytes 2359296 | tf_op jit(solution)/shard_map/all_to_all | solution.py:180
  424.2 271.5 %reduce-scatter.10.cloned.1.call-start = ((), (), s32[]{:S(2)}) async-start(), calls=%async_computation.13 | async-start | bytes 2654208 | tf_op jit(solution)/shard_map/reduce_scatter | solution.py:241
  428.8 356.7 %reduce-scatter.16.cloned.1.call-start = ((), (), s32[]{:S(2)}) async-start(), calls=%async_computation.16 | async-start | bytes 7962624
  659.1 293.0 %reduce-scatter.14.cloned.1.call-start = ((), (), s32[]{:S(2)}) async-start(), calls=%async_computation.15 | async-start | bytes 10616832 | tf_op jit(solution)/shard_map/reduce_scatter | solution.py:243
  669.6 599.3 %reduce-scatter.12.cloned.1.call-start = ((), (), s32[]{:S(2)}) async-start(), calls=%async_computation.14 | async-start | bytes 21233664 | tf_op jit(solution)/shard_map/reduce_scatter | solution.py:242
  692.0 641.7 %reduce-scatter.18.cloned.1.call-start = ((), (), s32[]{:S(2)}) async-start(), calls=%async_computation.17 | async-start | bytes 442368
  695.7 700.2 %all-reduce.5.cloned.1.call-start = ((), (), s32[]{:S(2)}) async-start(), calls=%async_computation.18 | async-start | bytes 5013504 | tf_op jit(solution)/shard_map/psum | solution.py:247
  954.3 317.5 %copy-start.19 = (f32[96,2304]{1,0:T(8,128)S(1)}, f32[96,2304]{1,0:T(8,128)}, u32[]{:S(2)}) copy-start(f32[96,2304]{1,0:T(8,128)} %param.28) | copy-start | bytes 2654212
  1407.2 25.8 %copy-start.14 = (f32[96,2304]{0,1:T(8,128)S(1)}, f32[96,2304]{0,1:T(8,128)}, u32[]{:S(2)}) copy-start(f32[96,2304]{0,1:T(8,128)} %copy.151) | copy-start | bytes 2654212
  1407.2 25.8 %copy-start.15 = (f32[96,2304]{0,1:T(8,128)S(1)}, f32[96,2304]{0,1:T(8,128)}, u32[]{:S(2)}) copy-start(f32[96,2304]{0,1:T(8,128)} %copy.148) | copy-start | bytes 2654212
  1407.2 25.8 %copy-start.16 = (f32[96,2304]{0,1:T(8,128)S(1)}, f32[96,2304]{0,1:T(8,128)}, u32[]{:S(2)}) copy-start(f32[96,2304]{0,1:T(8,128)} %copy.149) | copy-start | bytes 2654212
  (47 other events, 141.1 us)
Sparse Core Ops, SparseCore 0:
  10.8 67.8 all-gather.5
  99.6 40.1 all-gather.7
  142.5 136.8 all-gather.9
  282.0 78.3 all-gather.11
  429.0 67.5 reduce-scatter.9
  659.3 126.2 reduce-scatter.15
  789.6 162.4 reduce-scatter.13
  956.5 312.4 reduce-scatter.11
  1273.1 60.5 reduce-scatter.17
  1338.1 57.7 all-reduce.4
where the time goes:
time: 1480 us; the launch traced here: 1470 us
  waiting for transfers between devices  800 us (54%)
  matrix products  208 us (14%)
  local copies, waits for them, and re-layouts  159 us (11%)
  other arithmetic  134 us (9%)
  blocking collectives  132 us (9%)
  between operations  21 us (1%)
    reduce_scatter x1, waiting for transfers between devices, body(): lax.psum_scatter(grad_gu, 'dp', scatter_dimension=0, tiled=True)  315 us
    reduce_scatter x1, waiting for transfers between devices, body(): lax.psum_scatter(grad_down, 'dp', scatter_dimension=0, tiled=True)  164 us
    unnamed x12, waiting for transfers between devices  142 us
    all_to_all x1, blocking collectives, body(): lax.all_to_all(grad_blocks.reshape(group_rows, 3, 1, group_width), 'head'...  77.5 us
    all_gather x1, waiting for transfers between devices, body(): lax.all_gather(low_qkv, 'dp', axis=0, tiled=True)  69.5 us
    unnamed x115, local copies, waits for them, and re-layouts  62.8 us
    dot_general x4, matrix products, times_transposed(): lax.dot_general(left_rows, weight, (((1,), (1,)), ((), ())), preferred_el...  48.9 us
    psum x1, waiting for transfers between devices, body(): lax.psum(shard_qkv.astype(jnp.bfloat16), 'head').astype(jnp.float32)  46.9 us
  transfers between devices with their start and end apart: 13, of which 9 were waited for; matrix products, arithmetic and copies ran while one was open for 25% of the time, Pallas kernels for 0%

commit v1 on v0

v1 whole, which is shorter than its diff:
```python
import functools

import jax
import jax.numpy as jnp
import numpy as np
from jax import lax
from jax.experimental import pallas as pl
from jax.experimental.pallas import tpu as pltpu
from jax.sharding import PartitionSpec as P

HEADS = 12
HEAD_DIM = 64
BLOCK = 128
HALO = 384
MIB = 1024 * 1024

SLOPES = [2.0 ** (-(level + 1)) for level in range(8)] + [
    2.0 ** (-(level + 0.5)) for level in range(4)
]
LN_EPS = 1e-05
BETA_ONE = 0.9
BETA_TWO = 0.999
ADAM_EPS = 1e-08
CORR_ONE = 1.0 - 0.9**10
CORR_TWO = 1.0 - 0.999**10
RATE_MAT = 0.05
RATE_VEC = 0.5
DECAY_MAT = 0.01

BF16 = jnp.bfloat16
F32 = jnp.float32


def dot_nn(left, right):
    return lax.dot_general(left, right, (((1,), (0,)), ((), ())), preferred_element_type=F32)


def dot_nt(left, right):
    return lax.dot_general(left, right, (((1,), (1,)), ((), ())), preferred_element_type=F32)


def dot_tn(left, right):
    return lax.dot_general(left, right, (((0,), (0,)), ((), ())), preferred_element_type=F32)


def piece_copies(pieces, places, whole, sems, first):
    copies = []
    for number, (piece, (row, col)) in enumerate(zip(pieces, places)):
        rows, cols = piece.shape
        copies.append(
            pltpu.make_async_copy(
                piece, whole.at[pl.ds(row, rows), pl.ds(col, cols)], sems.at[first + number]
            )
        )
    return copies


def qkv_kernel(places_of, n_pieces, window_ref, *refs):
    pieces = refs[:n_pieces]
    pairs_ref, whole_ref, sems = refs[n_pieces:]

    @pl.when(pl.program_id(0) == 0)
    def _():
        copies = piece_copies(pieces, places_of(), whole_ref, sems, 0)
        for copy in copies:
            copy.start()
        for copy in copies:
            copy.wait()

    rows = window_ref[...]
    for third in range(3):
        width = 6 * BLOCK
        part = dot_nn(rows, whole_ref[:, third * width : (third + 1) * width]).astype(BF16)
        for pair in range(6):
            pairs_ref[third * 6 + pair] = part[:, pair * BLOCK : (pair + 1) * BLOCK]


def qkv_call(window, pieces, places_of):
    rows, width = window.shape
    tile = HALO
    return pl.pallas_call(
        functools.partial(qkv_kernel, places_of, len(pieces)),
        grid=(rows // tile,),
        in_specs=[pl.BlockSpec((tile, width), lambda i: (i, 0))]
        + [pl.BlockSpec(memory_space=pl.ANY)] * len(pieces),
        out_specs=[
            pl.BlockSpec((18, tile, BLOCK), lambda i: (0, i, 0)),
            pl.BlockSpec((width, 3 * width), lambda i: (0, 0)),
        ],
        out_shape=[
            jax.ShapeDtypeStruct((18, rows, BLOCK), BF16),
            jax.ShapeDtypeStruct((width, 3 * width), BF16),
        ],
        scratch_shapes=[pltpu.SemaphoreType.DMA((len(pieces),))],
        compiler_params=pltpu.CompilerParams(
            dimension_semantics=("arbitrary",), vmem_limit_bytes=32 * MIB
        ),
        cost_estimate=pl.CostEstimate(
            flops=2 * rows * width * 3 * width,
            bytes_accessed=2 * (rows * width * 4 + 6 * width * width),
            transcendentals=0,
        ),
        name="qkv",
    )(window, *pieces)


def run_of(ids_ref, block, count):
    own = ids_ref[block]

    def same(other):
        inside = jnp.logical_and(other >= 0, other < count)
        return jnp.logical_and(inside, ids_ref[jnp.clip(other, 0, count - 1)] == own)

    before = sum(same(block - step).astype(jnp.int32) for step in (1, 2, 3))
    after = sum(same(block + step).astype(jnp.int32) for step in (1, 2, 3))
    return block - before, before + after + 1


def halves_of(rows):
    lane = lax.broadcasted_iota(jnp.int32, rows.shape, 1)
    zero = jnp.zeros_like(rows)
    return jnp.concatenate(
        (jnp.where(lane < HEAD_DIM, rows, zero), jnp.where(lane < HEAD_DIM, zero, rows)), axis=0
    )


def fill_distances(table_ref):
    shape = table_ref.shape
    key = lax.broadcasted_iota(jnp.int32, shape, 0) - 3 * BLOCK
    query = lax.broadcasted_iota(jnp.int32, shape, 1)
    table_ref[...] = jnp.abs(key - query).astype(F32)


def biased_scores(keys, query_pair, distances, slope_one, slope_two):
    bias = jnp.concatenate((distances * slope_one, distances * slope_two), axis=1)
    return dot_nt(keys, query_pair) - bias


def untwine(both):
    mine = jnp.concatenate(
        (both[:HEAD_DIM, :BLOCK], both[HEAD_DIM:, BLOCK:]), axis=0
    )
    return mine.T


def attend_kernel(first_own, n_own, ids_ref, slopes_ref, q_ref, k_ref, v_ref, ctx_ref, lse_ref, table_ref):
    pair = pl.program_id(0)
    count = q_ref.shape[1] // BLOCK

    @pl.when(pair == 0)
    def _():
        fill_distances(table_ref)

    slope_one = slopes_ref[2 * pair]
    slope_two = slopes_ref[2 * pair + 1]

    def one_block(block, carry):
        start, length = run_of(ids_ref, block, count)
        own = jnp.logical_and(block >= first_own, block < first_own + n_own)
        active = jnp.logical_and(start < first_own + n_own, start + length > first_own)
        rows = pl.ds(pl.multiple_of(block * BLOCK, BLOCK), BLOCK)
        shift = pl.multiple_of((3 - (block - start)) * BLOCK, BLOCK)

        def variant(blocks):
            width = blocks * BLOCK
            span = pl.ds(pl.multiple_of(start * BLOCK, BLOCK), width)
            queries = halves_of(q_ref[0, rows, :] * jnp.asarray(HEAD_DIM**-0.5, BF16))
            scores = biased_scores(
                k_ref[0, span, :], queries, table_ref[pl.ds(shift, width), :], slope_one, slope_two
            )
            peak = jnp.max(scores, axis=0, keepdims=True)
            terms = jnp.exp(scores - peak)
            total = jnp.sum(terms, axis=0, keepdims=True)
            lse_ref[0, pl.ds(block, 1), :] = peak + jnp.log(total)

            @pl.when(own)
            def _():
                probs = (terms * (1.0 / total)).astype(BF16)
                both = dot_tn(v_ref[0, span, :], probs)
                place = pl.multiple_of((block - first_own) * BLOCK, BLOCK)
                ctx_ref[pl.ds(place, BLOCK), :] = untwine(both).astype(BF16)

        for blocks in (1, 2, 4):
            @pl.when(jnp.logical_and(active, length == blocks))
            def _(blocks=blocks):
                variant(blocks)

        return carry

    lax.fori_loop(0, count, one_block, 0)


def attend_call(ids, slopes, pairs, own_rows):
    rows = pairs.shape[1]
    count = rows // BLOCK
    width = HEADS * HEAD_DIM
    part = lambda third: pl.BlockSpec((1, rows, BLOCK), lambda p: (third * 6 + p, 0, 0))
    smem = pl.BlockSpec(memory_space=pltpu.SMEM)
    return pl.pallas_call(
        functools.partial(attend_kernel, HALO // BLOCK, own_rows // BLOCK),
        grid=(6,),
        in_specs=[smem, smem, part(0), part(1), part(2)],
        out_specs=[
            pl.BlockSpec((own_rows, BLOCK), lambda p: (0, p)),
            pl.BlockSpec((1, count, 2 * BLOCK), lambda p: (p, 0, 0)),
        ],
        out_shape=[
            jax.ShapeDtypeStruct((own_rows, width), BF16),
            jax.ShapeDtypeStruct((6, count, 2 * BLOCK), F32),
        ],
        scratch_shapes=[pltpu.VMEM((7 * BLOCK, BLOCK), F32)],
        compiler_params=pltpu.CompilerParams(
            dimension_semantics=("arbitrary",), vmem_limit_bytes=32 * MIB
        ),
        cost_estimate=pl.CostEstimate(
            flops=8 * 10**9, bytes_accessed=10 * 10**6, transcendentals=5 * 10**6
        ),
        name="attend",
    )(ids, slopes, pairs, pairs, pairs)


def attend_back_kernel(
    first_own, n_own, ids_ref, slopes_ref, q_ref, k_ref, v_ref, lse_ref, dctx_ref,
    dq_ref, dk_ref, dv_ref, table_ref, dk_sum, dv_sum,
):
    pair = pl.program_id(0)
    count = q_ref.shape[1] // BLOCK

    @pl.when(pair == 0)
    def _():
        fill_distances(table_ref)

    dk_sum[...] = jnp.zeros_like(dk_sum)
    dv_sum[...] = jnp.zeros_like(dv_sum)
    slope_one = slopes_ref[2 * pair]
    slope_two = slopes_ref[2 * pair + 1]

    def one_block(block, carry):
        start, length = run_of(ids_ref, block, count)
        own = jnp.logical_and(block >= first_own, block < first_own + n_own)
        active = jnp.logical_and(start < first_own + n_own, start + length > first_own)
        rows = pl.ds(pl.multiple_of(block * BLOCK, BLOCK), BLOCK)
        shift = pl.multiple_of((3 - (block - start)) * BLOCK, BLOCK)

        def variant(blocks):
            width = blocks * BLOCK
            span = pl.ds(pl.multiple_of(start * BLOCK, BLOCK), width)
            keys = k_ref[0, span, :]
            queries = halves_of(q_ref[0, rows, :] * jnp.asarray(HEAD_DIM**-0.5, BF16))
            scores = biased_scores(
                keys, queries, table_ref[pl.ds(shift, width), :], slope_one, slope_two
            )
            soft = jnp.exp(scores - lse_ref[0, pl.ds(block, 1), :])
            dctx = halves_of(dctx_ref[rows, :])
            dsoft = dot_nt(v_ref[0, span, :], dctx)
            dv_sum[span, :] += dot_nn(soft.astype(BF16), dctx)
            inner = jnp.sum(soft * dsoft, axis=0, keepdims=True)
            dscores = (soft * (dsoft - inner)).astype(BF16)
            dk_sum[span, :] += dot_nn(dscores, queries)

            @pl.when(own)
            def _():
                both = dot_tn(keys, dscores)
                place = pl.multiple_of((block - first_own) * BLOCK, BLOCK)
                dq_ref[pl.ds(place, BLOCK), :] = (untwine(both) * HEAD_DIM**-0.5).astype(BF16)

        for blocks in (1, 2, 4):
            @pl.when(jnp.logical_and(active, length == blocks))
            def _(blocks=blocks):
                variant(blocks)

        return carry

    lax.fori_loop(0, count, one_block, 0)
    mine = pl.ds(first_own * BLOCK, n_own * BLOCK)
    dk_ref[...] = dk_sum[mine, :].astype(BF16)
    dv_ref[...] = dv_sum[mine, :].astype(BF16)


def attend_back_call(ids, slopes, pairs, lse, dctx, own_rows):
    rows = pairs.shape[1]
    count = rows // BLOCK
    width = HEADS * HEAD_DIM
    part = lambda third: pl.BlockSpec((1, rows, BLOCK), lambda p: (third * 6 + p, 0, 0))
    smem = pl.BlockSpec(memory_space=pltpu.SMEM)
    return pl.pallas_call(
        functools.partial(attend_back_kernel, HALO // BLOCK, own_rows // BLOCK),
        grid=(6,),
        in_specs=[
            smem, smem, part(0), part(1), part(2),
            pl.BlockSpec((1, count, 2 * BLOCK), lambda p: (p, 0, 0)),
            pl.BlockSpec((rows, BLOCK), lambda p: (0, p)),
        ],
        out_specs=[pl.BlockSpec((own_rows, BLOCK), lambda p: (0, p))] * 3,
        out_shape=[jax.ShapeDtypeStruct((own_rows, width), BF16)] * 3,
        scratch_shapes=[
            pltpu.VMEM((7 * BLOCK, BLOCK), F32),
            pltpu.VMEM((rows, BLOCK), F32),
            pltpu.VMEM((rows, BLOCK), F32),
        ],
        compiler_params=pltpu.CompilerParams(
            dimension_semantics=("arbitrary",), vmem_limit_bytes=32 * MIB
        ),
        cost_estimate=pl.CostEstimate(
            flops=20 * 10**9, bytes_accessed=14 * 10**6, transcendentals=5 * 10**6
        ),
        name="attend_back",
    )(ids, slopes, pairs, pairs, pairs, lse, dctx)


FF_TILE = 512


def row_mean(values):
    return jnp.mean(values, axis=1, keepdims=True)


def norm_parts(values):
    center = values - row_mean(values)
    scale = lax.rsqrt(row_mean(center * center) + LN_EPS)
    return center * scale, scale


def norm_back(grad_unit, unit, scale):
    return scale * (grad_unit - row_mean(grad_unit) - unit * row_mean(grad_unit * unit))


def column_sum(values):
    return jnp.sum(values, axis=0, keepdims=True)


def middle_kernel(places_of, counts, ctx_ref, tok_ref, cot_ref, vec_ref, *refs):
    n_out, n_gu, n_down = counts
    n_pieces = sum(counts)
    pieces = refs[:n_pieces]
    (result_ref, hidden_ref, dgu_ref, dffn_ref, low_ref, dattn_ref, dfirst_ref, dctx_ref,
     sums_ref, w_out, w_gu, w_down, gate_grad, up_grad, sems) = refs[n_pieces:]
    step = pl.program_id(0)
    width = tok_ref.shape[1]
    ff = w_down.shape[0]

    def copies_of(which):
        place_out, place_gu, place_down = places_of()
        if which == 0:
            return piece_copies(pieces[:n_out], place_out, w_out, sems, 0)
        if which == 1:
            return piece_copies(pieces[n_out : n_out + n_gu], place_gu, w_gu, sems, n_out)
        return piece_copies(pieces[n_out + n_gu :], place_down, w_down, sems, n_out + n_gu)

    def wait_for(which):
        @pl.when(step == 0)
        def _():
            for copy in copies_of(which):
                copy.wait()

    @pl.when(step == 0)
    def _():
        sums_ref[...] = jnp.zeros_like(sums_ref)
        for which in range(3):
            for copy in copies_of(which):
                copy.start()

    gain_one, shift_one = vec_ref[0:1, :], vec_ref[1:2, :]
    gain_two, shift_two = vec_ref[2:3, :], vec_ref[3:4, :]
    wait_for(0)
    attn = dot_nn(ctx_ref[...], w_out[...])
    unit_one, scale_one = norm_parts(tok_ref[...].astype(F32) + attn + vec_ref[4:5, :])
    normed = unit_one * gain_one + shift_one
    low = normed.astype(BF16)
    low_ref[...] = low
    wait_for(1)
    wait_for(2)
    ffn = jnp.zeros((low.shape[0], width), F32)
    for tile in range(ff // FF_TILE):
        cols = slice(tile * FF_TILE, (tile + 1) * FF_TILE)
        gate = dot_nn(low, w_gu[:, cols])
        up = dot_nn(low, w_gu[:, ff + tile * FF_TILE : ff + (tile + 1) * FF_TILE])
        below = 0.5 + 0.5 * lax.erf(gate * np.float32(0.5**0.5))
        gelu = gate * below
        slope = below + gate * (jnp.exp(-0.5 * gate * gate) * np.float32((2.0 * np.pi) ** -0.5))
        hidden = (gelu * up).astype(BF16)
        hidden_ref[:, cols] = hidden
        gate_grad[:, cols] = up * slope
        up_grad[:, cols] = gelu
        ffn = ffn + dot_nn(hidden, w_down[cols, :])
    unit_two, scale_two = norm_parts(normed + ffn + vec_ref[5:6, :])
    result_ref[...] = (unit_two * gain_two + shift_two).astype(BF16)
    grad = cot_ref[...].astype(F32)
    sums_ref[2:3, :] += column_sum(grad * unit_two)
    sums_ref[3:4, :] += column_sum(grad)
    dsecond = norm_back(grad * gain_two, unit_two, scale_two)
    sums_ref[5:6, :] += column_sum(dsecond)
    dffn = dsecond.astype(BF16)
    dffn_ref[...] = dffn
    dnormed = dsecond
    for tile in range(ff // FF_TILE):
        cols = slice(tile * FF_TILE, (tile + 1) * FF_TILE)
        ups = slice(ff + tile * FF_TILE, ff + (tile + 1) * FF_TILE)
        dhidden = dot_nt(dffn, w_down[cols, :])
        dgate = (dhidden * gate_grad[:, cols]).astype(BF16)
        dup = (dhidden * up_grad[:, cols]).astype(BF16)
        dgu_ref[:, cols] = dgate
        dgu_ref[:, ups] = dup
        dnormed = dnormed + dot_nt(dgate, w_gu[:, cols]) + dot_nt(dup, w_gu[:, ups])
    sums_ref[0:1, :] += column_sum(dnormed * unit_one)
    sums_ref[1:2, :] += column_sum(dnormed)
    dfirst = norm_back(dnormed * gain_one, unit_one, scale_one)
    sums_ref[4:5, :] += column_sum(dfirst)
    dfirst_ref[...] = dfirst
    dattn = dfirst.astype(BF16)
    dattn_ref[...] = dattn
    dctx_ref[...] = dot_nt(dattn, w_out[...]).astype(BF16)


def middle_call(ctx, tokens, cotangent, vectors, pieces, places_of):
    rows, width = tokens.shape
    ff = 4 * width
    tile = 256
    by_rows = lambda cols: pl.BlockSpec((tile, cols), lambda i: (i, 0))
    counts = tuple(len(group) for group in pieces)
    flat = [piece for group in pieces for piece in group]
    shaped = lambda cols, dtype: jax.ShapeDtypeStruct((rows, cols), dtype)
    return pl.pallas_call(
        functools.partial(middle_kernel, places_of, counts),
        grid=(rows // tile,),
        in_specs=[by_rows(width)] * 3
        + [pl.BlockSpec((8, width), lambda i: (0, 0))]
        + [pl.BlockSpec(memory_space=pl.ANY)] * len(flat),
        out_specs=[
            by_rows(width), by_rows(ff), by_rows(2 * ff), by_rows(width), by_rows(width),
            by_rows(width), by_rows(width), by_rows(width),
            pl.BlockSpec((8, width), lambda i: (0, 0)),
        ],
        out_shape=[
            shaped(width, BF16), shaped(ff, BF16), shaped(2 * ff, BF16), shaped(width, BF16),
            shaped(width, BF16), shaped(width, BF16), shaped(width, F32), shaped(width, BF16),
            jax.ShapeDtypeStruct((8, width), F32),
        ],
        scratch_shapes=[
            pltpu.VMEM((width, width), BF16),
            pltpu.VMEM((width, 2 * ff), BF16),
            pltpu.VMEM((ff, width), BF16),
            pltpu.VMEM((tile, ff), F32),
            pltpu.VMEM((tile, ff), F32),
            pltpu.SemaphoreType.DMA((len(flat),)),
        ],
        compiler_params=pltpu.CompilerParams(
            dimension_semantics=("arbitrary",), vmem_limit_bytes=56 * MIB
        ),
        cost_estimate=pl.CostEstimate(
            flops=2 * 2 * rows * (width * width + 3 * ff * width),
            bytes_accessed=2 * (width * width + 3 * ff * width + 3 * rows * ff + 8 * rows * width),
            transcendentals=2 * rows * ff,
        ),
        name="middle",
    )(ctx, tokens, cotangent, vectors, *flat)


def adam_update(master, first_mom, second, grad_term, factor, step_rate, decay_rate):
    clipped = grad_term * factor
    first_new = BETA_ONE * first_mom + (1.0 - BETA_ONE) * clipped
    second_new = BETA_TWO * second + (1.0 - BETA_TWO) * clipped * clipped
    direction = first_new / CORR_ONE / (jnp.sqrt(second_new / CORR_TWO) + ADAM_EPS)
    master_new = master - step_rate * (direction + decay_rate * master)
    return (master_new, first_new, second_new, master_new.astype(jnp.bfloat16))


def halo_window(rows, groups):
    left = lax.ppermute(rows[-HALO:], "head", [(i, i + 1) for i in range(groups - 1)])
    right = lax.ppermute(rows[:HALO], "head", [(i + 1, i) for i in range(groups - 1)])
    return jnp.concatenate((left, rows, right), axis=0)


def whole_place():
    return [(0, 0)]


def body(
    tokens, segment_ids, cotangent, clip_norm,
    master_qkv, master_out, master_gu, master_down, master_vec,
    first_qkv, first_out, first_gu, first_down, first_vec,
    second_qkv, second_out, second_gu, second_down, second_vec,
):
    groups = lax.axis_size("head")
    own_rows, width = tokens.shape
    low = [w.astype(BF16) for w in (master_qkv, master_out, master_gu, master_down)]
    window = halo_window(tokens, groups)
    full = [lax.all_gather(w, "dp", axis=0, tiled=True) for w in low]
    full_vec = lax.all_gather(master_vec.astype(BF16), "dp", axis=1, tiled=True)
    vectors = jnp.pad(full_vec.astype(F32), ((0, 2), (0, 0)))
    slopes = jnp.asarray(np.array(SLOPES), F32)

    block_ids = segment_ids.reshape(-1, BLOCK)[:, 0]
    edge = HALO // BLOCK
    padded = jnp.pad(block_ids, (edge, edge), constant_values=-1)
    own_blocks = own_rows // BLOCK
    ids = lax.dynamic_slice_in_dim(
        padded, lax.axis_index("head") * own_blocks, own_blocks + 2 * edge
    )

    pairs, whole_qkv = qkv_call(window, [full[0]], whole_place)
    ctx, lse = attend_call(ids, slopes, pairs, own_rows)
    result, hidden, dgu, dffn, normed_low, dattn, dfirst, dctx, sums = middle_call(
        ctx, tokens, cotangent, vectors, [[full[1]], [full[2]], [full[3]]],
        lambda: [[(0, 0)], [(0, 0)], [(0, 0)]],
    )
    grad_down = dot_tn(hidden, dffn).astype(BF16)
    grad_gu = dot_tn(normed_low, dgu).astype(BF16)
    grad_out = dot_tn(ctx, dattn).astype(BF16)
    dctx_window = halo_window(dctx, groups)
    dq, dk, dv = attend_back_call(ids, slopes, pairs, lse, dctx_window, own_rows)
    djoined = jnp.concatenate((dq, dk, dv), axis=1)
    grad_qkv = dot_tn(tokens, djoined).astype(BF16)
    grad_input = dfirst + dot_nt(djoined, whole_qkv)

    def reduced(grad, axis):
        share = lax.psum_scatter(grad, "dp", scatter_dimension=axis, tiled=True)
        return lax.psum(share, "head").astype(F32)

    shards = [
        reduced(grad_qkv, 0), reduced(grad_out, 0), reduced(grad_gu, 0), reduced(grad_down, 0)
    ]
    vec_sum = lax.psum(sums[:6], ("dp", "head"))
    vec_cols = master_vec.shape[1]
    shards.append(
        lax.dynamic_slice_in_dim(vec_sum, lax.axis_index("dp") * vec_cols, vec_cols, axis=1)
    )
    squares = jnp.float32(0.0)
    for shard_piece in shards:
        squares = squares + jnp.sum(shard_piece * shard_piece)
    grad_norm = jnp.sqrt(lax.psum(squares, "dp"))
    factor = jnp.minimum(1.0, clip_norm[0] / grad_norm)
    masters = (master_qkv, master_out, master_gu, master_down, master_vec)
    firsts = (first_qkv, first_out, first_gu, first_down, first_vec)
    seconds = (second_qkv, second_out, second_gu, second_down, second_vec)
    updates = []
    for index in range(5):
        rate, decay = (RATE_MAT, DECAY_MAT) if index < 4 else (RATE_VEC, 0.0)
        updates.extend(
            adam_update(
                masters[index], firsts[index], seconds[index], shards[index], factor, rate, decay
            )
        )
    return (result, grad_input, *updates, grad_norm.reshape(1))


def solution(mesh):
    rows_split = P(("dp", "head"), None)
    mats, vecs = P("dp", None), P(None, "dp")
    state = (mats,) * 4 + (vecs,)
    in_specs = (rows_split, P("dp"), rows_split, P()) + state * 3
    out_specs = (rows_split, rows_split) + (mats,) * 16 + (vecs,) * 4 + (P(),)
    return jax.shard_map(body, mesh=mesh, in_specs=in_specs, out_specs=out_specs, check_vma=False)
```

time: 1480 us -> 995 us (0.67)
  matrix products: 208 us -> 33.7 us
  waiting for transfers between devices: 800 us -> 670 us
  local copies, waits for them, and re-layouts: 159 us -> 37.2 us
  Pallas kernels: 0 us -> 103 us
  other arithmetic: 134 us -> 33.2 us
  blocking collectives: 132 us -> 89.9 us
    dot_general x33 -> x5, matrix products: 208 us -> 33.7 us  [the longest x4 26.7 us: dot_tn(): lax.dot_general(left, right, (((0,), (0,)), ((), ())), preferred_element_...]
    all_gather x4, waiting for transfers between devices: 86.5 us -> 255 us  [body(): full = [lax.all_gather(w, 'dp', axis=0, tiled=True) for w in low]]
    reduce_scatter x3, waiting for transfers between devices: 479 us -> 330 us  [reduced(): share = lax.psum_scatter(grad, 'dp', scatter_dimension=axis, tiled=True)]
    pallas_call x0 -> x4, Pallas kernels: none -> 103 us  [the longest x1 41.8 us: middle_call(): pl.pallas_call(functools.partial(middle_kernel, places_of, counts), grid=...]
    all_to_all x1 -> x0, blocking collectives: 77.5 us -> none  [body(): lax.all_to_all(grad_blocks.reshape(group_rows, 3, 1, group_width), 'head'...]
    unnamed x12 -> x10, waiting for transfers between devices: 142 us -> 67.9 us
    convert_element_type x18 -> x4, other arithmetic: 57.3 us -> 4.77 us  [body(): w.astype(BF16)]
    all_to_all x3 -> x0, waiting for transfers between devices: 45.7 us -> none  [the longest x1 34.4 us: body(): lax.all_to_all(joined.reshape(tok_rows, 3, groups, group_width), 'head',...]
  transfers between devices with their start and end apart: 13 -> 13, of which waited for: 9 -> 11; matrix products, arithmetic and copies ran while one was open for 25% -> 4% of each run, Pallas kernels for 0% -> 3%
where the time goes in v1:
time: 995 us; the launch traced here: 994 us
  waiting for transfers between devices  670 us (67%)
  Pallas kernels  103 us (10%)
  blocking collectives  89.9 us (9%)
  local copies, waits for them, and re-layouts  37.2 us (4%)
  matrix products  33.7 us (3%)
  other arithmetic  33.2 us (3%)
  between operations  20 us (2%)
    reduce_scatter x3, waiting for transfers between devices, reduced(): share = lax.psum_scatter(grad, 'dp', scatter_dimension=axis, tiled=True)  330 us
    all_gather x4, waiting for transfers between devices, body(): full = [lax.all_gather(w, 'dp', axis=0, tiled=True) for w in low]  255 us
    unnamed x10, waiting for transfers between devices  67.9 us
    pallas_call x1, Pallas kernels, middle_call(): pl.pallas_call(functools.partial(middle_kernel, places_of, counts), grid=...  41.8 us
    psum x1, blocking collectives, body(): vec_sum = lax.psum(sums[:6], ('dp', 'head'))  40.8 us
    unnamed x82, local copies, waits for them, and re-layouts  35.4 us
    pallas_call x1, Pallas kernels, attend_back_call(): pl.pallas_call(functools.partial(attend_back_kernel, HALO // BLOCK, own_r...  30.6 us
    all_gather x1, blocking collectives, body(): full_vec = lax.all_gather(master_vec.astype(BF16), 'dp', axis=1, tiled=True)  27.4 us
  transfers between devices with their start and end apart: 13, of which 11 were waited for; matrix products, arithmetic and copies ran while one was open for 4% of the time, Pallas kernels for 3%

profile of v1, /device:TPU:0, one launch (start us, length us, event | category | flops | bytes accessed | tf_op | source)
XLA Modules:
  0.0 993.9 jit_solution(13990117361810579591)
XLA Ops:
  18.2 27.4 %all-gather = bf16[8,96,6]{1,2,0:T(8,128)(2,1)S(1)} all-gather(bf16[1,96,6]{1,2,0:T(8,128)(2,1)S(1)} %convert_bitcast_fusion), channel_id=1, replica_groups=mesh['dp'=8,'head'=4] {'dp'}, dimensions={0}, use_global_device_ids=true | all-gather | bytes 10368 | tf_op jit(solution)/shard_map/all_gather | solution.py:489
  48.8 30.2 %all-gather.6.cloned.1.call-done.refs_0_ = bf16[768,2304]{1,0:T(8,128)(2,1)} async-done(((bf16[96,2304]{1,0:T(8,128)(2,1)}), bf16[768,2304]{1,0:T(8,128)(2,1)}) %all-gather.6.cloned.1.call-update) | async-done | bytes 3538960 | tf_op jit(solution)/shard_map/all_gather | solution.py:488
  81.0 7.1 qkv.1
  89.8 23.2 %attend.1 = (bf16[768,768]{1,0:T(8,128)(2,1)S(1)}, f32[6,12,256]{2,1,0:T(8,128)S(1)}) custom-call(s32[12]{0:T(128)S(1)} %pad_dynamic-slice_fusion.ids_ref, f32[12]{0:T(128)S(1)} %copy-done.1, bf16[18,1536,128]{2,1,0:T(8,128)(2,1)S(1)} %get-tuple-element.39.q_ref.k_ref.v_ref, bf16[18,1536,128]{2,1,0:T(8,128)(2,1)S(1)} %get-tuple-element.39.q_ref.k_ref.v_ref, ...), custom_call_target="tpu_custom_call" | custom-call | flops 8000000000 | bytes 10000000 | tf_op jit(solution)/shard_map/attend/pallas_call | solution.py:199
  117.0 4.6 all-gather.8.cloned.1.call-done.refs_0_
  121.6 81.4 %all-gather.12.cloned.1.call-done.refs_2_ = bf16[3072,768]{1,0:T(8,128)(2,1)} async-done(((bf16[384,768]{1,0:T(8,128)(2,1)}), bf16[3072,768]{1,0:T(8,128)(2,1)}) %all-gather.12.cloned.1.call-update) | async-done | bytes 4718608 | tf_op jit(solution)/shard_map/all_gather | solution.py:488
  203.0 138.8 %all-gather.10.cloned.1.call-done.refs_1_ = bf16[768,6144]{1,0:T(8,128)(2,1)} async-done(((bf16[96,6144]{1,0:T(8,128)(2,1)}), bf16[768,6144]{1,0:T(8,128)(2,1)}) %all-gather.10.cloned.1.call-update) | async-done | bytes 9437200 | tf_op jit(solution)/shard_map/all_gather | solution.py:488
  341.9 41.8 %middle.1 = (bf16[768,768]{1,0:T(8,128)(2,1)}, bf16[768,3072]{1,0:T(8,128)(2,1)}, bf16[768,6144]{1,0:T(8,128)(2,1)}, bf16[768,768]{1,0:T(8,128)(2,1)}, bf16[768,...) custom-call(bf16[768,768]{1,0:T(8,128)(2,1)} %copy-done.4, ...), custom_call_target="tpu_custom_call" | custom-call | flops 23555211264 | bytes 38928384 | tf_op jit(solution)/shard_map/middle/pallas_call | solution.py:423
  388.4 4.0 collective-permute-done.3
  393.8 30.6 %attend_back.1 = (bf16[768,768]{1,0:T(8,128)(2,1)S(1)}, bf16[768,768]{1,0:T(8,128)(2,1)S(1)}, bf16[768,768]{1,0:T(8,128)(2,1)S(1)}) custom-call(s32[12]{0:T(128)S(1)} %pad_dynamic-slice_fusion.ids_ref, f32[12]{0:T(128)S(1)} %copy-done.1, bf16[18,1536,128]{2,1,0:T(8,128)(2,1)S(1)} %copy-done.3, bf16[18,1536,128]{2,1,0:T(8,128)(2,1)S(1)} %copy-done.3, ...), custom_call_target="tpu_custom_call" | custom-call | flops 20000000000 | bytes 14000000 | tf_op jit(solution)/shard_map/attend_back/pallas_call | solution.py:286
  429.6 4.0 copy.79
  438.7 8.0 convolution_convert_fusion.2
  447.9 13.3 %convolution_convert_fusion = bf16[768,6144]{1,0:T(8,128)(2,1)} fusion(bf16[768,768]{1,0:T(8,128)(2,1)S(1)} %copy-done.33, bf16[768,6144]{1,0:T(8,128)(2,1)} %get-tuple-element.51), kind=kOutput, calls=%fused_computation | convolution fusion | flops 7252475904 | bytes 20054016 | tf_op jit(solution)/shard_map/dot_general | solution.py:43
  461.4 67.7 %reduce-scatter.13.cloned.1.call-done = bf16[96,2304]{1,0:T(8,128)(2,1)} async-done(((bf16[768,2304]{1,0:T(8,128)(2,1)}), bf16[96,2304]{1,0:T(8,128)(2,1)}) %reduce-scatter.13.cloned.1.call-update) | async-done | bytes 442384
  531.2 65.4 %reduce-scatter.7.cloned.1.call-done = bf16[96,768]{1,0:T(8,128)(2,1)} async-done(((bf16[768,768]{1,0:T(8,128)(2,1)}), bf16[96,768]{1,0:T(8,128)(2,1)}) %reduce-scatter.7.cloned.1.call-update) | async-done | bytes 147472 | tf_op jit(solution)/shard_map/reduce_scatter | solution.py:517
  596.5 97.9 %reduce-scatter.11.cloned.1.call-done = bf16[384,768]{1,0:T(8,128)(2,1)} async-done(((bf16[3072,768]{1,0:T(8,128)(2,1)}), bf16[384,768]{1,0:T(8,128)(2,1)}) %reduce-scatter.11.cloned.1.call-update) | async-done | bytes 589840 | tf_op jit(solution)/shard_map/reduce_scatter | solution.py:517
  694.4 166.8 %reduce-scatter.9.cloned.1.call-done = bf16[96,6144]{1,0:T(8,128)(2,1)} async-done(((bf16[768,6144]{1,0:T(8,128)(2,1)}), bf16[96,6144]{1,0:T(8,128)(2,1)}) %reduce-scatter.9.cloned.1.call-update) | async-done | bytes 1179664 | tf_op jit(solution)/shard_map/reduce_scatter | solution.py:517
  868.6 40.8 %psum.46 = f32[6,768]{1,0:T(8,128)} all-reduce(f32[6,768]{1,0:T(8,128)} %bitcast.26), channel_id=1, replica_groups=mesh['dp'=8,'head'=4] {'dp','head'}, use_global_device_ids=true, to_apply=%region_12.13 | all-reduce | flops 4608 | bytes 36864 | tf_op jit(solution)/shard_map/psum | solution.py:523
  910.7 12.9 %all-reduce.5.cloned.1.call-done = (bf16[96,2304]{0,1:T(8,128)(2,1)}, bf16[96,768]{1,0:T(8,128)(2,1)}, bf16[96,6144]{1,0:T(8,128)(2,1)}, bf16[384,768]{1,0:T(8,128)(2,1)}) async-done(((bf16[96,2304]{0,1:T(8,128)(2,1)}, bf16[96,768]{1,0:T(8,128)(2,1)}, bf16[96,6144]{1,0:T(8,128)(2,1)}, bf16[384,768]{1,0:T(8,128)(2,1)}), (bf16[96,2304]{0,1:T(8,128)(2,1)}, bf16[96,768]{1,0:T(8,128)(2,1)}, ...) | async-done | bytes 2359312 | tf_op jit(solution)/shard_map/psum | solution.py:518
  934.9 7.1 convolution_add_fusion
  942.0 21.8 %psum.47 = f32[]{:T(128)} all-reduce(f32[]{:T(128)S(6)} %add.126), channel_id=1, replica_groups=mesh['dp'=8,'head'=4] {'dp'}, use_global_device_ids=true, to_apply=%region_14.15 | all-reduce | flops 1 | bytes 8 | tf_op jit(solution)/shard_map/psum | solution.py:531
  964.5 4.0 fusion.29
  974.8 4.4 fusion.20
  980.4 4.7 fusion.23
  (129 shorter events, 66.0 us)
Async XLA Ops:
  7.2 71.7 %all-gather.6.cloned.1.call-start = ((), (), s32[]{:S(2)}) async-start(), calls=%async_computation.4 | async-start | bytes 3981312 | tf_op jit(solution)/shard_map/all_gather | solution.py:488
  9.4 112.3 %all-gather.8.cloned.1.call-start = ((), (), s32[]{:S(2)}) async-start(), calls=%async_computation.5 | async-start | bytes 1327104 | tf_op jit(solution)/shard_map/all_gather | solution.py:488
  10.1 192.9 %all-gather.12.cloned.1.call-start = ((), (), s32[]{:S(2)}) async-start(), calls=%async_computation.7 | async-start | bytes 5308416 | tf_op jit(solution)/shard_map/all_gather | solution.py:488
  11.1 330.8 %all-gather.10.cloned.1.call-start = ((), (), s32[]{:S(2)}) async-start(), calls=%async_computation.6 | async-start | bytes 10616832 | tf_op jit(solution)/shard_map/all_gather | solution.py:488
  13.2 5.0 copy-start.28
  13.2 32.5 %copy-start.29 = (s32[3072]{0:T(1024)S(1)}, s32[3072]{0:T(1024)}, u32[]{:S(2)}) copy-start(s32[3072]{0:T(1024)} %param.21) | copy-start | bytes 36868
  13.2 515.9 %reduce-scatter.13.cloned.1.call-start = ((), (), s32[]{:S(2)}) async-start(), calls=%async_computation.11 | async-start | bytes 3981312
  14.5 32.0 %collective-permute-start = (bf16[384,768]{1,0:T(8,128)(2,1)S(1)}, bf16[384,768]{1,0:T(8,128)(2,1)S(1)}, u32[]{:S(2)}, u32[]{:S(2)}) collective-permute-start(bf16[384,768]{1,0:T(8,128)(2,1)S(1)} %get-tuple-element.173), channel_id=1, source_target_pairs={{0,1},{1,2},{2,3},{4,5},{5,6},{6,7},{8,9},{9,10},{10,11},{12,13},{... | collective-permute-start | bytes 1769480 | tf_op jit(solution)/shard_map/ppermute | solution.py:469
  16.9 30.4 %collective-permute-start.1 = (bf16[384,768]{1,0:T(8,128)(2,1)S(1)}, bf16[384,768]{1,0:T(8,128)(2,1)}, u32[]{:S(2)}, u32[]{:S(2)}) collective-permute-start(bf16[384,768]{1,0:T(8,128)(2,1)S(1)} %get-tuple-element.174), channel_id=1, source_target_pairs={{1,0},{2,1},{3,2},{5,4},{6,5},{7,6},{9,8},{10,9},{11,10},{13,12},{... | collective-permute-start | bytes 1769480 | tf_op jit(solution)/shard_map/ppermute | solution.py:470
  81.0 8.8 copy-start.1
  383.6 10.1 %copy-start.3 = (bf16[18,1536,128]{2,1,0:T(8,128)(2,1)S(1)}, bf16[18,1536,128]{2,1,0:T(8,128)(2,1)}, u32[]{:S(2)}) copy-start(bf16[18,1536,128]{2,1,0:T(8,128)(2,1)} %copy-done.2) | copy-start | bytes 21233668
  385.1 3.2 collective-permute-start.2
  386.8 5.5 collective-permute-start.3
  433.7 162.9 %reduce-scatter.7.cloned.1.call-start = ((), (), s32[]{:S(2)}) async-start(), calls=%async_computation.8 | async-start | bytes 1327104 | tf_op jit(solution)/shard_map/reduce_scatter | solution.py:517
  437.4 257.0 %reduce-scatter.11.cloned.1.call-start = ((), (), s32[]{:S(2)}) async-start(), calls=%async_computation.10 | async-start | bytes 5308416 | tf_op jit(solution)/shard_map/reduce_scatter | solution.py:517
  446.7 414.6 %reduce-scatter.9.cloned.1.call-start = ((), (), s32[]{:S(2)}) async-start(), calls=%async_computation.9 | async-start | bytes 10616832 | tf_op jit(solution)/shard_map/reduce_scatter | solution.py:517
  461.3 462.4 %all-reduce.5.cloned.1.call-start = ((), (), s32[]{:S(2)}) async-start(), calls=%async_computation.12 | async-start | bytes 5013504 | tf_op jit(solution)/shard_map/psum | solution.py:518
  865.9 69.1 %copy-start.7 = (bf16[768,2304]{1,0:T(8,128)(2,1)S(1)}, bf16[768,2304]{1,0:T(8,128)(2,1)}, u32[]{:S(2)}) copy-start(bf16[768,2304]{1,0:T(8,128)(2,1)} %copy-done.6) | copy-start | bytes 10616836
  974.7 4.4 copy-start.9
  974.8 5.6 copy-start.17
  980.4 4.7 copy-start.21
  980.4 4.7 copy-start.24
  980.4 4.7 copy-start.26
  980.4 4.7 copy-start.27
  (24 other events, 51.3 us)
Sparse Core Ops, SparseCore 0:
  10.8 68.0 all-gather.5
  81.7 39.8 all-gather.7
  124.4 78.5 all-gather.11
  205.6 136.1 all-gather.9
  433.8 95.2 reduce-scatter.12
  532.9 63.5 reduce-scatter.6
  600.2 94.1 reduce-scatter.10
  698.0 163.2 reduce-scatter.8
  864.5 59.1 all-reduce.4

commit v2 on v1

--- a/solution.py
+++ b/solution.py
@@ -43,25 +43,32 @@
     return lax.dot_general(left, right, (((0,), (0,)), ((), ())), preferred_element_type=F32)
 
 
-def piece_copies(pieces, places, whole, sems, first):
+def part_copies(parts, plan, whole, sems, first):
     copies = []
-    for number, (piece, (row, col)) in enumerate(zip(pieces, places)):
-        rows, cols = piece.shape
+    for number, (part, lead, row, rows, to_row, to_col) in enumerate(plan):
+        source = parts[part] if lead is None else parts[part].at[lead]
+        cols = source.shape[1]
         copies.append(
             pltpu.make_async_copy(
-                piece, whole.at[pl.ds(row, rows), pl.ds(col, cols)], sems.at[first + number]
+                source.at[pl.ds(row, rows), :],
+                whole.at[pl.ds(to_row, rows), pl.ds(to_col, cols)],
+                sems.at[first + number],
             )
         )
     return copies
 
 
-def qkv_kernel(places_of, n_pieces, window_ref, *refs):
+def aligned(value, unit):
+    return value if isinstance(value, int) else pl.multiple_of(value, unit)
+
+
+def qkv_kernel(plan_of, n_pieces, window_ref, *refs):
     pieces = refs[:n_pieces]
     pairs_ref, whole_ref, sems = refs[n_pieces:]
 
     @pl.when(pl.program_id(0) == 0)
     def _():
-        copies = piece_copies(pieces, places_of(), whole_ref, sems, 0)
+        copies = part_copies(pieces, plan_of(), whole_ref, sems, 0)
         for copy in copies:
             copy.start()
         for copy in copies:
@@ -75,11 +82,11 @@
             pairs_ref[third * 6 + pair] = part[:, pair * BLOCK : (pair + 1) * BLOCK]
 
 
-def qkv_call(window, pieces, places_of):
+def qkv_call(window, pieces, plan_of, n_copies):
     rows, width = window.shape
     tile = HALO
     return pl.pallas_call(
-        functools.partial(qkv_kernel, places_of, len(pieces)),
+        functools.partial(qkv_kernel, plan_of, len(pieces)),
         grid=(rows // tile,),
         in_specs=[pl.BlockSpec((tile, width), lambda i: (i, 0))]
         + [pl.BlockSpec(memory_space=pl.ANY)] * len(pieces),
@@ -91,7 +98,7 @@
             jax.ShapeDtypeStruct((18, rows, BLOCK), BF16),
             jax.ShapeDtypeStruct((width, 3 * width), BF16),
         ],
-        scratch_shapes=[pltpu.SemaphoreType.DMA((len(pieces),))],
+        scratch_shapes=[pltpu.SemaphoreType.DMA((n_copies,))],
         compiler_params=pltpu.CompilerParams(
             dimension_semantics=("arbitrary",), vmem_limit_bytes=32 * MIB
         ),
@@ -220,13 +227,13 @@
 
 
 def attend_back_kernel(
-    first_own, n_own, ids_ref, slopes_ref, q_ref, k_ref, v_ref, lse_ref, dctx_ref,
+    first_own, n_own, first_pair, ids_ref, slopes_ref, q_ref, k_ref, v_ref, lse_ref, dctx_ref,
     dq_ref, dk_ref, dv_ref, table_ref, dk_sum, dv_sum,
 ):
-    pair = pl.program_id(0)
+    pair = first_pair + pl.program_id(0)
     count = q_ref.shape[1] // BLOCK
 
-    @pl.when(pair == 0)
+    @pl.when(pl.program_id(0) == 0)
     def _():
         fill_distances(table_ref)
 
@@ -277,22 +284,23 @@
     dv_ref[...] = dv_sum[mine, :].astype(BF16)
 
 
-def attend_back_call(ids, slopes, pairs, lse, dctx, own_rows):
+def attend_back_call(ids, slopes, pairs, lse, dctx, own_rows, first_pair, n_pairs):
     rows = pairs.shape[1]
     count = rows // BLOCK
-    width = HEADS * HEAD_DIM
-    part = lambda third: pl.BlockSpec((1, rows, BLOCK), lambda p: (third * 6 + p, 0, 0))
+    part = lambda third: pl.BlockSpec(
+        (1, rows, BLOCK), lambda p: (third * 6 + first_pair + p, 0, 0)
+    )
     smem = pl.BlockSpec(memory_space=pltpu.SMEM)
     return pl.pallas_call(
-        functools.partial(attend_back_kernel, HALO // BLOCK, own_rows // BLOCK),
-        grid=(6,),
+        functools.partial(attend_back_kernel, HALO // BLOCK, own_rows // BLOCK, first_pair),
+        grid=(n_pairs,),
         in_specs=[
             smem, smem, part(0), part(1), part(2),
-            pl.BlockSpec((1, count, 2 * BLOCK), lambda p: (p, 0, 0)),
-            pl.BlockSpec((rows, BLOCK), lambda p: (0, p)),
+            pl.BlockSpec((1, count, 2 * BLOCK), lambda p: (first_pair + p, 0, 0)),
+            pl.BlockSpec((rows, BLOCK), lambda p: (0, first_pair + p)),
         ],
         out_specs=[pl.BlockSpec((own_rows, BLOCK), lambda p: (0, p))] * 3,
-        out_shape=[jax.ShapeDtypeStruct((own_rows, width), BF16)] * 3,
+        out_shape=[jax.ShapeDtypeStruct((own_rows, n_pairs * BLOCK), BF16)] * 3,
         scratch_shapes=[
             pltpu.VMEM((7 * BLOCK, BLOCK), F32),
             pltpu.VMEM((rows, BLOCK), F32),
@@ -302,7 +310,8 @@
             dimension_semantics=("arbitrary",), vmem_limit_bytes=32 * MIB
         ),
         cost_estimate=pl.CostEstimate(
-            flops=20 * 10**9, bytes_accessed=14 * 10**6, transcendentals=5 * 10**6
+            flops=n_pairs * 4 * 10**9, bytes_accessed=n_pairs * 2 * 10**6,
+            transcendentals=n_pairs * 10**6,
         ),
         name="attend_back",
     )(ids, slopes, pairs, pairs, pairs, lse, dctx)
@@ -329,23 +338,19 @@
     return jnp.sum(values, axis=0, keepdims=True)
 
 
-def middle_kernel(places_of, counts, ctx_ref, tok_ref, cot_ref, vec_ref, *refs):
-    n_out, n_gu, n_down = counts
-    n_pieces = sum(counts)
+def middle_kernel(plans_of, slot_of, counts, n_pieces, ctx_ref, tok_ref, cot_ref, vec_ref, *refs):
     pieces = refs[:n_pieces]
     (result_ref, hidden_ref, dgu_ref, dffn_ref, low_ref, dattn_ref, dfirst_ref, dctx_ref,
      sums_ref, w_out, w_gu, w_down, gate_grad, up_grad, sems) = refs[n_pieces:]
     step = pl.program_id(0)
     width = tok_ref.shape[1]
+    half = width // 2
     ff = w_down.shape[0]
+    slot = slot_of()
 
     def copies_of(which):
-        place_out, place_gu, place_down = places_of()
-        if which == 0:
-            return piece_copies(pieces[:n_out], place_out, w_out, sems, 0)
-        if which == 1:
-            return piece_copies(pieces[n_out : n_out + n_gu], place_gu, w_gu, sems, n_out)
-        return piece_copies(pieces[n_out + n_gu :], place_down, w_down, sems, n_out + n_gu)
+        target = (w_out, w_gu, w_down)[which]
+        return part_copies(pieces, plans_of()[which], target, sems, sum(counts[:which]))
 
     def wait_for(which):
         @pl.when(step == 0)
@@ -391,7 +396,8 @@
     dsecond = norm_back(grad * gain_two, unit_two, scale_two)
     sums_ref[5:6, :] += column_sum(dsecond)
     dffn = dsecond.astype(BF16)
-    dffn_ref[...] = dffn
+    dffn_ref[slot] = dffn[:, :half]
+    dffn_ref[1 - slot] = dffn[:, half:]
     dnormed = dsecond
     for tile in range(ff // FF_TILE):
         cols = slice(tile * FF_TILE, (tile + 1) * FF_TILE)
@@ -399,8 +405,8 @@
         dhidden = dot_nt(dffn, w_down[cols, :])
         dgate = (dhidden * gate_grad[:, cols]).astype(BF16)
         dup = (dhidden * up_grad[:, cols]).astype(BF16)
-        dgu_ref[:, cols] = dgate
-        dgu_ref[:, ups] = dup
+        dgu_ref[slot, :, cols] = dgate
+        dgu_ref[1 - slot, :, cols] = dup
         dnormed = dnormed + dot_nt(dgate, w_gu[:, cols]) + dot_nt(dup, w_gu[:, ups])
     sums_ref[0:1, :] += column_sum(dnormed * unit_one)
     sums_ref[1:2, :] += column_sum(dnormed)
@@ -408,32 +414,34 @@
     sums_ref[4:5, :] += column_sum(dfirst)
     dfirst_ref[...] = dfirst
     dattn = dfirst.astype(BF16)
-    dattn_ref[...] = dattn
+    dattn_ref[slot] = dattn[:, :half]
+    dattn_ref[1 - slot] = dattn[:, half:]
     dctx_ref[...] = dot_nt(dattn, w_out[...]).astype(BF16)
 
 
-def middle_call(ctx, tokens, cotangent, vectors, pieces, places_of):
+def middle_call(ctx, tokens, cotangent, vectors, pieces, plans_of, slot_of, counts):
     rows, width = tokens.shape
     ff = 4 * width
     tile = 256
     by_rows = lambda cols: pl.BlockSpec((tile, cols), lambda i: (i, 0))
-    counts = tuple(len(group) for group in pieces)
-    flat = [piece for group in pieces for piece in group]
+    paired = lambda cols: pl.BlockSpec((2, tile, cols), lambda i: (0, i, 0))
     shaped = lambda cols, dtype: jax.ShapeDtypeStruct((rows, cols), dtype)
     return pl.pallas_call(
-        functools.partial(middle_kernel, places_of, counts),
+        functools.partial(middle_kernel, plans_of, slot_of, counts, len(pieces)),
         grid=(rows // tile,),
         in_specs=[by_rows(width)] * 3
         + [pl.BlockSpec((8, width), lambda i: (0, 0))]
-        + [pl.BlockSpec(memory_space=pl.ANY)] * len(flat),
+        + [pl.BlockSpec(memory_space=pl.ANY)] * len(pieces),
         out_specs=[
-            by_rows(width), by_rows(ff), by_rows(2 * ff), by_rows(width), by_rows(width),
-            by_rows(width), by_rows(width), by_rows(width),
+            by_rows(width), by_rows(ff), paired(ff), paired(width // 2), by_rows(width),
+            paired(width // 2), by_rows(width), by_rows(width),
             pl.BlockSpec((8, width), lambda i: (0, 0)),
         ],
         out_shape=[
-            shaped(width, BF16), shaped(ff, BF16), shaped(2 * ff, BF16), shaped(width, BF16),
-            shaped(width, BF16), shaped(width, BF16), shaped(width, F32), shaped(width, BF16),
+            shaped(width, BF16), shaped(ff, BF16), jax.ShapeDtypeStruct((2, rows, ff), BF16),
+            jax.ShapeDtypeStruct((2, rows, width // 2), BF16), shaped(width, BF16),
+            jax.ShapeDtypeStruct((2, rows, width // 2), BF16), shaped(width, F32),
+            shaped(width, BF16),
             jax.ShapeDtypeStruct((8, width), F32),
         ],
         scratch_shapes=[
@@ -442,7 +450,7 @@
             pltpu.VMEM((ff, width), BF16),
             pltpu.VMEM((tile, ff), F32),
             pltpu.VMEM((tile, ff), F32),
-            pltpu.SemaphoreType.DMA((len(flat),)),
+            pltpu.SemaphoreType.DMA((sum(counts),)),
         ],
         compiler_params=pltpu.CompilerParams(
             dimension_semantics=("arbitrary",), vmem_limit_bytes=56 * MIB
@@ -453,16 +461,59 @@
             transcendentals=2 * rows * ff,
         ),
         name="middle",
-    )(ctx, tokens, cotangent, vectors, *flat)
-
-
-def adam_update(master, first_mom, second, grad_term, factor, step_rate, decay_rate):
-    clipped = grad_term * factor
-    first_new = BETA_ONE * first_mom + (1.0 - BETA_ONE) * clipped
-    second_new = BETA_TWO * second + (1.0 - BETA_TWO) * clipped * clipped
-    direction = first_new / CORR_ONE / (jnp.sqrt(second_new / CORR_TWO) + ADAM_EPS)
-    master_new = master - step_rate * (direction + decay_rate * master)
-    return (master_new, first_new, second_new, master_new.astype(jnp.bfloat16))
+    )(ctx, tokens, cotangent, vectors, *pieces)
+
+
+def adam_kernel(factor_ref, *refs):
+    masters, firsts, seconds, grads, outs = (
+        refs[:5], refs[5:10], refs[10:15], refs[15:20], refs[20:]
+    )
+    factor = factor_ref[0]
+    for index in range(5):
+        rate, decay = (RATE_MAT, DECAY_MAT) if index < 4 else (RATE_VEC, 0.0)
+        new_ref, first_ref, second_ref, copy_ref = outs[4 * index : 4 * index + 4]
+        master = masters[index][...]
+        clipped = grads[index][...].astype(F32) * factor
+        first = BETA_ONE * firsts[index][...] + (1.0 - BETA_ONE) * clipped
+        second = BETA_TWO * seconds[index][...] + (1.0 - BETA_TWO) * clipped * clipped
+        direction = first / CORR_ONE / (jnp.sqrt(second / CORR_TWO) + ADAM_EPS)
+        new = master - rate * (direction + decay * master)
+        new_ref[...] = new
+        first_ref[...] = first
+        second_ref[...] = second
+        copy_ref[...] = new.astype(BF16)
+
+
+def adam_call(masters, firsts, seconds, grads, factor):
+    steps = 6
+
+    def spec(array, index):
+        rows, cols = array.shape
+        if index == 4:
+            return pl.BlockSpec((rows, cols), lambda i: (0, 0))
+        return pl.BlockSpec((rows, cols // steps), lambda i: (0, i))
+
+    specs = [spec(array, index) for index, array in enumerate(masters)]
+    return pl.pallas_call(
+        adam_kernel,
+        grid=(steps,),
+        in_specs=[pl.BlockSpec(memory_space=pltpu.SMEM)] + specs * 4,
+        out_specs=[one for one in specs for _ in range(4)],
+        out_shape=[
+            jax.ShapeDtypeStruct(array.shape, dtype)
+            for array in masters
+            for dtype in (F32, F32, F32, BF16)
+        ],
+        compiler_params=pltpu.CompilerParams(
+            dimension_semantics=("arbitrary",), vmem_limit_bytes=40 * MIB
+        ),
+        cost_estimate=pl.CostEstimate(
+            flops=20 * sum(array.size for array in masters),
+            bytes_accessed=28 * sum(array.size for array in masters),
+            transcendentals=2 * sum(array.size for array in masters),
+        ),
+        name="adam",
+    )(factor, *masters, *firsts, *seconds, *grads)
 
 
 def halo_window(rows, groups):
@@ -471,77 +522,331 @@
     return jnp.concatenate((left, rows, right), axis=0)
 
 
-def whole_place():
-    return [(0, 0)]
-
-
-def body(
-    tokens, segment_ids, cotangent, clip_norm,
-    master_qkv, master_out, master_gu, master_down, master_vec,
-    first_qkv, first_out, first_gu, first_down, first_vec,
-    second_qkv, second_out, second_gu, second_down, second_vec,
-):
-    groups = lax.axis_size("head")
-    own_rows, width = tokens.shape
-    low = [w.astype(BF16) for w in (master_qkv, master_out, master_gu, master_down)]
-    window = halo_window(tokens, groups)
-    full = [lax.all_gather(w, "dp", axis=0, tiled=True) for w in low]
-    full_vec = lax.all_gather(master_vec.astype(BF16), "dp", axis=1, tiled=True)
-    vectors = jnp.pad(full_vec.astype(F32), ((0, 2), (0, 0)))
-    slopes = jnp.asarray(np.array(SLOPES), F32)
-
+def slope_table():
+    return jnp.asarray(np.array(SLOPES), F32)
+
+
+def window_ids(segment_ids, own_rows):
     block_ids = segment_ids.reshape(-1, BLOCK)[:, 0]
     edge = HALO // BLOCK
     padded = jnp.pad(block_ids, (edge, edge), constant_values=-1)
     own_blocks = own_rows // BLOCK
-    ids = lax.dynamic_slice_in_dim(
+    return lax.dynamic_slice_in_dim(
         padded, lax.axis_index("head") * own_blocks, own_blocks + 2 * edge
     )
 
-    pairs, whole_qkv = qkv_call(window, [full[0]], whole_place)
+
+def updated(masters, firsts, seconds, shards, grad_norm, clip_norm):
+    factor = jnp.minimum(1.0, clip_norm / grad_norm)
+    return adam_call(masters, firsts, seconds, shards, factor)
+
+
+def plain_body(tokens, segment_ids, cotangent, clip_norm, *state):
+    masters, firsts, seconds = state[:5], state[5:10], state[10:]
+    groups = lax.axis_size("head")
+    own_rows, width = tokens.shape
+    low = [w.astype(BF16) for w in masters]
+    window = halo_window(tokens, groups)
+    full = [lax.all_gather(w, "dp", axis=0, tiled=True) for w in low[:4]]
+    full_vec = lax.all_gather(low[4], "dp", axis=1, tiled=True)
+    vectors = jnp.pad(full_vec.astype(F32), ((0, 2), (0, 0)))
+    slopes = slope_table()
+    ids = window_ids(segment_ids, own_rows)
+
+    def whole_plan(part, rows):
+        return [(part, None, 0, rows, 0, 0)]
+
+    pairs, whole_qkv = qkv_call(window, [full[0]], lambda: whole_plan(0, width), 1)
     ctx, lse = attend_call(ids, slopes, pairs, own_rows)
     result, hidden, dgu, dffn, normed_low, dattn, dfirst, dctx, sums = middle_call(
-        ctx, tokens, cotangent, vectors, [[full[1]], [full[2]], [full[3]]],
-        lambda: [[(0, 0)], [(0, 0)], [(0, 0)]],
-    )
-    grad_down = dot_tn(hidden, dffn).astype(BF16)
-    grad_gu = dot_tn(normed_low, dgu).astype(BF16)
-    grad_out = dot_tn(ctx, dattn).astype(BF16)
+        ctx, tokens, cotangent, vectors, full[1:],
+        lambda: (whole_plan(0, width), whole_plan(1, width), whole_plan(2, 4 * width)),
+        lambda: 0, (1, 1, 1),
+    )
+    joined_back = lambda two: jnp.concatenate((two[0], two[1]), axis=1)
+    grad_down = dot_tn(hidden, joined_back(dffn)).astype(BF16)
+    grad_gu = dot_tn(normed_low, joined_back(dgu)).astype(BF16)
+    grad_out = dot_tn(ctx, joined_back(dattn)).astype(BF16)
     dctx_window = halo_window(dctx, groups)
-    dq, dk, dv = attend_back_call(ids, slopes, pairs, lse, dctx_window, own_rows)
+    dq, dk, dv = attend_back_call(ids, slopes, pairs, lse, dctx_window, own_rows, 0, 6)
     djoined = jnp.concatenate((dq, dk, dv), axis=1)
     grad_qkv = dot_tn(tokens, djoined).astype(BF16)
     grad_input = dfirst + dot_nt(djoined, whole_qkv)
 
-    def reduced(grad, axis):
-        share = lax.psum_scatter(grad, "dp", scatter_dimension=axis, tiled=True)
+    def reduced(grad):
+        share = lax.psum_scatter(grad, "dp", scatter_dimension=0, tiled=True)
         return lax.psum(share, "head").astype(F32)
 
-    shards = [
-        reduced(grad_qkv, 0), reduced(grad_out, 0), reduced(grad_gu, 0), reduced(grad_down, 0)
-    ]
+    shards = [reduced(grad) for grad in (grad_qkv, grad_out, grad_gu, grad_down)]
     vec_sum = lax.psum(sums[:6], ("dp", "head"))
-    vec_cols = master_vec.shape[1]
+    vec_cols = masters[4].shape[1]
     shards.append(
         lax.dynamic_slice_in_dim(vec_sum, lax.axis_index("dp") * vec_cols, vec_cols, axis=1)
     )
-    squares = jnp.float32(0.0)
-    for shard_piece in shards:
-        squares = squares + jnp.sum(shard_piece * shard_piece)
-    grad_norm = jnp.sqrt(lax.psum(squares, "dp"))
-    factor = jnp.minimum(1.0, clip_norm[0] / grad_norm)
-    masters = (master_qkv, master_out, master_gu, master_down, master_vec)
-    firsts = (first_qkv, first_out, first_gu, first_down, first_vec)
-    seconds = (second_qkv, second_out, second_gu, second_down, second_vec)
-    updates = []
-    for index in range(5):
-        rate, decay = (RATE_MAT, DECAY_MAT) if index < 4 else (RATE_VEC, 0.0)
-        updates.extend(
-            adam_update(
-                masters[index], firsts[index], seconds[index], shards[index], factor, rate, decay
-            )
+    squares = sum(jnp.sum(piece * piece) for piece in shards)
+    grad_norm = jnp.sqrt(lax.psum(squares, "dp")).reshape(1)
+    updates = updated(masters, firsts, seconds, shards, grad_norm, clip_norm)
+    return (result, grad_input, *updates, grad_norm)
+
+
+SWAP_CORE = ("head", [(i, i ^ 1) for i in range(4)])
+SWAP_X = ("head", [(i, i ^ 2) for i in range(4)])
+SWAP_Y = ("dp", [(i, i ^ 1) for i in range(8)])
+SWAP_Z = [None] + [("dp", [(i, i ^ (2 * step)) for i in range(8)]) for step in (1, 2, 3)]
+
+
+def swap(values, how):
+    return lax.ppermute(values, *how)
+
+
+def position():
+    dp, head = lax.axis_index("dp"), lax.axis_index("head")
+    return dp // 2, dp % 2, head // 2, head % 2
+
+
+def z_others(z):
+    return (z + 1 - 2 * (z % 2), (z + 2) % 4, 3 - z)
+
+
+def dp_order(z, y):
+    others = z_others(z)
+    first = [z * 2 + y, z * 2 + 1 - y]
+    return first + [other * 2 + y for other in others] + [other * 2 + 1 - y for other in others]
+
+
+def half_of(values, which, axis):
+    size = values.shape[axis] // 2
+    return lax.dynamic_slice_in_dim(values, which * size, size, axis)
+
+
+def spread_z(mine):
+    return [swap(mine, SWAP_Z[step]) for step in (1, 2, 3)]
+
+
+def tied(values, after):
+    return lax.optimization_barrier((values, *after))[0]
+
+
+def together(*values):
+    return lax.optimization_barrier(values)
+
+
+def slab_sum(mine, other):
+    return (mine.astype(F32) + other.astype(F32)).astype(BF16)
+
+
+def pick(values, index):
+    return lax.dynamic_index_in_dim(values, index, 0, keepdims=False)
+
+
+def ordered(mine, other, which, axis):
+    return jnp.where(
+        which == 0,
+        jnp.concatenate((mine, other), axis=axis),
+        jnp.concatenate((other, mine), axis=axis),
+    )
+
+
+def cube_body(tokens, segment_ids, cotangent, clip_norm, *state):
+    masters, firsts, seconds = state[:5], state[5:10], state[10:]
+    groups = lax.axis_size("head")
+    own_rows, width = tokens.shape
+    ff = 4 * width
+    half = width // 2
+    shard = width // 8
+    z, y, x, core = position()
+    low = [w.astype(BF16) for w in masters]
+
+    mine_qkv = half_of(low[0], core, 1)
+    all_qkv = lax.all_gather(mine_qkv, "dp", axis=0, tiled=False)
+
+    mine_gu = half_of(half_of(low[2], core, 1), x, 0)
+    z_gu = spread_z(mine_gu)
+    y_gu = swap(mine_gu, SWAP_Y)
+    x_gu = swap(mine_gu, SWAP_X)
+    mine_gu, y_gu, x_gu, *z_gu = together(mine_gu, y_gu, x_gu, *z_gu)
+
+    vec_rows = jnp.pad(low[4], ((0, 10), (0, half - shard)))
+    mine_rest = jnp.concatenate((half_of(low[3], core, 1), half_of(low[1], core, 1), vec_rows), axis=0)
+    rest_rows = mine_rest.shape[0]
+    mine_rest = tied(mine_rest, (y_gu,))
+    all_rest = lax.all_gather(mine_rest, "dp", axis=0, tiled=False)
+
+    near_gu = jnp.concatenate((y_gu, *z_gu), axis=0)
+    far_gu = swap(near_gu[shard // 2 :], SWAP_Y)
+    near_x_gu = swap(near_gu, SWAP_X)
+    window = halo_window(tokens, groups)
+    far_gu, all_qkv, window = together(far_gu, all_qkv, window)
+    other_qkv = swap(all_qkv, SWAP_CORE)
+
+    def qkv_plan():
+        core = position()[3]
+        plan = []
+        for swapped in (0, 1):
+            col = aligned((core + swapped * (1 - 2 * core)) * (3 * half), BLOCK)
+            plan += [(swapped, dp, 0, shard, dp * shard, col) for dp in range(8)]
+        return plan
+
+    def middle_plans():
+        z, y, x, core = position()
+        order = dp_order(z, y)
+        out_plan, gu_plan, down_plan = [], [], []
+        for swapped in (0, 1):
+            side = core + swapped * (1 - 2 * core)
+            for dp in range(8):
+                col = aligned(side * half, BLOCK)
+                out_plan.append((12 + swapped, dp, ff // 8, shard, dp * shard, col))
+                down_plan.append((12 + swapped, dp, 0, ff // 8, dp * (ff // 8), col))
+            for flipped in (0, 1):
+                rows_half = x + flipped * (1 - 2 * x)
+                for number, dp in enumerate(order):
+                    places = ((0, 0), (1, 0), (1, 1), (1, 2), (1, 3), (2, 0), (2, 1), (2, 2))
+                    part, index = places[number]
+                    row = aligned(dp * shard + rows_half * (shard // 2), 16)
+                    gu_plan.append(
+                        (6 * swapped + 3 * flipped + part, None, index * (shard // 2), shard // 2, row,
+                         aligned(side * ff, BLOCK))
+                    )
+        return out_plan, gu_plan, down_plan
+
+    slopes = slope_table()
+    ids = window_ids(segment_ids, own_rows)
+    pairs, whole_qkv = qkv_call(window, [all_qkv, other_qkv], qkv_plan, 16)
+    pairs, near_x_gu = together(pairs, near_x_gu)
+    ctx, lse = attend_call(ids, slopes, pairs, own_rows)
+    far_x_gu = swap(far_gu, SWAP_X)
+    parts_gu = [mine_gu, near_gu, far_gu, x_gu, near_x_gu]
+    swapped_gu = [swap(part, SWAP_CORE) for part in parts_gu]
+    ctx, lse, far_x_gu, all_rest, *swapped_gu = together(ctx, lse, far_x_gu, all_rest, *swapped_gu)
+    parts_gu = parts_gu + [far_x_gu] + swapped_gu + [swap(far_x_gu, SWAP_CORE)]
+    other_rest = swap(all_rest, SWAP_CORE)
+    vec_all = all_rest[:, rest_rows - 16 : rest_rows - 8, :shard].astype(F32)
+    vectors = vec_all.transpose(1, 0, 2).reshape(8, width)
+    result, hidden, dgu, dffn, normed_low, dattn, dfirst, dctx, sums = middle_call(
+        ctx, tokens, cotangent, vectors, parts_gu + [all_rest, other_rest],
+        middle_plans, lambda: position()[3], (16, 32, 16),
+    )
+
+    def core_send(left, right):
+        return swap(dot_tn(left, right[1]).astype(BF16), SWAP_CORE)
+
+    def core_keep(left, right, theirs):
+        return (dot_tn(left, right[0]) + theirs.astype(F32)).astype(BF16)
+
+    their_gu = core_send(normed_low, dgu)
+    dctx_window = halo_window(dctx, groups)
+    their_down = core_send(hidden, dffn)
+    their_out = core_send(ctx, dattn)
+    vec_low = sums.astype(BF16)
+    their_vec = swap(vec_low, SWAP_CORE)
+    their_gu, their_down, their_out, their_vec, dctx_window = together(
+        their_gu, their_down, their_out, their_vec, dctx_window
+    )
+    vec_cols = jnp.pad(slab_sum(vec_low, their_vec).T, ((0, 0), (0, BLOCK - 8)))
+    sum_down = core_keep(hidden, dffn, their_down)
+    sum_gu = core_keep(normed_low, dgu, their_gu)
+    sum_out = core_keep(ctx, dattn, their_out)
+
+    first_cols = ff // 2
+    by_x = sum_gu[:, :first_cols].reshape(8, 2, shard // 2, first_cols)
+    one_x = lax.dynamic_index_in_dim(by_x, x, 1, keepdims=False)
+    one_away = lax.dynamic_index_in_dim(by_x, 1 - x, 1, keepdims=False)
+    two = jnp.concatenate((sum_gu[:, first_cols:], sum_out, vec_cols), axis=1)
+    two = two.reshape(4, 2, shard, two.shape[1])
+    two_y = lax.dynamic_index_in_dim(two, y, 1, keepdims=False)
+    two_away = lax.dynamic_index_in_dim(two, 1 - y, 1, keepdims=False)
+    share_down = lax.psum_scatter(sum_down, "dp", scatter_dimension=0, tiled=True)
+
+    def z_send(values, z):
+        return [swap(pick(values, place), SWAP_Z[step]) for step, place in zip((1, 2, 3), z_others(z))]
+
+    def z_keep(values, theirs, z):
+        total = pick(values, z).astype(F32)
+        for other in theirs:
+            total = total + other.astype(F32)
+        return total.astype(BF16)
+
+    def split_y(values):
+        values = values.reshape(4, 2, *values.shape[1:])
+        return (
+            lax.dynamic_index_in_dim(values, y, 1, keepdims=False),
+            lax.dynamic_index_in_dim(values, 1 - y, 1, keepdims=False),
         )
-    return (result, grad_input, *updates, grad_norm.reshape(1))
+
+    def back_part(first_pair, wait_for):
+        return attend_back_call(
+            ids, slopes, tied(pairs, wait_for), lse, dctx_window, own_rows, first_pair, 3
+        )
+
+    def qkv_sum(back):
+        grad = dot_tn(tokens, jnp.concatenate(back, axis=1)).astype(BF16)
+        grad = grad.reshape(8, 2, shard // 2, grad.shape[1])
+        theirs = swap(lax.dynamic_index_in_dim(grad, 1 - core, 1, keepdims=False), SWAP_CORE)
+        return slab_sum(lax.dynamic_index_in_dim(grad, core, 1, keepdims=False), theirs)
+
+    one_their = swap(one_away, SWAP_X)
+    two_their = swap(two_away, SWAP_Y)
+    back_a = back_part(0, (one_away, two_away, sum_down))
+    one_their, two_their, *back_a = together(one_their, two_their, *back_a)
+    a_y, a_away = split_y(qkv_sum(back_a))
+    one_y, one_away = split_y(slab_sum(one_x, one_their))
+    two_y = slab_sum(two_y, two_their)
+    one_their = swap(one_away, SWAP_Y)
+    two_their = z_send(two_y, z)
+    a_their = swap(a_away, SWAP_Y)
+    back_b = back_part(3, (a_away, one_away, two_y))
+    one_their, a_their, *rest = together(one_their, a_their, *two_their, *back_b)
+    two_their, back_b = rest[:3], rest[3:]
+    b_y, b_away = split_y(qkv_sum(back_b))
+    one_y = slab_sum(one_y, one_their)
+    a_y = slab_sum(a_y, a_their)
+    two_z = z_keep(two_y, two_their, z)
+    b_their = swap(b_away, SWAP_Y)
+    one_their = z_send(one_y, z)
+    a_their = z_send(a_y, z)
+    two_their = swap(two_z, SWAP_X)
+    djoined = jnp.concatenate([piece for pair in zip(back_a, back_b) for piece in pair], axis=1)
+    grad_input = dfirst + dot_nt(djoined, whole_qkv)
+    b_their, two_their, share_down, grad_input, *rest = together(
+        b_their, two_their, share_down, grad_input, *one_their, *a_their
+    )
+    one_their, a_their = rest[:3], rest[3:]
+    b_y = slab_sum(b_y, b_their)
+    one_z = z_keep(one_y, one_their, z)
+    a_z = z_keep(a_y, a_their, z)
+    b_their = z_send(b_y, z)
+    one_their = swap(one_z, SWAP_X)
+    a_their = swap(a_z, SWAP_X)
+    down_their = swap(share_down, SWAP_X)
+    one_their, a_their, down_their, *b_their = together(one_their, a_their, down_their, *b_their)
+    b_z = z_keep(b_y, b_their, z)
+    b_their = swap(b_z, SWAP_X)
+    share_down = slab_sum(share_down, down_their)
+    ab = jnp.concatenate((slab_sum(a_z, a_their), slab_sum(b_z, b_their)), axis=1)
+    share_qkv = ordered(ab, swap(ab, SWAP_CORE), core, 0)
+    share_qkv = share_qkv.reshape(shard, 2, 3, half).transpose(0, 2, 1, 3).reshape(shard, 3 * width)
+    two_sum = slab_sum(two_z, two_their)
+    gu_two, share_out, share_vec = (
+        two_sum[:, :first_cols], two_sum[:, first_cols : first_cols + half], two_sum[:, first_cols + half :]
+    )
+    gu_one = ordered(one_z, one_their, x, 0)
+
+    def both_cores(mine):
+        return ordered(mine, swap(mine, SWAP_CORE), core, 1)
+
+    shards = [
+        share_qkv,
+        both_cores(share_out),
+        both_cores(jnp.concatenate((gu_one, gu_two), axis=1)),
+        both_cores(share_down),
+        share_vec[:, :6].T,
+    ]
+    squares = sum(jnp.sum(jnp.square(piece.astype(F32))) for piece in shards).reshape(1, 1)
+    for how in (SWAP_Y, SWAP_Z[1], SWAP_Z[2]):
+        squares = squares + swap(squares, how)
+    grad_norm = jnp.sqrt(squares[0])
+    updates = updated(masters, firsts, seconds, shards, grad_norm, clip_norm)
+    return (result, grad_input, *updates, grad_norm)
 
 
 def solution(mesh):
@@ -550,4 +855,6 @@
     state = (mats,) * 4 + (vecs,)
     in_specs = (rows_split, P("dp"), rows_split, P()) + state * 3
     out_specs = (rows_split, rows_split) + (mats,) * 16 + (vecs,) * 4 + (P(),)
+    cube = mesh.shape["dp"] == 8 and mesh.shape["head"] == 4
+    body = cube_body if cube else plain_body
     return jax.shard_map(body, mesh=mesh, in_specs=in_specs, out_specs=out_specs, check_vma=False)

time: 995 us -> 522 us (0.52)
  waiting for transfers between devices: 670 us -> 123 us
  blocking collectives: 89.9 us -> 0 us
  starting transfers between devices: 7.01 us -> 89.5 us
  local copies, waits for them, and re-layouts: 37.2 us -> 83.5 us
  Pallas kernels: 103 us -> 129 us
    reduce_scatter x3 -> x1, waiting for transfers between devices: 330 us -> 0.01 us  [cube_body(): lax.psum_scatter(sum_down, 'dp', scatter_dimension=0, tiled=True)]
    all_gather x4 -> x2, waiting for transfers between devices: 255 us -> 0.02 us  [the longest x1 0.02 us: cube_body(): all_rest = lax.all_gather(mine_rest, 'dp', axis=0, tiled=False)]
    ppermute x0 -> x51, waiting for transfers between devices: none -> 121 us  [swap(): return lax.ppermute(values, *how)]
    ppermute x0 -> x51, starting transfers between devices: none -> 83 us  [swap(): return lax.ppermute(values, *how)]
    unnamed x10 -> x3, waiting for transfers between devices: 67.9 us -> 0.05 us
    psum x2 -> x0, blocking collectives: 62.5 us -> none  [the longest x1 40.8 us: body(): vec_sum = lax.psum(sums[:6], ('dp', 'head'))]
    all_gather x1 -> x0, blocking collectives: 27.4 us -> none  [body(): full_vec = lax.all_gather(master_vec.astype(BF16), 'dp', axis=1, tiled=True)]
    unnamed x82 -> x169, local copies, waits for them, and re-layouts: 35.4 us -> 56 us
  transfers between devices with their start and end apart: 13 -> 58, of which waited for: 11 -> 16; matrix products, arithmetic and copies ran while one was open for 4% -> 16% of each run, Pallas kernels for 3% -> 15%
where the time goes in v2:
time: 522 us; the launch traced here: 516 us
  Pallas kernels  129 us (25%)
  waiting for transfers between devices  123 us (24%)
  starting transfers between devices  89.5 us (17%)
  local copies, waits for them, and re-layouts  83.5 us (16%)
  matrix products  38.5 us (7%)
  other arithmetic  30.4 us (6%)
  between operations  22.1 us (4%)
    ppermute x51, waiting for transfers between devices, swap(): return lax.ppermute(values, *how)  121 us
    ppermute x51, starting transfers between devices, swap(): return lax.ppermute(values, *how)  83 us
    unnamed x169, local copies, waits for them, and re-layouts  56 us
    pallas_call x1, Pallas kernels, middle_call(): pl.pallas_call(functools.partial(middle_kernel, plans_of, slot_of, counts...  43.7 us
    pallas_call x2, Pallas kernels, attend_back_call(): pl.pallas_call(functools.partial(attend_back_kernel, HALO // BLOCK, own_r...  40.4 us
    dot_general x8, matrix products, dot_tn(): lax.dot_general(left, right, (((0,), (0,)), ((), ())), preferred_element_...  35.6 us
    pallas_call x1, Pallas kernels, attend_call(): pl.pallas_call(functools.partial(attend_kernel, HALO // BLOCK, own_rows /...  28.2 us
  transfers between devices with their start and end apart: 58, of which 16 were waited for; matrix products, arithmetic and copies ran while one was open for 16% of the time, Pallas kernels for 15%

profile of v2, /device:TPU:0, one launch (start us, length us, event | category | flops | bytes accessed | tf_op | source)
XLA Modules:
  0.0 515.9 jit_solution(14500741455925214789)
XLA Ops:
  22.9 8.3 %collective-permute-done.2 = bf16[48,3072]{1,0:T(8,128)(2,1)S(1)} collective-permute-done((bf16[48,3072]{1,0:T(8,128)(2,1)S(1)}, bf16[48,3072]{1,0:T(8,128)(2,1)S(1)}, u32[]{:S(2)}, u32[]{:S(2)}) %collective-permute-start.2) | collective-permute-done | bytes 294944 | tf_op jit(solution)/shard_map/ppermute | solution.py:599
  31.2 14.7 %collective-permute-done.3 = bf16[48,3072]{1,0:T(8,128)(2,1)S(1)} collective-permute-done((bf16[48,3072]{1,0:T(8,128)(2,1)S(1)}, bf16[48,3072]{1,0:T(8,128)(2,1)S(1)}, u32[]{:S(2)}, u32[]{:S(2)}) %collective-permute-start.3) | collective-permute-done | bytes 294944 | tf_op jit(solution)/shard_map/ppermute | solution.py:599
  51.5 29.3 %collective-permute-done.5.refs_2_ = bf16[144,3072]{1,0:T(8,128)(2,1)} collective-permute-done((bf16[144,3072]{1,0:T(8,128)(2,1)S(1)}, bf16[144,3072]{1,0:T(8,128)(2,1)}, u32[]{:S(2)}, u32[]{:S(2)}) %collective-permute-start.5) | collective-permute-done | bytes 884768 | tf_op jit(solution)/shard_map/ppermute | solution.py:599
  88.4 7.2 %qkv.1 = (bf16[18,1536,128]{2,1,0:T(8,128)(2,1)S(1)}, bf16[768,2304]{1,0:T(8,128)(2,1)S(1)}) custom-call(bf16[1536,768]{1,0:T(8,128)(2,1)S(1)} %pad_maximum_fusion.window_ref, bf16[8,96,1152]{2,1,0:T(8,128)(2,1)S(1)} %bitcast.135, bf16[8,96,1152]{2,1,0:T(8,128)(2,1)S(1)} %collective-permute-done.8.refs_1_), custom_call_target="tpu_custom_call" | custom-call | flops 5435817984 | bytes 16515072 | tf_op jit(solution)/shard_map/qkv/pallas_call | solution.py:88
  100.3 16.2 %collective-permute-done.9.refs_4_ = bf16[192,3072]{1,0:T(8,128)(2,1)} collective-permute-done((bf16[192,3072]{1,0:T(8,128)(2,1)}, bf16[192,3072]{1,0:T(8,128)(2,1)}, u32[]{:S(2)}, u32[]{:S(2)}) %collective-permute-start.9) | collective-permute-done | bytes 1179680 | tf_op jit(solution)/shard_map/ppermute | solution.py:599
  123.3 28.2 %attend.1 = (bf16[768,768]{1,0:T(8,128)(2,1)S(1)}, f32[6,12,256]{2,1,0:T(8,128)S(1)}) custom-call(s32[12]{0:T(128)S(1)} %pad_dynamic-slice_fusion.ids_ref, f32[12]{0:T(128)S(1)} %copy-done.25, bf16[18,1536,128]{2,1,0:T(8,128)(2,1)S(1)} %copy-done.29, bf16[18,1536,128]{2,1,0:T(8,128)(2,1)S(1)} %copy-done.29, bf16[18,1536,128]{2,1,0:T(8,128)(2,1)S(1)} %copy-done.29), custom_call_target="tpu_custom_call" | custom-call | flops 8000000000 | bytes 10000000 | tf_op jit(solution)/shard_map/attend/pallas_call | solution.py:206
  157.7 5.2 %collective-permute-done.16.refs_11_ = bf16[144,3072]{1,0:T(8,128)(2,1)} collective-permute-done((bf16[144,3072]{1,0:T(8,128)(2,1)}, bf16[144,3072]{1,0:T(8,128)(2,1)}, u32[]{:S(2)}, u32[]{:S(2)}) %collective-permute-start.16) | collective-permute-done | bytes 884768 | tf_op jit(solution)/shard_map/ppermute | solution.py:599
  164.5 43.7 %middle.1 = (bf16[768,768]{1,0:T(8,128)(2,1)}, bf16[768,3072]{1,0:T(8,128)(2,1)}, bf16[2,768,3072]{2,1,0:T(8,128)(2,1)}, bf16[2,768,384]{2,1,0:T(8,128)(2,1)}, b...) custom-call(bf16[768,768]{1,0:T(8,128)(2,1)} %copy-done.26, ...), custom_call_target="tpu_custom_call" | custom-call | flops 23555211264 | bytes 38928384 | tf_op jit(solution)/shard_map/middle/pallas_call | solution.py:429
  208.2 8.9 %convolution_convert_fusion = bf16[768,3072]{1,0:T(8,128)(2,1)} fusion(bf16[768,768]{1,0:T(8,128)(2,1)} %get-tuple-element.143, bf16[2,768,3072]{2,1,0:T(8,128)(2,1)} %get-tuple-element.144), kind=kOutput, calls=%fused_computation.3 | convolution fusion | flops 3626237952 | bytes 10616832 | tf_op jit(solution)/shard_map/dot_general | solution.py:43
  217.5 3.9 convolution_convert_fusion.1
  235.6 8.0 %add_convert_fusion = bf16[768,3072]{1,0:T(8,128)(2,1)S(1)} fusion(bf16[768,3072]{1,0:T(8,128)(2,1)} %collective-permute-done.18, bf16[768,768]{1,0:T(8,128)(2,1)} %get-tuple-element.143, bf16[2,768,3072]{2,1,0:T(8,128)(2,1)} %get-tuple-element.144), kind=kOutput, calls=%fused_computation | convolution fusion | flops 3630956544 | bytes 15335424 | tf_op jit(solution)/shard_map/dot_general | solution.py:43
  248.6 4.1 collective-permute-start.24
  252.7 5.2 %add_convert_fusion.1 = bf16[3072,384]{1,0:T(8,128)(2,1)} fusion(bf16[3072,384]{1,0:T(8,128)(2,1)} %collective-permute-done.19, bf16[768,3072]{1,0:T(8,128)(2,1)S(1)} %bitcast.153, bf16[2,768,384]{2,1,0:T(8,128)(2,1)S(1)} %copy-done.76), kind=kOutput, calls=%fused_computation.6 | convolution fusion | flops 1815478272 | bytes 10027008 | tf_op jit(solution)/shard_map/dot_general | solution.py:43
  265.6 20.2 %attend_back.2 = (bf16[768,384]{1,0:T(8,128)(2,1)S(1)}, bf16[768,384]{1,0:T(8,128)(2,1)S(1)}, bf16[768,384]{1,0:T(8,128)(2,1)S(1)}) custom-call(s32[12]{0:T(128)S(1)} %pad_dynamic-slice_fusion.ids_ref, f32[12]{0:T(128)S(1)} %copy-done.25, bf16[18,1536,128]{2,1,0:T(8,128)(2,1)S(1)} %copy-done.30, bf16[18,1536,128]{2,1,0:T(8,128)(2,1)S(1)} %copy-done.30, ...), custom_call_target="tpu_custom_call" | custom-call | flops 12000000000 | bytes 6000000 | tf_op jit(solution)/shard_map/attend_back/pallas_call | solution.py:294
  286.6 3.8 copy.79
  295.3 4.8 collective-permute-start.27
  302.2 5.8 %collective-permute-start.30 = (bf16[96,2048]{0,1:T(8,128)(2,1)}, bf16[96,2048]{0,1:T(8,128)(2,1)}, u32[]{:S(2)}, u32[]{:S(2)}) collective-permute-start(bf16[96,2048]{0,1:T(8,128)(2,1)} %get-tuple-element.228), channel_id=1, source_target_pairs={{0,16},{4,20},{8,24},{12,28},{16,0},{20,4},{24,8},{28,12},{1,17},{... | collective-permute-start | bytes 1179656 | tf_op jit(solution)/shard_map/ppermute | solution.py:599
  323.5 20.2 %attend_back.3 = (bf16[768,384]{1,0:T(8,128)(2,1)S(1)}, bf16[768,384]{1,0:T(8,128)(2,1)S(1)}, bf16[768,384]{1,0:T(8,128)(2,1)S(1)}) custom-call(s32[12]{0:T(128)S(1)} %pad_dynamic-slice_fusion.ids_ref, f32[12]{0:T(128)S(1)} %copy-done.25, bf16[18,1536,128]{2,1,0:T(8,128)(2,1)S(1)} %copy-done.31, bf16[18,1536,128]{2,1,0:T(8,128)(2,1)S(1)} %copy-done.31, ...), custom_call_target="tpu_custom_call" | custom-call | flops 12000000000 | bytes 6000000 | tf_op jit(solution)/shard_map/attend_back/pallas_call | solution.py:294
  346.2 5.4 %collective-permute-done.31 = bf16[96,2048]{0,1:T(8,128)(2,1)} collective-permute-done((bf16[96,2048]{0,1:T(8,128)(2,1)}, bf16[96,2048]{0,1:T(8,128)(2,1)}, u32[]{:S(2)}, u32[]{:S(2)}) %collective-permute-start.31) | collective-permute-done | bytes 393248 | tf_op jit(solution)/shard_map/ppermute | solution.py:599
  353.2 13.1 %collective-permute-start.38 = (bf16[48,1152]{1,0:T(8,128)(2,1)}, bf16[48,1152]{1,0:T(8,128)(2,1)S(1)}, u32[]{:S(2)}, u32[]{:S(2)}) collective-permute-start(bf16[48,1152]{1,0:T(8,128)(2,1)} %get-tuple-element.244), channel_id=1, source_target_pairs={{0,8},{4,12},{8,0},{12,4},{16,24},{20,28},{24,16},{28,20},{1,9},{5... | collective-permute-start | bytes 331784 | tf_op jit(solution)/shard_map/ppermute | solution.py:599
  391.8 18.2 %collective-permute-done.36 = bf16[48,1536]{0,1:T(8,128)(2,1)S(1)} collective-permute-done((bf16[48,1536]{0,1:T(8,128)(2,1)S(1)}, bf16[48,1536]{0,1:T(8,128)(2,1)S(1)}, u32[]{:S(2)}, u32[]{:S(2)}) %collective-permute-start.36) | collective-permute-done | bytes 147488 | tf_op jit(solution)/shard_map/ppermute | solution.py:599
  413.8 8.5 %collective-permute-start.44 = (bf16[48,1152]{1,0:T(8,128)(2,1)}, bf16[48,1152]{1,0:T(8,128)(2,1)}, u32[]{:S(2)}, u32[]{:S(2)}) collective-permute-start(bf16[48,1152]{1,0:T(8,128)(2,1)} %get-tuple-element.241), channel_id=1, source_target_pairs={{0,8},{4,12},{8,0},{12,4},{16,24},{20,28},{24,16},{28,20},{1,9},{5... | collective-permute-start | bytes 331784 | tf_op jit(solution)/shard_map/ppermute | solution.py:599
  434.2 12.6 %collective-permute-done.42 = bf16[48,1152]{1,0:T(8,128)(2,1)S(1)} collective-permute-done((bf16[48,1152]{1,0:T(8,128)(2,1)S(1)}, bf16[48,1152]{1,0:T(8,128)(2,1)S(1)}, u32[]{:S(2)}, u32[]{:S(2)}) %collective-permute-start.42) | collective-permute-done | bytes 110624 | tf_op jit(solution)/shard_map/ppermute | solution.py:599
  498.7 9.1 %adam.1 = (f32[96,2304]{1,0:T(8,128)}, f32[96,2304]{1,0:T(8,128)}, f32[96,2304]{1,0:T(8,128)}, bf16[96,2304]{1,0:T(8,128)(2,1)}, f32[96,768]{1,0:T(8,128)}, /*in...) custom-call(f32[1]{0:T(128)S(6)} %min.3.factor_ref, ...), custom_call_target="tpu_custom_call" | custom-call | flops 23604480 | bytes 33046272 | tf_op jit(solution)/shard_map/adam/pallas_call | solution.py:497
  (350 shorter events, 188.9 us)
Async XLA Ops:
  7.2 73.6 %all-gather.5.cloned.1.call-start = ((), (), s32[]{:S(2)}) async-start(), calls=%async_computation.2 | async-start | bytes 1990656 | tf_op jit(solution)/shard_map/all_gather | solution.py:661
  9.1 144.2 %all-gather.7.cloned.1.call-start = ((), (), s32[]{:S(2)}) async-start(), calls=%async_computation.3 | async-start | bytes 3428352 | tf_op jit(solution)/shard_map/all_gather | solution.py:673
  16.5 29.4 %collective-permute-start.3 = (bf16[48,3072]{1,0:T(8,128)(2,1)S(1)}, bf16[48,3072]{1,0:T(8,128)(2,1)S(1)}, u32[]{:S(2)}, u32[]{:S(2)}) collective-permute-start(bf16[48,3072]{1,0:T(8,128)(2,1)S(1)} %dynamic_slice.188.refs_0_), channel_id=1, source_target_pairs={{0,16},{4,20},{8,24},{12,28},{16,0},{20,4},{24,8},{28,12},{1,17},{... | collective-permute-start | bytes 884744 | tf_op jit(solution)/shard_map/ppermute | solution.py:599
  19.1 26.8 %collective-permute-start.4 = (bf16[48,3072]{1,0:T(8,128)(2,1)S(1)}, bf16[48,3072]{1,0:T(8,128)(2,1)S(1)}, u32[]{:S(2)}, u32[]{:S(2)}) collective-permute-start(bf16[48,3072]{1,0:T(8,128)(2,1)S(1)} %dynamic_slice.188.refs_0_), channel_id=1, source_target_pairs={{0,24},{4,28},{8,16},{12,20},{16,8},{20,12},{24,0},{28,4},{1,25},{... | collective-permute-start | bytes 884744 | tf_op jit(solution)/shard_map/ppermute | solution.py:599
  46.0 365.8 %reduce-scatter.2.cloned.1.call-start = ((), (), s32[]{:S(2)}) async-start(), calls=%async_computation.1 | async-start | bytes 2654208 | tf_op jit(solution)/shard_map/reduce_scatter | solution.py:758
  48.8 32.0 %collective-permute-start.5 = (bf16[144,3072]{1,0:T(8,128)(2,1)S(1)}, bf16[144,3072]{1,0:T(8,128)(2,1)}, u32[]{:S(2)}, u32[]{:S(2)}) collective-permute-start(bf16[144,3072]{1,0:T(8,128)(2,1)S(1)} %pad_maximum_fusion.2), channel_id=1, source_target_pairs={{0,4},{4,0},{8,12},{12,8},{16,20},{20,16},{24,28},{28,24},{1,5},{5... | collective-permute-start | bytes 2654216 | tf_op jit(solution)/shard_map/ppermute | solution.py:599
  87.8 28.6 %collective-permute-start.9 = (bf16[192,3072]{1,0:T(8,128)(2,1)}, bf16[192,3072]{1,0:T(8,128)(2,1)}, u32[]{:S(2)}, u32[]{:S(2)}) collective-permute-start(bf16[192,3072]{1,0:T(8,128)(2,1)} %constant_dynamic-update-slice_fusion.refs_1_), channel_id=1, source_target_pairs={{0,2},{1,3},{2,0},{3,1},{4,6},{5,7},{6,4},{7,5},{8,10},{9,11},{10,... | collective-permute-start | bytes 3538952 | tf_op jit(solution)/shard_map/ppermute | solution.py:599
  88.2 65.0 %collective-permute-start.12 = (bf16[192,3072]{1,0:T(8,128)(2,1)}, bf16[192,3072]{1,0:T(8,128)(2,1)}, u32[]{:S(2)}, u32[]{:S(2)}) collective-permute-start(bf16[192,3072]{1,0:T(8,128)(2,1)} %constant_dynamic-update-slice_fusion.refs_1_), channel_id=1, source_target_pairs={{0,1},{1,0},{2,3},{3,2},{4,5},{5,4},{6,7},{7,6},{8,9},{9,8},{10,11... | collective-permute-start | bytes 3538952 | tf_op jit(solution)/shard_map/ppermute | solution.py:599
  116.5 36.9 %collective-permute-start.15 = (bf16[192,3072]{1,0:T(8,128)(2,1)}, bf16[192,3072]{1,0:T(8,128)(2,1)S(1)}, u32[]{:S(2)}, u32[]{:S(2)}) collective-permute-start(bf16[192,3072]{1,0:T(8,128)(2,1)} %collective-permute-done.9.refs_4_), channel_id=1, source_target_pairs={{0,1},{1,0},{2,3},{3,2},{4,5},{5,4},{6,7},{7,6},{8,9},{9,8},{10,11... | collective-permute-start | bytes 3538952 | tf_op jit(solution)/shard_map/ppermute | solution.py:599
  117.0 36.3 %collective-permute-start.10 = (bf16[144,3072]{1,0:T(8,128)(2,1)}, bf16[144,3072]{1,0:T(8,128)(2,1)S(1)}, u32[]{:S(2)}, u32[]{:S(2)}) collective-permute-start(bf16[144,3072]{1,0:T(8,128)(2,1)} %collective-permute-done.5.refs_2_), channel_id=1, source_target_pairs={{0,2},{1,3},{2,0},{3,1},{4,6},{5,7},{6,4},{7,5},{8,10},{9,11},{10,... | collective-permute-start | bytes 2654216 | tf_op jit(solution)/shard_map/ppermute | solution.py:599
  117.3 36.0 %collective-permute-start.13 = (bf16[144,3072]{1,0:T(8,128)(2,1)}, bf16[144,3072]{1,0:T(8,128)(2,1)S(1)}, u32[]{:S(2)}, u32[]{:S(2)}) collective-permute-start(bf16[144,3072]{1,0:T(8,128)(2,1)} %collective-permute-done.5.refs_2_), channel_id=1, source_target_pairs={{0,1},{1,0},{2,3},{3,2},{4,5},{5,4},{6,7},{7,6},{8,9},{9,8},{10,11... | collective-permute-start | bytes 2654216 | tf_op jit(solution)/shard_map/ppermute | solution.py:599
  119.9 33.3 %collective-permute-start.14 = (bf16[48,3072]{1,0:T(8,128)(2,1)}, bf16[48,3072]{1,0:T(8,128)(2,1)S(1)}, u32[]{:S(2)}, u32[]{:S(2)}) collective-permute-start(bf16[48,3072]{1,0:T(8,128)(2,1)} %copy-done.70), channel_id=1, source_target_pairs={{0,1},{1,0},{2,3},{3,2},{4,5},{5,4},{6,7},{7,6},{8,9},{9,8},{10,11... | collective-permute-start | bytes 884744 | tf_op jit(solution)/shard_map/ppermute | solution.py:599
  247.4 39.2 %collective-permute-start.25 = (bf16[4,96,2048]{2,1,0:T(8,128)(2,1)}, bf16[4,96,2048]{2,1,0:T(8,128)(2,1)}, u32[]{:S(2)}, u32[]{:S(2)}) collective-permute-start(bf16[4,96,2048]{2,1,0:T(8,128)(2,1)} %get-tuple-element.226), channel_id=1, source_target_pairs={{0,4},{4,0},{8,12},{12,8},{16,20},{20,16},{24,28},{28,24},{1,5},{5... | collective-permute-start | bytes 4718600 | tf_op jit(solution)/shard_map/ppermute | solution.py:599
  248.6 38.0 %collective-permute-start.24 = (bf16[8,48,1536]{2,1,0:T(8,128)(2,1)}, bf16[8,48,1536]{2,1,0:T(8,128)(2,1)}, u32[]{:S(2)}, u32[]{:S(2)}) collective-permute-start(bf16[8,48,1536]{2,1,0:T(8,128)(2,1)} %dynamic-slice_bitcast_fusion.1), channel_id=1, source_target_pairs={{0,2},{1,3},{2,0},{3,1},{4,6},{5,7},{6,4},{7,5},{8,10},{9,11},{10,... | collective-permute-start | bytes 3538952 | tf_op jit(solution)/shard_map/ppermute | solution.py:599
  301.8 44.3 %collective-permute-start.29 = (bf16[96,2048]{0,1:T(8,128)(2,1)}, bf16[96,2048]{0,1:T(8,128)(2,1)}, u32[]{:S(2)}, u32[]{:S(2)}) collective-permute-start(bf16[96,2048]{0,1:T(8,128)(2,1)} %get-tuple-element.229), channel_id=1, source_target_pairs={{0,8},{4,12},{8,0},{12,4},{16,24},{20,28},{24,16},{28,20},{1,9},{5... | collective-permute-start | bytes 1179656 | tf_op jit(solution)/shard_map/ppermute | solution.py:599
  302.2 44.0 %collective-permute-start.30 = (bf16[96,2048]{0,1:T(8,128)(2,1)}, bf16[96,2048]{0,1:T(8,128)(2,1)}, u32[]{:S(2)}, u32[]{:S(2)}) collective-permute-start(bf16[96,2048]{0,1:T(8,128)(2,1)} %get-tuple-element.228), channel_id=1, source_target_pairs={{0,16},{4,20},{8,24},{12,28},{16,0},{20,4},{24,8},{28,12},{1,17},{... | collective-permute-start | bytes 1179656 | tf_op jit(solution)/shard_map/ppermute | solution.py:599
  308.0 43.6 %collective-permute-start.31 = (bf16[96,2048]{0,1:T(8,128)(2,1)}, bf16[96,2048]{0,1:T(8,128)(2,1)}, u32[]{:S(2)}, u32[]{:S(2)}) collective-permute-start(bf16[96,2048]{0,1:T(8,128)(2,1)} %get-tuple-element.227), channel_id=1, source_target_pairs={{0,24},{4,28},{8,16},{12,20},{16,8},{20,12},{24,0},{28,4},{1,25},{... | collective-permute-start | bytes 1179656 | tf_op jit(solution)/shard_map/ppermute | solution.py:599
  312.1 39.4 %collective-permute-start.26 = (bf16[4,48,1536]{2,1,0:T(8,128)(2,1)}, bf16[4,48,1536]{2,1,0:T(8,128)(2,1)}, u32[]{:S(2)}, u32[]{:S(2)}) collective-permute-start(bf16[4,48,1536]{2,1,0:T(8,128)(2,1)} %get-tuple-element.234), channel_id=1, source_target_pairs={{0,4},{4,0},{8,12},{12,8},{16,20},{20,16},{24,28},{28,24},{1,5},{5... | collective-permute-start | bytes 1769480 | tf_op jit(solution)/shard_map/ppermute | solution.py:599
  319.2 32.3 %collective-permute-start.28 = (bf16[4,48,1152]{2,1,0:T(8,128)(2,1)S(1)}, bf16[4,48,1152]{2,1,0:T(8,128)(2,1)S(1)}, u32[]{:S(2)}, u32[]{:S(2)}) collective-permute-start(bf16[4,48,1152]{2,1,0:T(8,128)(2,1)S(1)} %dynamic-slice_bitcast_fusion.9), channel_id=1, source_target_pairs={{0,4},{4,0},{8,12},{12,8},{16,20},{20,16},{24,28},{28,24},{1,5},{5... | collective-permute-start | bytes 1327112 | tf_op jit(solution)/shard_map/ppermute | solution.py:599
  353.2 29.6 %collective-permute-start.38 = (bf16[48,1152]{1,0:T(8,128)(2,1)}, bf16[48,1152]{1,0:T(8,128)(2,1)S(1)}, u32[]{:S(2)}, u32[]{:S(2)}) collective-permute-start(bf16[48,1152]{1,0:T(8,128)(2,1)} %get-tuple-element.244), channel_id=1, source_target_pairs={{0,8},{4,12},{8,0},{12,4},{16,24},{20,28},{24,16},{28,20},{1,9},{5... | collective-permute-start | bytes 331784 | tf_op jit(solution)/shard_map/ppermute | solution.py:599
  380.5 29.6 %collective-permute-start.36 = (bf16[48,1536]{0,1:T(8,128)(2,1)S(1)}, bf16[48,1536]{0,1:T(8,128)(2,1)S(1)}, u32[]{:S(2)}, u32[]{:S(2)}) collective-permute-start(bf16[48,1536]{0,1:T(8,128)(2,1)S(1)} %get-tuple-element.231), channel_id=1, source_target_pairs={{0,16},{4,20},{8,24},{12,28},{16,0},{20,4},{24,8},{28,12},{1,17},{... | collective-permute-start | bytes 442376 | tf_op jit(solution)/shard_map/ppermute | solution.py:599
  382.8 27.3 %collective-permute-start.37 = (bf16[48,1536]{0,1:T(8,128)(2,1)S(1)}, bf16[48,1536]{0,1:T(8,128)(2,1)S(1)}, u32[]{:S(2)}, u32[]{:S(2)}) collective-permute-start(bf16[48,1536]{0,1:T(8,128)(2,1)S(1)} %get-tuple-element.230), channel_id=1, source_target_pairs={{0,24},{4,28},{8,16},{12,20},{16,8},{20,12},{24,0},{28,4},{1,25},{... | collective-permute-start | bytes 442376 | tf_op jit(solution)/shard_map/ppermute | solution.py:599
  384.0 26.0 %collective-permute-start.34 = (bf16[96,2048]{0,1:T(8,128)(2,1)S(1)}, bf16[96,2048]{0,1:T(8,128)(2,1)S(1)}, u32[]{:S(2)}, u32[]{:S(2)}) collective-permute-start(bf16[96,2048]{0,1:T(8,128)(2,1)S(1)} %fusion.24), channel_id=1, source_target_pairs={{0,2},{1,3},{2,0},{3,1},{4,6},{5,7},{6,4},{7,5},{8,10},{9,11},{10,... | collective-permute-start | bytes 1179656 | tf_op jit(solution)/shard_map/ppermute | solution.py:599
  386.6 25.1 %collective-permute-start.33 = (bf16[4,48,1152]{2,1,0:T(8,128)(2,1)S(1)}, bf16[4,48,1152]{2,1,0:T(8,128)(2,1)}, u32[]{:S(2)}, u32[]{:S(2)}) collective-permute-start(bf16[4,48,1152]{2,1,0:T(8,128)(2,1)S(1)} %dynamic-slice_bitcast_fusion.8), channel_id=1, source_target_pairs={{0,4},{4,0},{8,12},{12,8},{16,20},{20,16},{24,28},{28,24},{1,5},{5... | collective-permute-start | bytes 1327112 | tf_op jit(solution)/shard_map/ppermute | solution.py:599
  (113 other events, 923.9 us)
Sparse Core Ops, SparseCore 0:
  10.8 68.9 all-gather.4
  82.5 60.7 all-gather.6
  258.1 101.2 reduce-scatter.1

commit v3 on v2

v3 whole, which is shorter than its diff:
```python
import functools

import jax
import jax.numpy as jnp
import numpy as np
from jax import lax
from jax.experimental import pallas as pl
from jax.experimental.pallas import tpu as pltpu
from jax.sharding import PartitionSpec as P

HEADS = 12
HEAD_DIM = 64
BLOCK = 128
HALO = 384
VMEM_GRANT = 60 * 1024 * 1024

SLOPES = [2.0 ** (-(level + 1)) for level in range(8)] + [
    2.0 ** (-(level + 0.5)) for level in range(4)
]
LN_EPS = 1e-05
BETA_ONE = 0.9
BETA_TWO = 0.999
ADAM_EPS = 1e-08
CORR_ONE = 1.0 - 0.9**10
CORR_TWO = 1.0 - 0.999**10
RATE_MAT = 0.05
RATE_VEC = 0.5
DECAY_MAT = 0.01

SHORT = pl.CostEstimate(flops=1000, bytes_accessed=1000, transcendentals=0)

BF16 = jnp.bfloat16
F32 = jnp.float32


def dot_nn(left, right):
    return lax.dot_general(left, right, (((1,), (0,)), ((), ())), preferred_element_type=F32)


def dot_nt(left, right):
    return lax.dot_general(left, right, (((1,), (1,)), ((), ())), preferred_element_type=F32)


def dot_tn(left, right):
    return lax.dot_general(left, right, (((0,), (0,)), ((), ())), preferred_element_type=F32)


def part_copies(parts, plan, whole, sems, first):
    copies = []
    for number, (part, lead, row, rows, to_row, to_col) in enumerate(plan):
        source = parts[part] if lead is None else parts[part].at[lead]
        cols = source.shape[1]
        copies.append(
            pltpu.make_async_copy(
                source.at[pl.ds(row, rows), :],
                whole.at[pl.ds(to_row, rows), pl.ds(to_col, cols)],
                sems.at[first + number],
            )
        )
    return copies


def aligned(value, unit):
    return value if isinstance(value, int) else pl.multiple_of(value, unit)


def qkv_kernel(plan_of, n_pieces, window_ref, *refs):
    pieces = refs[:n_pieces]
    pairs_ref, whole_ref, sems = refs[n_pieces:]

    @pl.when(pl.program_id(0) == 0)
    def _():
        copies = part_copies(pieces, plan_of(), whole_ref, sems, 0)
        for copy in copies:
            copy.start()
        for copy in copies:
            copy.wait()

    rows = window_ref[...]
    for third in range(3):
        width = 6 * BLOCK
        part = dot_nn(rows, whole_ref[:, third * width : (third + 1) * width]).astype(BF16)
        for pair in range(6):
            pairs_ref[third * 6 + pair] = part[:, pair * BLOCK : (pair + 1) * BLOCK]


def qkv_call(window, pieces, plan_of, n_copies):
    rows, width = window.shape
    tile = HALO
    return pl.pallas_call(
        functools.partial(qkv_kernel, plan_of, len(pieces)),
        grid=(rows // tile,),
        in_specs=[pl.BlockSpec((tile, width), lambda i: (i, 0))]
        + [pl.BlockSpec(memory_space=pl.ANY)] * len(pieces),
        out_specs=[
            pl.BlockSpec((18, tile, BLOCK), lambda i: (0, i, 0)),
            pl.BlockSpec((width, 3 * width), lambda i: (0, 0)),
        ],
        out_shape=[
            jax.ShapeDtypeStruct((18, rows, BLOCK), BF16),
            jax.ShapeDtypeStruct((width, 3 * width), BF16),
        ],
        scratch_shapes=[pltpu.SemaphoreType.DMA((n_copies,))],
        compiler_params=pltpu.CompilerParams(
            dimension_semantics=("arbitrary",), vmem_limit_bytes=VMEM_GRANT
        ),
        cost_estimate=SHORT,
        name="qkv",
    )(window, *pieces)


def run_of(ids_ref, block, count):
    own = ids_ref[block]

    def same(other):
        inside = jnp.logical_and(other >= 0, other < count)
        return jnp.logical_and(inside, ids_ref[jnp.clip(other, 0, count - 1)] == own)

    before = sum(same(block - step).astype(jnp.int32) for step in (1, 2, 3))
    after = sum(same(block + step).astype(jnp.int32) for step in (1, 2, 3))
    return block - before, before + after + 1


def halves_of(rows):
    lane = lax.broadcasted_iota(jnp.int32, rows.shape, 1)
    zero = jnp.zeros_like(rows)
    return jnp.concatenate(
        (jnp.where(lane < HEAD_DIM, rows, zero), jnp.where(lane < HEAD_DIM, zero, rows)), axis=0
    )


def fill_distances(table_ref):
    shape = table_ref.shape
    key = lax.broadcasted_iota(jnp.int32, shape, 0) - 3 * BLOCK
    query = lax.broadcasted_iota(jnp.int32, shape, 1)
    table_ref[...] = jnp.abs(key - query).astype(F32)


def biased_scores(keys, query_pair, distances, slope_one, slope_two):
    bias = jnp.concatenate((distances * slope_one, distances * slope_two), axis=1)
    return dot_nt(keys, query_pair) - bias


def untwine(both):
    mine = jnp.concatenate(
        (both[:HEAD_DIM, :BLOCK], both[HEAD_DIM:, BLOCK:]), axis=0
    )
    return mine.T


GROUP = 3


def attend_kernel(first_own, n_own, first_group, ids_ref, slopes_ref, q_ref, k_ref, v_ref, ctx_ref, lse_ref, table_ref):
    group = first_group + pl.program_id(0)
    count = q_ref.shape[1] // BLOCK

    @pl.when(pl.program_id(0) == 0)
    def _():
        fill_distances(table_ref)

    def one_block(number, carry):
        block = number + first_own
        start, length = run_of(ids_ref, block, count)
        rows = pl.ds(pl.multiple_of(block * BLOCK, BLOCK), BLOCK)
        place = pl.ds(pl.multiple_of(number * BLOCK, BLOCK), BLOCK)
        shift = pl.multiple_of((3 - (block - start)) * BLOCK, BLOCK)

        def variant(blocks):
            width = blocks * BLOCK
            span = pl.ds(pl.multiple_of(start * BLOCK, BLOCK), width)
            distances = table_ref[pl.ds(shift, width), :]
            for pair in range(GROUP):
                head = 2 * (group * GROUP + pair)
                queries = halves_of(q_ref[pair, rows, :] * jnp.asarray(HEAD_DIM**-0.5, BF16))
                scores = biased_scores(
                    k_ref[pair, span, :], queries, distances, slopes_ref[head], slopes_ref[head + 1]
                )
                peak = jnp.max(scores, axis=0, keepdims=True)
                terms = jnp.exp(scores - peak)
                total = jnp.sum(terms, axis=0, keepdims=True)
                lse = peak + jnp.log(total)
                lse_ref[pair, 0:1, place] = lse[:, :BLOCK]
                lse_ref[pair, 1:2, place] = lse[:, BLOCK:]
                probs = (terms * (1.0 / total)).astype(BF16)
                both = dot_tn(v_ref[pair, span, :], probs)
                ctx_ref[place, pair * BLOCK : (pair + 1) * BLOCK] = untwine(both).astype(BF16)

        for blocks in (1, 2, 4):
            @pl.when(length == blocks)
            def _(blocks=blocks):
                variant(blocks)

        return carry

    lax.fori_loop(0, n_own, one_block, 0)


def attend_call(ids, slopes, pairs, own_rows, first_group, n_groups):
    rows = pairs.shape[1]
    steps = 6 // GROUP
    wide = GROUP * BLOCK
    part = lambda third: pl.BlockSpec(
        (GROUP, rows, BLOCK), lambda g: (third * steps + first_group + g, 0, 0)
    )
    smem = pl.BlockSpec(memory_space=pltpu.SMEM)
    return pl.pallas_call(
        functools.partial(attend_kernel, HALO // BLOCK, own_rows // BLOCK, first_group),
        grid=(n_groups,),
        in_specs=[smem, smem, part(0), part(1), part(2)],
        out_specs=[
            pl.BlockSpec((own_rows, wide), lambda g: (0, g)),
            pl.BlockSpec((GROUP, 2, own_rows), lambda g: (g, 0, 0)),
        ],
        out_shape=[
            jax.ShapeDtypeStruct((own_rows, n_groups * wide), BF16),
            jax.ShapeDtypeStruct((n_groups * GROUP, 2, own_rows), F32),
        ],
        scratch_shapes=[pltpu.VMEM((7 * BLOCK, BLOCK), F32)],
        compiler_params=pltpu.CompilerParams(
            dimension_semantics=("arbitrary",), vmem_limit_bytes=VMEM_GRANT
        ),
        cost_estimate=SHORT,
        name="attend",
    )(ids, slopes, pairs, pairs, pairs)


def attend_back_kernel(
    first_own, n_own, first_group, ids_ref, slopes_ref, q_ref, k_ref, v_ref, stats_ref, dctx_ref,
    dq_ref, dk_ref, dv_ref, table_ref, dk_sum, dv_sum,
):
    group = first_group + pl.program_id(0)
    count = q_ref.shape[1] // BLOCK

    @pl.when(pl.program_id(0) == 0)
    def _():
        fill_distances(table_ref)

    dk_sum[...] = jnp.zeros_like(dk_sum)
    dv_sum[...] = jnp.zeros_like(dv_sum)
    end_own = first_own + n_own

    def one_block(block, carry):
        start, length = run_of(ids_ref, block, count)
        own = jnp.logical_and(block >= first_own, block < end_own)
        key_start = jnp.where(own, start, jnp.maximum(start, first_own))
        key_end = jnp.where(own, start + length, jnp.minimum(start + length, end_own))
        n_keys = key_end - key_start
        rows = pl.ds(pl.multiple_of(block * BLOCK, BLOCK), BLOCK)
        place = pl.ds(pl.multiple_of(block * BLOCK, BLOCK), BLOCK)
        shift = pl.multiple_of((3 - (block - key_start)) * BLOCK, BLOCK)

        def variant(blocks):
            width = blocks * BLOCK
            span = pl.ds(pl.multiple_of(key_start * BLOCK, BLOCK), width)
            distances = table_ref[pl.ds(shift, width), :]
            for pair in range(GROUP):
                head = 2 * (group * GROUP + pair)
                lanes = slice(pair * BLOCK, (pair + 1) * BLOCK)
                keys = k_ref[pair, span, :]
                queries = halves_of(q_ref[pair, rows, :] * jnp.asarray(HEAD_DIM**-0.5, BF16))
                scores = biased_scores(
                    keys, queries, distances, slopes_ref[head], slopes_ref[head + 1]
                )
                lse = jnp.concatenate(
                    (stats_ref[pair, 0:1, rows], stats_ref[pair, 1:2, rows]), axis=1
                )
                inner = jnp.concatenate(
                    (stats_ref[pair, 2:3, rows], stats_ref[pair, 3:4, rows]), axis=1
                )
                soft = jnp.exp(scores - lse)
                dctx = halves_of(dctx_ref[rows, lanes])
                dsoft = dot_nt(v_ref[pair, span, :], dctx)
                dv_sum[pair, span, :] += dot_nn(soft.astype(BF16), dctx)
                dscores = (soft * (dsoft - inner)).astype(BF16)
                dk_sum[pair, span, :] += dot_nn(dscores, queries)
                dq_ref[place, lanes] = (untwine(dot_tn(keys, dscores)) * HEAD_DIM**-0.5).astype(BF16)

        for blocks in (1, 2, 3, 4):
            @pl.when(n_keys == blocks)
            def _(blocks=blocks):
                variant(blocks)

        return carry

    lax.fori_loop(0, count, one_block, 0)
    mine = pl.ds(first_own * BLOCK, n_own * BLOCK)
    for pair in range(GROUP):
        lanes = slice(pair * BLOCK, (pair + 1) * BLOCK)
        dk_ref[:, lanes] = dk_sum[pair, mine, :].astype(BF16)
        dv_ref[:, lanes] = dv_sum[pair, mine, :].astype(BF16)


def attend_back_call(ids, slopes, pairs, stats, dctx, own_rows, first_group, n_groups):
    rows = pairs.shape[1]
    steps = 6 // GROUP
    wide = GROUP * BLOCK
    part = lambda third: pl.BlockSpec(
        (GROUP, rows, BLOCK), lambda g: (third * steps + first_group + g, 0, 0)
    )
    smem = pl.BlockSpec(memory_space=pltpu.SMEM)
    return pl.pallas_call(
        functools.partial(attend_back_kernel, HALO // BLOCK, own_rows // BLOCK, first_group),
        grid=(n_groups,),
        in_specs=[
            smem, smem, part(0), part(1), part(2),
            pl.BlockSpec((GROUP, 4, rows), lambda g: (first_group + g, 0, 0)),
            pl.BlockSpec((rows, wide), lambda g: (0, first_group + g)),
        ],
        out_specs=[pl.BlockSpec((rows, wide), lambda g: (0, g))]
        + [pl.BlockSpec((own_rows, wide), lambda g: (0, g))] * 2,
        out_shape=[jax.ShapeDtypeStruct((rows, n_groups * wide), BF16)]
        + [jax.ShapeDtypeStruct((own_rows, n_groups * wide), BF16)] * 2,
        scratch_shapes=[
            pltpu.VMEM((7 * BLOCK, BLOCK), F32),
            pltpu.VMEM((GROUP, rows, BLOCK), F32),
            pltpu.VMEM((GROUP, rows, BLOCK), F32),
        ],
        compiler_params=pltpu.CompilerParams(
            dimension_semantics=("arbitrary",), vmem_limit_bytes=VMEM_GRANT
        ),
        cost_estimate=SHORT,
        name="attend_back",
    )(ids, slopes, pairs, pairs, pairs, stats, dctx)


FF_TILE = 512


def row_mean(values):
    return jnp.mean(values, axis=1, keepdims=True)


def norm_parts(values):
    center = values - row_mean(values)
    scale = lax.rsqrt(row_mean(center * center) + LN_EPS)
    return center * scale, scale


def norm_back(grad_unit, unit, scale):
    return scale * (grad_unit - row_mean(grad_unit) - unit * row_mean(grad_unit * unit))


def column_sum(values):
    return jnp.sum(values, axis=0, keepdims=True)


def middle_kernel(plans_of, slot_of, counts, n_pieces, ctx_ref, tok_ref, cot_ref, vec_ref, *refs):
    pieces = refs[:n_pieces]
    (result_ref, hidden_ref, dgu_ref, dffn_ref, low_ref, dattn_ref, dfirst_ref, dctx_ref,
     inner_ref, sums_ref, w_out, w_gu, w_down, gate_grad, up_grad, sems) = refs[n_pieces:]
    step = pl.program_id(0)
    width = tok_ref.shape[1]
    half = width // 2
    ff = w_down.shape[0]
    slot = slot_of()

    def copies_of(which):
        target = (w_out, w_gu, w_down)[which]
        return part_copies(pieces, plans_of()[which], target, sems, sum(counts[:which]))

    def wait_for(which):
        @pl.when(step == 0)
        def _():
            for copy in copies_of(which):
                copy.wait()

    @pl.when(step == 0)
    def _():
        sums_ref[...] = jnp.zeros_like(sums_ref)
        for which in range(3):
            for copy in copies_of(which):
                copy.start()

    gain_one, shift_one = vec_ref[0:1, :], vec_ref[1:2, :]
    gain_two, shift_two = vec_ref[2:3, :], vec_ref[3:4, :]
    wait_for(0)
    attn = dot_nn(ctx_ref[...], w_out[...])
    unit_one, scale_one = norm_parts(tok_ref[...].astype(F32) + attn + vec_ref[4:5, :])
    normed = unit_one * gain_one + shift_one
    low = normed.astype(BF16)
    low_ref[...] = low
    wait_for(1)
    wait_for(2)
    ffn = jnp.zeros((low.shape[0], width), F32)
    for tile in range(ff // FF_TILE):
        cols = slice(tile * FF_TILE, (tile + 1) * FF_TILE)
        gate = dot_nn(low, w_gu[:, cols])
        up = dot_nn(low, w_gu[:, ff + tile * FF_TILE : ff + (tile + 1) * FF_TILE])
        below = 0.5 + 0.5 * lax.erf(gate * np.float32(0.5**0.5))
        gelu = gate * below
        slope = below + gate * (jnp.exp(-0.5 * gate * gate) * np.float32((2.0 * np.pi) ** -0.5))
        hidden = (gelu * up).astype(BF16)
        hidden_ref[:, cols] = hidden
        gate_grad[:, cols] = up * slope
        up_grad[:, cols] = gelu
        ffn = ffn + dot_nn(hidden, w_down[cols, :])
    unit_two, scale_two = norm_parts(normed + ffn + vec_ref[5:6, :])
    result_ref[...] = (unit_two * gain_two + shift_two).astype(BF16)
    grad = cot_ref[...].astype(F32)
    sums_ref[2:3, :] += column_sum(grad * unit_two)
    sums_ref[3:4, :] += column_sum(grad)
    dsecond = norm_back(grad * gain_two, unit_two, scale_two)
    sums_ref[5:6, :] += column_sum(dsecond)
    dffn = dsecond.astype(BF16)
    dffn_ref[slot] = dffn[:, :half]
    dffn_ref[1 - slot] = dffn[:, half:]
    dnormed = dsecond
    for tile in range(ff // FF_TILE):
        cols = slice(tile * FF_TILE, (tile + 1) * FF_TILE)
        ups = slice(ff + tile * FF_TILE, ff + (tile + 1) * FF_TILE)
        dhidden = dot_nt(dffn, w_down[cols, :])
        dgate = (dhidden * gate_grad[:, cols]).astype(BF16)
        dup = (dhidden * up_grad[:, cols]).astype(BF16)
        chunk, place = divmod(tile * FF_TILE, ff // 2)
        dgu_ref[slot, chunk, :, place : place + FF_TILE] = dgate
        dgu_ref[1 - slot, chunk, :, place : place + FF_TILE] = dup
        dnormed = dnormed + dot_nt(dgate, w_gu[:, cols]) + dot_nt(dup, w_gu[:, ups])
    sums_ref[0:1, :] += column_sum(dnormed * unit_one)
    sums_ref[1:2, :] += column_sum(dnormed)
    dfirst = norm_back(dnormed * gain_one, unit_one, scale_one)
    sums_ref[4:5, :] += column_sum(dfirst)
    dfirst_ref[...] = dfirst
    dattn = dfirst.astype(BF16)
    dattn_ref[...] = dattn
    dctx = dot_nt(dattn, w_out[...]).astype(BF16)
    dctx_ref[...] = dctx
    head = lax.broadcasted_iota(jnp.int32, (16, width), 0)
    column = lax.broadcasted_iota(jnp.int32, (16, width), 1)
    member = jnp.where(column // HEAD_DIM == head, 1.0, 0.0).astype(BF16)
    product = dctx.astype(F32) * ctx_ref[...].astype(F32)
    high = product.astype(BF16)
    rest = (product - high.astype(F32)).astype(BF16)
    inner_ref[...] = dot_nt(member, high) + dot_nt(member, rest)


def middle_call(ctx, tokens, cotangent, vectors, pieces, plans_of, slot_of, counts):
    rows, width = tokens.shape
    ff = 4 * width
    tile = 256
    by_rows = lambda cols: pl.BlockSpec((tile, cols), lambda i: (i, 0))
    paired = lambda cols: pl.BlockSpec((2, tile, cols), lambda i: (0, i, 0))
    shaped = lambda cols, dtype: jax.ShapeDtypeStruct((rows, cols), dtype)
    return pl.pallas_call(
        functools.partial(middle_kernel, plans_of, slot_of, counts, len(pieces)),
        grid=(rows // tile,),
        in_specs=[by_rows(width)] * 3
        + [pl.BlockSpec((8, width), lambda i: (0, 0))]
        + [pl.BlockSpec(memory_space=pl.ANY)] * len(pieces),
        out_specs=[
            by_rows(width), by_rows(ff),
            pl.BlockSpec((2, 2, tile, ff // 2), lambda i: (0, 0, i, 0)),
            paired(width // 2), by_rows(width),
            by_rows(width), by_rows(width), by_rows(width),
            pl.BlockSpec((16, tile), lambda i: (0, i)),
            pl.BlockSpec((8, width), lambda i: (0, 0)),
        ],
        out_shape=[
            shaped(width, BF16), shaped(ff, BF16), jax.ShapeDtypeStruct((2, 2, rows, ff // 2), BF16),
            jax.ShapeDtypeStruct((2, rows, width // 2), BF16), shaped(width, BF16),
            shaped(width, BF16), shaped(width, F32),
            shaped(width, BF16),
            jax.ShapeDtypeStruct((16, rows), F32),
            jax.ShapeDtypeStruct((8, width), F32),
        ],
        scratch_shapes=[
            pltpu.VMEM((width, width), BF16),
            pltpu.VMEM((width, 2 * ff), BF16),
            pltpu.VMEM((ff, width), BF16),
            pltpu.VMEM((tile, ff), F32),
            pltpu.VMEM((tile, ff), F32),
            pltpu.SemaphoreType.DMA((sum(counts),)),
        ],
        compiler_params=pltpu.CompilerParams(
            dimension_semantics=("arbitrary",), vmem_limit_bytes=VMEM_GRANT
        ),
        cost_estimate=SHORT,
        name="middle",
    )(ctx, tokens, cotangent, vectors, *pieces)


def collect_kernel(plan_of, n_parts, *refs):
    parts, wholes = refs[:n_parts], refs[n_parts : n_parts + 5]
    total_ref, sems = refs[n_parts + 5 :]
    copies = []
    for number, entry in enumerate(plan_of()):
        part, row, rows, col, cols, whole, to_row, to_col = entry
        copies.append(
            pltpu.make_async_copy(
                parts[part].at[pl.ds(row, rows), pl.ds(col, cols)],
                wholes[whole].at[pl.ds(to_row, rows), pl.ds(to_col, cols)],
                sems.at[number],
            )
        )
    for copy in copies:
        copy.start()
    for copy in copies:
        copy.wait()
    total = jnp.zeros((1, 1), F32)
    for whole in wholes:
        values = whole[...].astype(F32)
        total = total + jnp.sum(jnp.sum(values * values, axis=0, keepdims=True), axis=1, keepdims=True)
    total_ref[...] = jnp.broadcast_to(total, total_ref.shape)


def collect_call(parts, plan_of, n_copies, shapes):
    vmem = pl.BlockSpec(memory_space=pltpu.VMEM)
    return pl.pallas_call(
        functools.partial(collect_kernel, plan_of, len(parts)),
        in_specs=[pl.BlockSpec(memory_space=pl.ANY)] * len(parts),
        out_specs=[vmem] * 6,
        out_shape=[jax.ShapeDtypeStruct(shape, BF16) for shape in shapes]
        + [jax.ShapeDtypeStruct((8, BLOCK), F32)],
        scratch_shapes=[pltpu.SemaphoreType.DMA((n_copies,))],
        compiler_params=pltpu.CompilerParams(vmem_limit_bytes=VMEM_GRANT),
        cost_estimate=SHORT,
        name="collect",
    )(*parts)


def adam_kernel(factor_ref, *refs):
    masters, firsts, seconds, grads, outs = (
        refs[:5], refs[5:10], refs[10:15], refs[15:20], refs[20:]
    )
    factor = factor_ref[0]
    for index in range(5):
        rate, decay = (RATE_MAT, DECAY_MAT) if index < 4 else (RATE_VEC, 0.0)
        new_ref, first_ref, second_ref, copy_ref = outs[4 * index : 4 * index + 4]
        master = masters[index][...]
        clipped = grads[index][...].astype(F32) * factor
        first = BETA_ONE * firsts[index][...] + (1.0 - BETA_ONE) * clipped
        second = BETA_TWO * seconds[index][...] + (1.0 - BETA_TWO) * clipped * clipped
        direction = first / CORR_ONE / (jnp.sqrt(second / CORR_TWO) + ADAM_EPS)
        new = master - rate * (direction + decay * master)
        new_ref[...] = new
        first_ref[...] = first
        second_ref[...] = second
        copy_ref[...] = new.astype(BF16)


def adam_call(masters, firsts, seconds, grads, factor):
    steps = 6

    def spec(array, index):
        rows, cols = array.shape
        if index == 4:
            return pl.BlockSpec((rows, cols), lambda i: (0, 0))
        return pl.BlockSpec((rows, cols // steps), lambda i: (0, i))

    specs = [spec(array, index) for index, array in enumerate(masters)]
    return pl.pallas_call(
        adam_kernel,
        grid=(steps,),
        in_specs=[pl.BlockSpec(memory_space=pltpu.SMEM)] + specs * 4,
        out_specs=[one for one in specs for _ in range(4)],
        out_shape=[
            jax.ShapeDtypeStruct(array.shape, dtype)
            for array in masters
            for dtype in (F32, F32, F32, BF16)
        ],
        compiler_params=pltpu.CompilerParams(
            dimension_semantics=("arbitrary",), vmem_limit_bytes=VMEM_GRANT
        ),
        cost_estimate=SHORT,
        name="adam",
    )(factor, *masters, *firsts, *seconds, *grads)


def halo_window(rows, groups):
    left = lax.ppermute(rows[-HALO:], "head", [(i, i + 1) for i in range(groups - 1)])
    right = lax.ppermute(rows[:HALO], "head", [(i + 1, i) for i in range(groups - 1)])
    return jnp.concatenate((left, rows, right), axis=0)


def halo_stats(lse, inner, groups):
    stats = jnp.concatenate((lse, inner[:HEADS].reshape(6, 2, -1)), axis=1)
    left = lax.ppermute(stats[:, :, -HALO:], "head", [(i, i + 1) for i in range(groups - 1)])
    right = lax.ppermute(stats[:, :, :HALO], "head", [(i + 1, i) for i in range(groups - 1)])
    return jnp.concatenate((left, stats, right), axis=2)


def slope_table():
    return jnp.asarray(np.array(SLOPES), F32)


def window_ids(segment_ids, own_rows):
    block_ids = segment_ids.reshape(-1, BLOCK)[:, 0]
    edge = HALO // BLOCK
    padded = jnp.pad(block_ids, (edge, edge), constant_values=-1)
    own_blocks = own_rows // BLOCK
    return lax.dynamic_slice_in_dim(
        padded, lax.axis_index("head") * own_blocks, own_blocks + 2 * edge
    )


def updated(masters, firsts, seconds, shards, grad_norm, clip_norm):
    factor = jnp.minimum(1.0, clip_norm / grad_norm)
    return adam_call(masters, firsts, seconds, shards, factor)


def plain_body(tokens, segment_ids, cotangent, clip_norm, *state):
    masters, firsts, seconds = state[:5], state[5:10], state[10:]
    groups = lax.axis_size("head")
    own_rows, width = tokens.shape
    low = [w.astype(BF16) for w in masters]
    window = halo_window(tokens, groups)
    full = [lax.all_gather(w, "dp", axis=0, tiled=True) for w in low[:4]]
    full_vec = lax.all_gather(low[4], "dp", axis=1, tiled=True)
    vectors = jnp.pad(full_vec.astype(F32), ((0, 2), (0, 0)))
    slopes = slope_table()
    ids = window_ids(segment_ids, own_rows)

    def whole_plan(part, rows):
        return [(part, None, 0, rows, 0, 0)]

    pairs, whole_qkv = qkv_call(window, [full[0]], lambda: whole_plan(0, width), 1)
    ctx, lse = attend_call(ids, slopes, pairs, own_rows, 0, 6 // GROUP)
    result, hidden, dgu, dffn, normed_low, dattn, dfirst, dctx, inner, sums = middle_call(
        ctx, tokens, cotangent, vectors, full[1:],
        lambda: (whole_plan(0, width), whole_plan(1, width), whole_plan(2, 4 * width)),
        lambda: 0, (1, 1, 1),
    )
    joined_back = lambda two: jnp.concatenate((two[0], two[1]), axis=1)
    grad_down = dot_tn(hidden, joined_back(dffn)).astype(BF16)
    grad_gu = dot_tn(normed_low, jnp.concatenate((dgu[0, 0], dgu[0, 1], dgu[1, 0], dgu[1, 1]), axis=1)).astype(BF16)
    grad_out = dot_tn(ctx, dattn).astype(BF16)
    dctx_window = halo_window(dctx, groups)
    stats = halo_stats(lse, inner, groups)
    dq, dk, dv = attend_back_call(ids, slopes, pairs, stats, dctx_window, own_rows, 0, 6 // GROUP)
    dq = dq[HALO:-HALO]
    djoined = jnp.concatenate((dq, dk, dv), axis=1)
    grad_qkv = dot_tn(tokens, djoined).astype(BF16)
    grad_input = dfirst + dot_nt(djoined, whole_qkv)

    def reduced(grad):
        share = lax.psum_scatter(grad, "dp", scatter_dimension=0, tiled=True)
        return lax.psum(share, "head").astype(F32)

    shards = [reduced(grad) for grad in (grad_qkv, grad_out, grad_gu, grad_down)]
    vec_sum = lax.psum(sums[:6], ("dp", "head"))
    vec_cols = masters[4].shape[1]
    shards.append(
        lax.dynamic_slice_in_dim(vec_sum, lax.axis_index("dp") * vec_cols, vec_cols, axis=1)
    )
    squares = sum(jnp.sum(piece * piece) for piece in shards)
    grad_norm = jnp.sqrt(lax.psum(squares, "dp")).reshape(1)
    updates = updated(masters, firsts, seconds, shards, grad_norm, clip_norm)
    return (result, grad_input, *updates, grad_norm)


SWAP_CORE = ("head", [(i, i ^ 1) for i in range(4)])
SWAP_X = ("head", [(i, i ^ 2) for i in range(4)])
SWAP_Y = ("dp", [(i, i ^ 1) for i in range(8)])
SWAP_Z = [None] + [("dp", [(i, i ^ (2 * step)) for i in range(8)]) for step in (1, 2, 3)]


MIDDLE_Z = ("dp", [(2, 4), (3, 5), (4, 2), (5, 3)])
OUTWARD_Z = ("dp", [(2, 0), (3, 1), (4, 6), (5, 7)])


def swap(values, how):
    return lax.ppermute(values, *how)


def position():
    dp, head = lax.axis_index("dp"), lax.axis_index("head")
    return dp // 2, dp % 2, head // 2, head % 2


def half_of(values, which, axis):
    size = values.shape[axis] // 2
    return lax.dynamic_slice_in_dim(values, which * size, size, axis)


def together(*values):
    return lax.optimization_barrier(values)


def slab_sum(mine, other):
    return (mine.astype(F32) + other.astype(F32)).astype(BF16)


def split(values, which, axis):
    return (
        lax.dynamic_index_in_dim(values, which, axis, keepdims=False),
        lax.dynamic_index_in_dim(values, 1 - which, axis, keepdims=False),
    )


def split_y(values, y):
    return split(values.reshape(4, 2, *values.shape[1:]), y, 1)


def trade(values, axis):
    return lax.all_to_all(values, axis, split_axis=0, concat_axis=0, tiled=True)


def cube_body(tokens, segment_ids, cotangent, clip_norm, *state):
    masters, firsts, seconds = state[:5], state[5:10], state[10:]
    groups = lax.axis_size("head")
    own_rows, width = tokens.shape
    ff = 4 * width
    half = width // 2
    shard = width // 8
    z, y, x, core = position()
    low = [w.astype(BF16) for w in masters]
    slopes = slope_table()
    ids = window_ids(segment_ids, own_rows)

    own_q = half_of(low[0], core, 1)
    own_g = half_of(half_of(low[2], core, 1), x, 0)
    vec_rows = jnp.pad(low[4], ((0, 10), (0, half - shard)))
    own_r = jnp.concatenate((half_of(low[3], core, 1), half_of(low[1], core, 1), vec_rows), axis=0)
    rest_rows = own_r.shape[0]

    def pair_of(own):
        return jnp.stack((own, swap(own, SWAP_Z[1])))

    pair_q, pair_r, own_g = together(pair_of(own_q), pair_of(own_r), own_g)

    mid_q = swap(pair_q, MIDDLE_Z)
    pair_y_q = swap(pair_q, SWAP_Y)
    pair_g = pair_of(own_g)
    window = halo_window(tokens, groups)
    mid_q, pair_y_q, pair_g, pair_r, window = together(mid_q, pair_y_q, pair_g, pair_r, window)

    end_q = swap(mid_q, OUTWARD_Z)
    mid_g = swap(pair_g, MIDDLE_Z)
    pair_y_g = swap(pair_g, SWAP_Y)
    xpair_g = swap(pair_g, SWAP_X)
    near_q = [pair_q, pair_y_q]
    across_q = [swap(part, SWAP_CORE) for part in near_q]
    end_q, mid_g, pair_y_g, pair_g, xpair_g, pair_r, *rest = together(
        end_q, mid_g, pair_y_g, pair_g, xpair_g, pair_r, *near_q, *across_q
    )
    near_q, across_q = rest[:2], rest[2:]

    other_q = mid_q + end_q
    other_y_q = swap(other_q, SWAP_Y)
    end_g = swap(mid_g, OUTWARD_Z)
    mid_r = swap(pair_r, MIDDLE_Z)
    xpair_y_g = swap(pair_y_g, SWAP_X)
    other_q, other_y_q, end_g, xpair_y_g, mid_r, pair_r = together(
        other_q, other_y_q, end_g, xpair_y_g, mid_r, pair_r
    )

    other_g = mid_g + end_g
    other_y_g = swap(other_g, SWAP_Y)
    end_r = swap(mid_r, OUTWARD_Z)
    xother_g = swap(other_g, SWAP_X)
    late_q = [other_q, other_y_q]
    late_across_q = [swap(part, SWAP_CORE) for part in late_q]

    def pair_rows(z, y):
        near = z + 1 - 2 * (z % 2)
        far_one, far_two = 2 - z // 2, 3 - 3 * (z // 2)
        first = [[z * 2 + y, near * 2 + y], [z * 2 + 1 - y, near * 2 + 1 - y]]
        return first + [
            [far_one * 2 + y, far_two * 2 + y], [far_one * 2 + 1 - y, far_two * 2 + 1 - y]
        ]

    def qkv_plan():
        z, y, _, core = position()
        plan = []
        for swapped in (0, 1):
            col = aligned((core + swapped * (1 - 2 * core)) * (3 * half), BLOCK)
            for part, rows in enumerate(pair_rows(z, y)):
                for index, dp in enumerate(rows):
                    plan.append((part + 4 * swapped, index, 0, shard, aligned(dp * shard, 32), col))
        return plan

    pairs, whole_qkv = qkv_call(window, near_q + late_q + across_q + late_across_q, qkv_plan, 16)
    pairs, other_g, other_y_g, end_r = together(pairs, other_g, other_y_g, end_r)

    xother_y_g = swap(other_y_g, SWAP_X)
    other_r = mid_r + end_r
    pair_y_r, other_y_r = swap(pair_r, SWAP_Y), swap(other_r, SWAP_Y)
    near_r = [pair_r, other_r]
    across_r = [swap(part, SWAP_CORE) for part in near_r]
    near_g = [pair_g, pair_y_g, other_g, other_y_g, xpair_g, xpair_y_g]
    across_g = [swap(part, SWAP_CORE) for part in near_g]
    ctx, lse = attend_call(ids, slopes, pairs, own_rows, 0, 2)
    ctx, lse, xother_g, xother_y_g, pair_y_r, other_y_r, *rest = together(
        ctx, lse, xother_g, xother_y_g, pair_y_r, other_y_r, *near_r, *across_r, *across_g
    )
    near_r, across_r, across_g = rest[:2], rest[2:4], rest[4:]
    late_g = [xother_g, xother_y_g]
    parts_g = near_g + late_g + across_g + [swap(part, SWAP_CORE) for part in late_g]
    parts_r = [near_r[0], pair_y_r, near_r[1], other_y_r]
    order = jnp.stack([index for indices in pair_rows(z, y) for index in indices])
    vec_all = jnp.concatenate([part[:, rest_rows - 16 : rest_rows - 8, :shard] for part in parts_r])
    vec_all = vec_all.astype(F32)
    parts_r = parts_r + [
        across_r[0], swap(pair_y_r, SWAP_CORE), across_r[1], swap(other_y_r, SWAP_CORE)
    ]
    vectors = jnp.zeros_like(vec_all).at[order].set(vec_all).transpose(1, 0, 2).reshape(8, width)

    def middle_plans():
        z, y, x, core = position()
        rows_of = pair_rows(z, y)
        out_plan, gu_plan, down_plan = [], [], []
        for swapped in (0, 1):
            side = core + swapped * (1 - 2 * core)
            for part in range(4):
                for index, dp in enumerate(rows_of[part]):
                    col = aligned(side * half, BLOCK)
                    place = (16 + 4 * swapped + part, index)
                    out_plan.append((*place, ff // 8, shard, aligned(dp * shard, 32), col))
                    down_plan.append((*place, 0, ff // 8, aligned(dp * (ff // 8), BLOCK), col))
            for flipped in (0, 1):
                rows_half = x + flipped * (1 - 2 * x)
                for part in range(4):
                    for index, dp in enumerate(rows_of[part]):
                        place = (4 * flipped + part, index)
                        row = aligned(dp * shard + rows_half * (shard // 2), 16)
                        gu_plan.append(
                            (8 * swapped + place[0], place[1], 0, shard // 2, row, aligned(side * ff, BLOCK))
                        )
        return out_plan, gu_plan, down_plan

    result, hidden, dgu, dffn, normed_low, dattn, dfirst, dctx, inner, sums = middle_call(
        ctx, tokens, cotangent, vectors, parts_g + parts_r,
        middle_plans, lambda: position()[3], (16, 32, 16),
    )

    def core_keep(left, right, theirs):
        return (dot_tn(left, right) + theirs.astype(F32)).astype(BF16)

    their_down = swap(dot_tn(hidden, dffn[1]).astype(BF16), SWAP_CORE)
    one_theirs = swap(dot_tn(normed_low, dgu[1, 0]).astype(BF16), SWAP_CORE)
    two_theirs = dot_tn(normed_low, dgu[1, 1]).astype(BF16)
    their_down, one_theirs, two_theirs, hidden, normed_low = together(
        their_down, one_theirs, two_theirs, hidden, normed_low
    )
    two_theirs = swap(two_theirs, SWAP_CORE)
    sum_down = core_keep(hidden, dffn[0], their_down)
    sum_one = core_keep(normed_low, dgu[0, 0], one_theirs).reshape(8, 2, shard // 2, ff // 2)
    sum_down, sum_one, two_theirs, normed_low = together(sum_down, sum_one, two_theirs, normed_low)
    share_down = lax.psum_scatter(sum_down, "dp", scatter_dimension=0, tiled=True)

    def core_rows(grad):
        mine, away = split(grad.reshape(8, 2, shard // 2, grad.shape[1]), core, 1)
        return slab_sum(mine, swap(away, SWAP_CORE))

    def z_send(values):
        others = (z + 1 - 2 * (z % 2), (z + 2) % 4, 3 - z)
        return [
            swap(lax.dynamic_index_in_dim(values, other, 0, keepdims=False), SWAP_Z[step])
            for step, other in zip((1, 2, 3), others)
        ]

    def z_sum(values, theirs):
        total = lax.dynamic_index_in_dim(values, z, 0, keepdims=False).astype(F32)
        for other in theirs:
            total = total + other.astype(F32)
        return total.astype(BF16)

    def qkv_grad(back):
        joined = jnp.concatenate((back[0][HALO:-HALO], back[1], back[2]), axis=1)
        return core_rows(dot_tn(tokens, joined).astype(BF16))

    cut = ff // 2
    one, one_away = split(sum_one, x, 1)
    two, two_away = split_y(core_keep(normed_low, dgu[0, 1], two_theirs).reshape(8, shard, cut), y)
    dctx_window = halo_window(dctx, groups)
    stats = halo_stats(lse, inner, groups)
    one, one_away, two, two_away, dctx_window, stats = together(
        one, one_away, two, two_away, dctx_window, stats
    )
    one_their = swap(one_away, SWAP_X)
    two_their = swap(two_away, SWAP_Y)
    vec_cols = jnp.pad(sums.astype(BF16).T, ((0, 0), (0, BLOCK - 8)))
    sum_ov = core_rows(jnp.concatenate((dot_tn(ctx, dattn).astype(BF16), vec_cols), axis=1))
    back_a = attend_back_call(ids, slopes, pairs, stats, dctx_window, own_rows, 0, 1)
    one_their, two_their, dctx_window, sum_ov, *back_a = together(
        one_their, two_their, dctx_window, sum_ov, *back_a
    )
    two = slab_sum(two, two_their)
    two_their = z_send(two)
    one = jnp.concatenate((slab_sum(one, one_their), qkv_grad(back_a), sum_ov), axis=2)
    one, one_away = split_y(one, y)
    one_their = swap(one_away, SWAP_Y)
    back_b = attend_back_call(ids, slopes, pairs, stats, dctx_window, own_rows, 1, 1)
    one_their, share_down, *rest = together(one_their, share_down, *two_their, *back_b)
    two_their, back_b = rest[:3], rest[3:]

    one = slab_sum(one, one_their)
    one_their = z_send(one)
    grad_b = trade(qkv_grad(back_b), "dp")
    two_mine = z_sum(two, two_their)
    two_other = swap(two_mine, SWAP_X)
    down_other = swap(share_down, SWAP_X)
    djoined = jnp.concatenate(
        (back_a[0][HALO:-HALO], back_b[0][HALO:-HALO], back_a[1], back_b[1], back_a[2], back_b[2]), axis=1
    )
    grad_input = dfirst + dot_nt(djoined, whole_qkv)
    grad_b, two_other, down_other, grad_input, *one_their = together(
        grad_b, two_other, down_other, grad_input, *one_their
    )
    b_mine = jnp.sum(grad_b.astype(F32), axis=0).astype(BF16)
    one_mine = jnp.concatenate((z_sum(one, one_their), b_mine), axis=1)
    one_other = swap(one_mine, SWAP_X)
    two_sum, down_sum = slab_sum(two_mine, two_other), slab_sum(share_down, down_other)
    two_across, down_across = swap(two_sum, SWAP_CORE), swap(down_sum, SWAP_CORE)
    rest_sum = slab_sum(one_mine[:, cut:], one_other[:, cut:])
    parts = [
        one_mine, one_other, rest_sum, two_sum, down_sum,
        swap(one_mine, SWAP_CORE), swap(one_other, SWAP_CORE), swap(rest_sum, SWAP_CORE),
        two_across, down_across,
    ]

    def collect_plan():
        _, _, x, core = position()
        rows = shard // 2
        plan = []
        for swapped in (0, 1):
            side = core + swapped * (1 - 2 * core)
            first = 5 * swapped
            for flipped in (0, 1):
                to_row = aligned((x + flipped * (1 - 2 * x)) * rows, 16)
                plan.append((first + flipped, 0, rows, 0, cut, 2, to_row, aligned(side * ff, BLOCK)))
            plan.append((first + 3, 0, shard, 0, cut, 2, 0, aligned(side * ff + cut, BLOCK)))
            plan.append((first + 4, 0, ff // 8, 0, half, 3, 0, aligned(side * half, BLOCK)))
            to_row = aligned(side * rows, 16)
            later = 3 * half + width + BLOCK
            for third in range(3):
                for part in (0, 1):
                    plan.append(
                        (first + 2, 0, rows, part * later + third * half, half, 0, to_row,
                         third * width + part * half)
                    )
            plan.append((first + 2, 0, rows, 3 * half, width, 1, to_row, 0))
            plan.append((first + 2, 0, rows, 3 * half + width, BLOCK, 4, to_row, 0))
        return plan

    *shards, squares = collect_call(
        parts, collect_plan, 24,
        [(shard, 3 * width), (shard, width), (shard, 2 * ff), (ff // 8, width), (shard, BLOCK)],
    )
    shards[4] = shards[4][:, :6].T
    squares = squares[:1]
    for how in (SWAP_Y, SWAP_Z[1], SWAP_Z[2]):
        squares = squares + swap(squares, how)
    grad_norm = jnp.sqrt(squares[0, :1])
    updates = updated(masters, firsts, seconds, shards, grad_norm, clip_norm)
    return (result, grad_input, *updates, grad_norm)


def solution(mesh):
    rows_split = P(("dp", "head"), None)
    mats, vecs = P("dp", None), P(None, "dp")
    state = (mats,) * 4 + (vecs,)
    in_specs = (rows_split, P("dp"), rows_split, P()) + state * 3
    out_specs = (rows_split, rows_split) + (mats,) * 16 + (vecs,) * 4 + (P(),)
    cube = mesh.shape["dp"] == 8 and mesh.shape["head"] == 4
    body = cube_body if cube else plain_body
    return jax.shard_map(body, mesh=mesh, in_specs=in_specs, out_specs=out_specs, check_vma=False)
```

time: 522 us -> 461 us (0.88)
  local copies, waits for them, and re-layouts: 83.5 us -> 34.1 us
  waiting for transfers between devices: 123 us -> 147 us
  Pallas kernels: 129 us -> 114 us
  starting transfers between devices: 89.5 us -> 75 us
  other arithmetic: 30.4 us -> 22.1 us
    unnamed x169 -> x133, local copies, waits for them, and re-layouts: 56 us -> 13.6 us
    all_to_all x0 -> x1, waiting for transfers between devices: none -> 25.6 us  [trade(): return lax.all_to_all(values, axis, split_axis=0, concat_axis=0, tiled=True)]
    ppermute x51 -> x61, starting transfers between devices: 83 us -> 60.6 us  [swap(): return lax.ppermute(values, *how)]
    pallas_call x2, Pallas kernels: 40.4 us -> 25.1 us  [attend_back_call(): pl.pallas_call(functools.partial(attend_back_kernel, HALO // BLOCK, own_r...]
    pallas_call x1, Pallas kernels: 28.2 us -> 16.3 us  [attend_call(): pl.pallas_call(functools.partial(attend_kernel, HALO // BLOCK, own_rows /...]
    reduce_sum x5 -> x1, other arithmetic: 7.13 us -> 0.12 us  [cube_body(): b_mine = jnp.sum(grad_b.astype(F32), axis=0).astype(BF16)]
    ppermute x51 -> x61, waiting for transfers between devices: 121 us -> 114 us  [swap(): return lax.ppermute(values, *how)]
    reduce_scatter x1, waiting for transfers between devices: 0.01 us -> 6.56 us  [cube_body(): lax.psum_scatter(sum_down, 'dp', scatter_dimension=0, tiled=True)]
  transfers between devices with their start and end apart: 58 -> 69, of which waited for: 16 -> 28; matrix products, arithmetic and copies ran while one was open for 16% -> 15% of each run, Pallas kernels for 15% -> 12%
where the time goes in v3:
time: 461 us; the launch traced here: 452 us
  waiting for transfers between devices  147 us (32%)
  Pallas kernels  114 us (25%)
  starting transfers between devices  75 us (16%)
  matrix products  42.9 us (9%)
  local copies, waits for them, and re-layouts  34.1 us (7%)
  other arithmetic  22.1 us (5%)
  between operations  17.3 us (4%)
    ppermute x61, waiting for transfers between devices, swap(): return lax.ppermute(values, *how)  114 us
    ppermute x61, starting transfers between devices, swap(): return lax.ppermute(values, *how)  60.6 us
    pallas_call x1, Pallas kernels, middle_call(): pl.pallas_call(functools.partial(middle_kernel, plans_of, slot_of, counts...  44.4 us
    dot_general x9, matrix products, dot_tn(): lax.dot_general(left, right, (((0,), (0,)), ((), ())), preferred_element_...  37.8 us
    all_to_all x1, waiting for transfers between devices, trade(): return lax.all_to_all(values, axis, split_axis=0, concat_axis=0, tiled=True)  25.6 us
    pallas_call x2, Pallas kernels, attend_back_call(): pl.pallas_call(functools.partial(attend_back_kernel, HALO // BLOCK, own_r...  25.1 us
    pallas_call x1, Pallas kernels, attend_call(): pl.pallas_call(functools.partial(attend_kernel, HALO // BLOCK, own_rows /...  16.3 us
    unnamed x133, local copies, waits for them, and re-layouts  13.6 us
  transfers between devices with their start and end apart: 69, of which 28 were waited for; matrix products, arithmetic and copies ran while one was open for 15% of the time, Pallas kernels for 12%

profile of v3, /device:TPU:0, one launch (start us, length us, event | category | flops | bytes accessed | tf_op | source)
XLA Modules:
  0.0 452.4 jit_solution(6945261476601836921)
XLA Ops:
  21.2 5.7 %collective-permute-done = bf16[96,1152]{1,0:T(8,128)(2,1)} collective-permute-done((bf16[96,1152]{1,0:T(8,128)(2,1)}, bf16[96,1152]{1,0:T(8,128)(2,1)}, u32[]{:S(2)}, u32[]{:S(2)}) %collective-permute-start) | collective-permute-done | bytes 221216 | tf_op jit(solution)/shard_map/ppermute | solution.py:662
  38.2 6.1 %collective-permute-done.4 = bf16[48,3072]{1,0:T(8,128)(2,1)S(1)} collective-permute-done((bf16[48,3072]{1,0:T(8,128)(2,1)S(1)}, bf16[48,3072]{1,0:T(8,128)(2,1)S(1)}, u32[]{:S(2)}, u32[]{:S(2)}) %collective-permute-start.4) | collective-permute-done | bytes 294944 | tf_op jit(solution)/shard_map/ppermute | solution.py:662
  49.1 14.4 %collective-permute-done.7 = bf16[2,96,1152]{2,1,0:T(8,128)(2,1)S(1)} collective-permute-done((bf16[2,96,1152]{2,1,0:T(8,128)(2,1)S(1)}, bf16[2,96,1152]{2,1,0:T(8,128)(2,1)S(1)}, u32[]{:S(2)}, u32[]{:S(2)}) %collective-permute-start.7) | collective-permute-done | bytes 442400 | tf_op jit(solution)/shard_map/ppermute | solution.py:662
  67.2 10.8 %collective-permute-done.13.refs_3_ = bf16[2,96,1152]{2,1,0:T(8,128)(2,1)S(1)} collective-permute-done((bf16[2,96,1152]{2,1,0:T(8,128)(2,1)S(1)}, bf16[2,96,1152]{2,1,0:T(8,128)(2,1)S(1)}, u32[]{:S(2)}, u32[]{:S(2)}) %collective-permute-start.13) | collective-permute-done | bytes 442400 | tf_op jit(solution)/shard_map/ppermute | solution.py:662
  86.4 12.6 %collective-permute-done.19.refs_3_ = bf16[2,48,3072]{2,1,0:T(8,128)(2,1)S(1)} collective-permute-done((bf16[2,48,3072]{2,1,0:T(8,128)(2,1)S(1)}, bf16[2,48,3072]{2,1,0:T(8,128)(2,1)S(1)}, u32[]{:S(2)}, u32[]{:S(2)}) %collective-permute-start.19) | collective-permute-done | bytes 589856 | tf_op jit(solution)/shard_map/ppermute | solution.py:662
  101.6 11.8 %qkv.1 = (bf16[18,1536,128]{2,1,0:T(8,128)(2,1)}, bf16[768,2304]{1,0:T(8,128)(2,1)}) custom-call(bf16[1536,768]{1,0:T(8,128)(2,1)} %pad_maximum_fusion.1.window_ref, bf16[2,96,1152]{2,1,0:T(8,128)(2,1)} %copy-done.12, bf16[2,96,1152]{2,1,0:T(8,128)(2,1)} %copy-done.36, bf16[2,96,1152]{2,1,0:T(8,128)(2,1)} %copy-done.13, bf16[2,96,1152]{2,1,0:T(8,128)(2,1)} %copy-done.39, ...), custom_call_target="tpu_custom_call" | custom-call | flops 1000 | bytes 1000 | tf_op jit(solution)/shard_map/qkv/pallas_call | solution.py:90
  118.0 16.3 %attend.1 = (bf16[768,768]{1,0:T(8,128)(2,1)}, f32[6,2,768]{2,1,0:T(2,128)}) custom-call(s32[12]{0:T(128)} %pad_dynamic-slice_fusion.ids_ref, f32[12]{0:T(128)} %constant.179.clone.slopes_ref, bf16[18,1536,128]{2,1,0:T(8,128)(2,1)} %get-tuple-element.171.q_ref.k_ref.v_ref, bf16[18,1536,128]{2,1,0:T(8,128)(2,1)} %get-tuple-element.171.q_ref.k_ref.v_ref, ...), custom_call_target="tpu_custom_call" | custom-call | flops 1000 | bytes 1000 | tf_op jit(solution)/shard_map/attend/pallas_call | solution.py:207
  143.0 44.4 %middle.1 = (bf16[768,768]{1,0:T(8,128)(2,1)}, bf16[768,3072]{1,0:T(8,128)(2,1)}, bf16[2,2,768,1536]{3,2,1,0:T(8,128)(2,1)}, bf16[2,768,384]{2,1,0:T(8,128)(2,1)...) custom-call(bf16[768,768]{1,0:T(8,128)(2,1)} %get-tuple-element.181., ...), custom_call_target="tpu_custom_call" | custom-call | flops 1000 | bytes 1000 | tf_op jit(solution)/shard_map/middle/pallas_call | solution.py:444
  187.4 5.6 %convolution_convert_fusion.2 = bf16[768,1536]{1,0:T(8,128)(2,1)} fusion(bf16[768,768]{1,0:T(8,128)(2,1)} %get-tuple-element.207, bf16[2,2,768,1536]{3,2,1,0:T(8,128)(2,1)} %get-tuple-element.200), kind=kOutput, calls=%fused_computation.6 | convolution fusion | flops 1813118976 | bytes 5898240 | tf_op jit(solution)/shard_map/dot_general | solution.py:45
  201.3 5.5 %convolution_convert_fusion.1 = bf16[768,1536]{1,0:T(8,128)(2,1)} fusion(bf16[768,768]{1,0:T(8,128)(2,1)} %get-tuple-element.207, bf16[2,2,768,1536]{3,2,1,0:T(8,128)(2,1)} %get-tuple-element.200), kind=kOutput, calls=%fused_computation.5 | convolution fusion | flops 1813118976 | bytes 5898240 | tf_op jit(solution)/shard_map/dot_general | solution.py:45
  221.6 5.6 %add_convert_fusion.2 = bf16[3072,384]{1,0:T(8,128)(2,1)} fusion(bf16[3072,384]{1,0:T(8,128)(2,1)} %collective-permute-done.37, bf16[768,3072]{1,0:T(8,128)(2,1)S(1)} %bitcast.138, bf16[2,768,384]{2,1,0:T(8,128)(2,1)S(1)} %copy-done.60), kind=kOutput, calls=%fused_computation.3 | convolution fusion | flops 1815478272 | bytes 10027008 | tf_op jit(solution)/shard_map/dot_general | solution.py:45
  227.2 4.8 %add_convert_fusion = bf16[768,1536]{1,0:T(8,128)(2,1)S(1)} fusion(bf16[768,1536]{1,0:T(8,128)(2,1)} %collective-permute-done.39, bf16[768,768]{1,0:T(8,128)(2,1)} %get-tuple-element.207, bf16[2,2,768,1536]{3,2,1,0:T(8,128)(2,1)} %get-tuple-element.200), kind=kOutput, calls=%fused_computation.1 | convolution fusion | flops 1815478272 | bytes 8257536 | tf_op jit(solution)/shard_map/dot_general | solution.py:45
  235.1 7.5 %collective-permute-start.44 = (bf16[8,48,1536]{2,1,0:T(8,128)(2,1)}, bf16[8,48,1536]{2,1,0:T(8,128)(2,1)}, u32[]{:S(2)}, u32[]{:S(2)}) collective-permute-start(bf16[8,48,1536]{2,1,0:T(8,128)(2,1)} %get-tuple-element.213), channel_id=1, source_target_pairs={{0,2},{1,3},{2,0},{3,1},{4,6},{5,7},{6,4},{7,5},{8,10},{9,11},{10,... | collective-permute-start | bytes 3538952 | tf_op jit(solution)/shard_map/ppermute | solution.py:662
  247.6 12.6 %attend_back.2 = (bf16[1536,384]{1,0:T(8,128)(2,1)}, bf16[768,384]{1,0:T(8,128)(2,1)}, bf16[768,384]{1,0:T(8,128)(2,1)}) custom-call(s32[12]{0:T(128)} %pad_dynamic-slice_fusion.ids_ref, f32[12]{0:T(128)} %constant.179.clone.slopes_ref, bf16[18,1536,128]{2,1,0:T(8,128)(2,1)} %get-tuple-element.171.q_ref.k_ref.v_ref, ...), custom_call_target="tpu_custom_call" | custom-call | flops 1000 | bytes 1000 | tf_op jit(solution)/shard_map/attend_back/pallas_call | solution.py:302
  260.2 8.8 %collective-permute-done.44 = bf16[8,48,1536]{2,1,0:T(8,128)(2,1)} collective-permute-done((bf16[8,48,1536]{2,1,0:T(8,128)(2,1)}, bf16[8,48,1536]{2,1,0:T(8,128)(2,1)}, u32[]{:S(2)}, u32[]{:S(2)}) %collective-permute-start.44) | collective-permute-done | bytes 1179680 | tf_op jit(solution)/shard_map/ppermute | solution.py:662
  268.9 7.2 %collective-permute-done.45 = bf16[4,96,1536]{2,1,0:T(8,128)(2,1)} collective-permute-done((bf16[4,96,1536]{2,1,0:T(8,128)(2,1)}, bf16[4,96,1536]{2,1,0:T(8,128)(2,1)}, u32[]{:S(2)}, u32[]{:S(2)}) %collective-permute-start.45) | collective-permute-done | bytes 1179680 | tf_op jit(solution)/shard_map/ppermute | solution.py:662
  291.0 5.8 %collective-permute-start.49 = (bf16[96,1536]{1,0:T(8,128)(2,1)}, bf16[96,1536]{1,0:T(8,128)(2,1)}, u32[]{:S(2)}, u32[]{:S(2)}) collective-permute-start(bf16[96,1536]{1,0:T(8,128)(2,1)} %get-tuple-element.290), channel_id=1, source_target_pairs={{0,8},{4,12},{8,0},{12,4},{16,24},{20,28},{24,16},{28,20},{1,9},{5... | collective-permute-start | bytes 884744 | tf_op jit(solution)/shard_map/ppermute | solution.py:662
  299.1 12.5 %attend_back.3 = (bf16[1536,384]{1,0:T(8,128)(2,1)}, bf16[768,384]{1,0:T(8,128)(2,1)}, bf16[768,384]{1,0:T(8,128)(2,1)}) custom-call(s32[12]{0:T(128)} %pad_dynamic-slice_fusion.ids_ref, f32[12]{0:T(128)} %constant.179.clone.slopes_ref, bf16[18,1536,128]{2,1,0:T(8,128)(2,1)} %get-tuple-element.171.q_ref.k_ref.v_ref, ...), custom_call_target="tpu_custom_call" | custom-call | flops 1000 | bytes 1000 | tf_op jit(solution)/shard_map/attend_back/pallas_call | solution.py:302
  311.6 13.4 %collective-permute-done.50 = bf16[96,1536]{1,0:T(8,128)(2,1)} collective-permute-done((bf16[96,1536]{1,0:T(8,128)(2,1)S(1)}, bf16[96,1536]{1,0:T(8,128)(2,1)}, u32[]{:S(2)}, u32[]{:S(2)}) %collective-permute-start.50) | collective-permute-done | bytes 294944 | tf_op jit(solution)/shard_map/ppermute | solution.py:662
  326.3 6.6 %reduce-scatter.2.cloned.1.call-done = bf16[384,384]{1,0:T(8,128)(2,1)} async-done(((bf16[3072,384]{1,0:T(8,128)(2,1)}), bf16[384,384]{1,0:T(8,128)(2,1)}) %reduce-scatter.2.cloned.1.call-update) | async-done | bytes 294928 | tf_op jit(solution)/shard_map/reduce_scatter | solution.py:839
  359.5 5.1 %fusion.44 = f32[768,768]{1,0:T(8,128)S(1)} fusion(bf16[768,2304]{1,0:T(8,128)(2,1)} %constant_dynamic-update-slice_fusion, bf16[768,2304]{1,0:T(8,128)(2,1)S(1)} %copy-done.55), kind=kOutput, calls=%fused_computation.111 | convolution fusion | flops 2717908992 | bytes 9437184 | tf_op jit(solution)/shard_map/dot_general | solution.py:41
  371.2 25.6 %all-to-all-done = bf16[8,48,1152]{2,1,0:T(8,128)(2,1)S(1)} async-done(((bf16[8,48,1152]{2,1,0:T(8,128)(2,1)}), bf16[8,48,1152]{2,1,0:T(8,128)(2,1)S(1)}, u32[]{:S(2)}, u32[]{:S(2)}) %all-to-all-start) | async-done | bytes 884768 | tf_op jit(solution)/shard_map/all_to_all | solution.py:695
  400.9 9.1 %collective-permute-done.58.refs_1_ = bf16[48,4736]{1,0:T(8,128)(2,1)S(1)} collective-permute-done((bf16[48,4736]{1,0:T(8,128)(2,1)S(1)}, bf16[48,4736]{1,0:T(8,128)(2,1)S(1)}, u32[]{:S(2)}, u32[]{:S(2)}) %collective-permute-start.58) | collective-permute-done | bytes 454688 | tf_op jit(solution)/shard_map/ppermute | solution.py:662
  430.9 13.3 %adam.1 = (f32[96,2304]{1,0:T(8,128)}, f32[96,2304]{1,0:T(8,128)}, f32[96,2304]{1,0:T(8,128)}, bf16[96,2304]{1,0:T(8,128)(2,1)}, f32[96,768]{1,0:T(8,128)}, /*in...) custom-call(f32[1]{0:T(128)S(6)} %min.3.factor_ref, ...), custom_call_target="tpu_custom_call" | custom-call | flops 1000 | bytes 1000 | tf_op jit(solution)/shard_map/adam/pallas_call | solution.py:551
  (332 shorter events, 164.1 us)
Async XLA Ops:
  7.2 325.6 %reduce-scatter.2.cloned.1.call-start = ((), (), s32[]{:S(2)}) async-start(), calls=%async_computation.2 | async-start | bytes 2654208 | tf_op jit(solution)/shard_map/reduce_scatter | solution.py:839
  10.2 17.8 %collective-permute-start.1 = (bf16[496,384]{1,0:T(8,128)(2,1)S(1)}, bf16[496,384]{1,0:T(8,128)(2,1)S(1)}, u32[]{:S(2)}, u32[]{:S(2)}) collective-permute-start(bf16[496,384]{1,0:T(8,128)(2,1)S(1)} %get-tuple-element.296), channel_id=1, source_target_pairs={{0,8},{4,12},{8,0},{12,4},{16,24},{20,28},{24,16},{28,20},{1,9},{5... | collective-permute-start | bytes 1142792 | tf_op jit(solution)/shard_map/ppermute | solution.py:662
  17.6 19.1 %collective-permute-start.6 = (bf16[384,768]{1,0:T(8,128)(2,1)}, bf16[384,768]{1,0:T(8,128)(2,1)S(1)}, u32[]{:S(2)}, u32[]{:S(2)}) collective-permute-start(bf16[384,768]{1,0:T(8,128)(2,1)} %get-tuple-element.294), channel_id=1, source_target_pairs={{1,0},{2,1},{3,2},{5,4},{6,5},{7,6},{9,8},{10,9},{11,10},{13,12},{... | collective-permute-start | bytes 1769480 | tf_op jit(solution)/shard_map/ppermute | solution.py:571
  44.5 19.0 %collective-permute-start.10 = (bf16[2,48,3072]{2,1,0:T(8,128)(2,1)S(1)}, bf16[2,48,3072]{2,1,0:T(8,128)(2,1)S(1)}, u32[]{:S(2)}, u32[]{:S(2)}) collective-permute-start(bf16[2,48,3072]{2,1,0:T(8,128)(2,1)S(1)} %pad_maximum_fusion.4.refs_0_), channel_id=1, source_target_pairs={{0,2},{1,3},{2,0},{3,1},{4,6},{5,7},{6,4},{7,5},{8,10},{9,11},{10,... | collective-permute-start | bytes 1769480 | tf_op jit(solution)/shard_map/ppermute | solution.py:662
  63.5 17.8 %collective-permute-start.16 = (bf16[2,496,384]{2,1,0:T(8,128)(2,1)S(1)}, bf16[2,496,384]{2,1,0:T(8,128)(2,1)S(1)}, u32[]{:S(2)}, u32[]{:S(2)}) collective-permute-start(bf16[2,496,384]{2,1,0:T(8,128)(2,1)S(1)} %pad_maximum_fusion.3.refs_16_), channel_id=1, source_target_pairs={{8,16},{12,20},{16,8},{20,12},{9,17},{13,21},{17,9},{21,13},{10,18... | collective-permute-start | bytes 2285576 | tf_op jit(solution)/shard_map/ppermute | solution.py:662
  81.3 19.4 %collective-permute-start.20 = (bf16[2,496,384]{2,1,0:T(8,128)(2,1)S(1)}, bf16[2,496,384]{2,1,0:T(8,128)(2,1)S(1)}, u32[]{:S(2)}, u32[]{:S(2)}) collective-permute-start(bf16[2,496,384]{2,1,0:T(8,128)(2,1)S(1)} %collective-permute-done.16), channel_id=1, source_target_pairs={{8,0},{12,4},{16,24},{20,28},{9,1},{13,5},{17,25},{21,29},{10,2},{... | collective-permute-start | bytes 2285576 | tf_op jit(solution)/shard_map/ppermute | solution.py:662
  84.6 32.2 %collective-permute-start.23 = (bf16[2,496,384]{2,1,0:T(8,128)(2,1)S(1)}, bf16[2,496,384]{2,1,0:T(8,128)(2,1)}, u32[]{:S(2)}, u32[]{:S(2)}) collective-permute-start(bf16[2,496,384]{2,1,0:T(8,128)(2,1)S(1)} %pad_maximum_fusion.3.refs_16_), channel_id=1, source_target_pairs={{0,4},{4,0},{8,12},{12,8},{16,20},{20,16},{24,28},{28,24},{1,5},{5... | collective-permute-start | bytes 2285576 | tf_op jit(solution)/shard_map/ppermute | solution.py:662
  85.5 29.5 %collective-permute-start.31 = (bf16[2,48,3072]{2,1,0:T(8,128)(2,1)S(1)}, bf16[2,48,3072]{2,1,0:T(8,128)(2,1)}, u32[]{:S(2)}, u32[]{:S(2)}) collective-permute-start(bf16[2,48,3072]{2,1,0:T(8,128)(2,1)S(1)} %collective-permute-done.10.refs_4_), channel_id=1, source_target_pairs={{0,1},{1,0},{2,3},{3,2},{4,5},{5,4},{6,7},{7,6},{8,9},{9,8},{10,11... | collective-permute-start | bytes 1769480 | tf_op jit(solution)/shard_map/ppermute | solution.py:662
  86.2 30.6 %collective-permute-start.25 = (bf16[2,496,384]{2,1,0:T(8,128)(2,1)S(1)}, bf16[2,496,384]{2,1,0:T(8,128)(2,1)}, u32[]{:S(2)}, u32[]{:S(2)}) collective-permute-start(bf16[2,496,384]{2,1,0:T(8,128)(2,1)S(1)} %pad_maximum_fusion.3.refs_16_), channel_id=1, source_target_pairs={{0,1},{1,0},{2,3},{3,2},{4,5},{5,4},{6,7},{7,6},{8,9},{9,8},{10,11... | collective-permute-start | bytes 2285576 | tf_op jit(solution)/shard_map/ppermute | solution.py:662
  115.1 19.5 %collective-permute-start.24 = (bf16[2,496,384]{2,1,0:T(8,128)(2,1)S(1)}, bf16[2,496,384]{2,1,0:T(8,128)(2,1)S(1)}, u32[]{:S(2)}, u32[]{:S(2)}) collective-permute-start(bf16[2,496,384]{2,1,0:T(8,128)(2,1)S(1)} %add.222.refs_18_), channel_id=1, source_target_pairs={{0,4},{4,0},{8,12},{12,8},{16,20},{20,16},{24,28},{28,24},{1,5},{5... | collective-permute-start | bytes 2285576 | tf_op jit(solution)/shard_map/ppermute | solution.py:662
  116.0 18.6 %collective-permute-start.26 = (bf16[2,496,384]{2,1,0:T(8,128)(2,1)S(1)}, bf16[2,496,384]{2,1,0:T(8,128)(2,1)}, u32[]{:S(2)}, u32[]{:S(2)}) collective-permute-start(bf16[2,496,384]{2,1,0:T(8,128)(2,1)S(1)} %add.222.refs_18_), channel_id=1, source_target_pairs={{0,1},{1,0},{2,3},{3,2},{4,5},{5,4},{6,7},{7,6},{8,9},{9,8},{10,11... | collective-permute-start | bytes 2285576 | tf_op jit(solution)/shard_map/ppermute | solution.py:662
  116.2 18.0 %collective-permute-start.22 = (bf16[2,48,3072]{2,1,0:T(8,128)(2,1)}, bf16[2,48,3072]{2,1,0:T(8,128)(2,1)S(1)}, u32[]{:S(2)}, u32[]{:S(2)}) collective-permute-start(bf16[2,48,3072]{2,1,0:T(8,128)(2,1)} %copy-done.27), channel_id=1, source_target_pairs={{0,2},{1,3},{2,0},{3,1},{4,6},{5,7},{6,4},{7,5},{8,10},{9,11},{10,... | collective-permute-start | bytes 1769480 | tf_op jit(solution)/shard_map/ppermute | solution.py:662
  116.8 17.5 %collective-permute-start.29 = (bf16[2,48,3072]{2,1,0:T(8,128)(2,1)S(1)}, bf16[2,48,3072]{2,1,0:T(8,128)(2,1)}, u32[]{:S(2)}, u32[]{:S(2)}) collective-permute-start(bf16[2,48,3072]{2,1,0:T(8,128)(2,1)S(1)} %add.221.refs_2_), channel_id=1, source_target_pairs={{0,1},{1,0},{2,3},{3,2},{4,5},{5,4},{6,7},{7,6},{8,9},{9,8},{10,11... | collective-permute-start | bytes 1769480 | tf_op jit(solution)/shard_map/ppermute | solution.py:662
  206.8 20.4 %collective-permute-start.39 = (bf16[768,1536]{1,0:T(8,128)(2,1)}, bf16[768,1536]{1,0:T(8,128)(2,1)}, u32[]{:S(2)}, u32[]{:S(2)}) collective-permute-start(bf16[768,1536]{1,0:T(8,128)(2,1)} %convolution_convert_fusion.1), channel_id=1, source_target_pairs={{0,1},{1,0},{2,3},{3,2},{4,5},{5,4},{6,7},{7,6},{8,9},{9,8},{10,11... | collective-permute-start | bytes 7077896 | tf_op jit(solution)/shard_map/ppermute | solution.py:662
  235.1 33.8 %collective-permute-start.44 = (bf16[8,48,1536]{2,1,0:T(8,128)(2,1)}, bf16[8,48,1536]{2,1,0:T(8,128)(2,1)}, u32[]{:S(2)}, u32[]{:S(2)}) collective-permute-start(bf16[8,48,1536]{2,1,0:T(8,128)(2,1)} %get-tuple-element.213), channel_id=1, source_target_pairs={{0,2},{1,3},{2,0},{3,1},{4,6},{5,7},{6,4},{7,5},{8,10},{9,11},{10,... | collective-permute-start | bytes 3538952 | tf_op jit(solution)/shard_map/ppermute | solution.py:662
  242.7 33.5 %collective-permute-start.45 = (bf16[4,96,1536]{2,1,0:T(8,128)(2,1)}, bf16[4,96,1536]{2,1,0:T(8,128)(2,1)}, u32[]{:S(2)}, u32[]{:S(2)}) collective-permute-start(bf16[4,96,1536]{2,1,0:T(8,128)(2,1)} %get-tuple-element.214), channel_id=1, source_target_pairs={{0,4},{4,0},{8,12},{12,8},{16,20},{20,16},{24,28},{28,24},{1,5},{5... | collective-permute-start | bytes 3538952 | tf_op jit(solution)/shard_map/ppermute | solution.py:662
  285.7 40.5 %collective-permute-start.48 = (bf16[4,48,3584]{2,1,0:T(8,128)(2,1)}, bf16[4,48,3584]{2,1,0:T(8,128)(2,1)}, u32[]{:S(2)}, u32[]{:S(2)}) collective-permute-start(bf16[4,48,3584]{2,1,0:T(8,128)(2,1)} %dynamic-slice_bitcast_fusion), channel_id=1, source_target_pairs={{0,4},{4,0},{8,12},{12,8},{16,20},{20,16},{24,28},{28,24},{1,5},{5... | collective-permute-start | bytes 4128776 | tf_op jit(solution)/shard_map/ppermute | solution.py:662
  291.0 20.6 %collective-permute-start.49 = (bf16[96,1536]{1,0:T(8,128)(2,1)}, bf16[96,1536]{1,0:T(8,128)(2,1)}, u32[]{:S(2)}, u32[]{:S(2)}) collective-permute-start(bf16[96,1536]{1,0:T(8,128)(2,1)} %get-tuple-element.290), channel_id=1, source_target_pairs={{0,8},{4,12},{8,0},{12,4},{16,24},{20,28},{24,16},{28,20},{1,9},{5... | collective-permute-start | bytes 884744 | tf_op jit(solution)/shard_map/ppermute | solution.py:662
  296.7 28.2 %collective-permute-start.50 = (bf16[96,1536]{1,0:T(8,128)(2,1)S(1)}, bf16[96,1536]{1,0:T(8,128)(2,1)}, u32[]{:S(2)}, u32[]{:S(2)}) collective-permute-start(bf16[96,1536]{1,0:T(8,128)(2,1)S(1)} %get-tuple-element.289), channel_id=1, source_target_pairs={{0,16},{4,20},{8,24},{12,28},{16,0},{20,4},{24,8},{28,12},{1,17},{... | collective-permute-start | bytes 884744 | tf_op jit(solution)/shard_map/ppermute | solution.py:662
  296.8 28.2 %collective-permute-start.51 = (bf16[96,1536]{1,0:T(8,128)(2,1)S(1)}, bf16[96,1536]{1,0:T(8,128)(2,1)}, u32[]{:S(2)}, u32[]{:S(2)}) collective-permute-start(bf16[96,1536]{1,0:T(8,128)(2,1)S(1)} %get-tuple-element.288), channel_id=1, source_target_pairs={{0,24},{4,28},{8,16},{12,20},{16,8},{20,12},{24,0},{28,4},{1,25},{... | collective-permute-start | bytes 884744 | tf_op jit(solution)/shard_map/ppermute | solution.py:662
  342.2 26.4 %collective-permute-start.55 = (bf16[48,3584]{1,0:T(8,128)(2,1)}, bf16[48,3584]{1,0:T(8,128)(2,1)S(1)}, u32[]{:S(2)}, u32[]{:S(2)}) collective-permute-start(bf16[48,3584]{1,0:T(8,128)(2,1)} %get-tuple-element.283), channel_id=1, source_target_pairs={{0,8},{4,12},{8,0},{12,4},{16,24},{20,28},{24,16},{28,20},{1,9},{5... | collective-permute-start | bytes 1032200 | tf_op jit(solution)/shard_map/ppermute | solution.py:662
  344.4 26.8 %collective-permute-start.56 = (bf16[48,3584]{1,0:T(8,128)(2,1)}, bf16[48,3584]{1,0:T(8,128)(2,1)S(1)}, u32[]{:S(2)}, u32[]{:S(2)}) collective-permute-start(bf16[48,3584]{1,0:T(8,128)(2,1)} %get-tuple-element.282), channel_id=1, source_target_pairs={{0,16},{4,20},{8,24},{12,28},{16,0},{20,4},{24,8},{28,12},{1,17},{... | collective-permute-start | bytes 1032200 | tf_op jit(solution)/shard_map/ppermute | solution.py:662
  345.2 26.0 %collective-permute-start.57 = (bf16[48,3584]{1,0:T(8,128)(2,1)}, bf16[48,3584]{1,0:T(8,128)(2,1)S(1)}, u32[]{:S(2)}, u32[]{:S(2)}) collective-permute-start(bf16[48,3584]{1,0:T(8,128)(2,1)} %get-tuple-element.281), channel_id=1, source_target_pairs={{0,24},{4,28},{8,16},{12,20},{16,8},{20,12},{24,0},{28,4},{1,25},{... | collective-permute-start | bytes 1032200 | tf_op jit(solution)/shard_map/ppermute | solution.py:662
  347.9 48.9 %all-to-all-start = ((bf16[8,48,1152]{2,1,0:T(8,128)(2,1)}), bf16[8,48,1152]{2,1,0:T(8,128)(2,1)S(1)}, u32[]{:S(2)}, u32[]{:S(2)}) async-start(bf16[8,48,1152]{2,1,0:T(8,128)(2,1)} %fusion.20), calls=%async_computation.1 | async-start | bytes 1769472 | tf_op jit(solution)/shard_map/all_to_all | solution.py:695
  (109 other events, 1343.1 us)
Sparse Core Ops, SparseCore 0:
  247.7 85.0 reduce-scatter.1

commit v4 on v3

--- a/solution.py
+++ b/solution.py
@@ -245,7 +245,9 @@
         own = jnp.logical_and(block >= first_own, block < end_own)
         key_start = jnp.where(own, start, jnp.maximum(start, first_own))
         key_end = jnp.where(own, start + length, jnp.minimum(start + length, end_own))
-        n_keys = key_end - key_start
+        whole = key_end - key_start == 3
+        key_start = jnp.where(whole, start, key_start)
+        n_keys = jnp.where(whole, length, key_end - key_start)
         rows = pl.ds(pl.multiple_of(block * BLOCK, BLOCK), BLOCK)
         place = pl.ds(pl.multiple_of(block * BLOCK, BLOCK), BLOCK)
         shift = pl.multiple_of((3 - (block - key_start)) * BLOCK, BLOCK)
@@ -276,7 +278,7 @@
                 dk_sum[pair, span, :] += dot_nn(dscores, queries)
                 dq_ref[place, lanes] = (untwine(dot_tn(keys, dscores)) * HEAD_DIM**-0.5).astype(BF16)
 
-        for blocks in (1, 2, 3, 4):
+        for blocks in (1, 2, 4):
             @pl.when(n_keys == blocks)
             def _(blocks=blocks):
                 variant(blocks)
@@ -381,8 +383,6 @@
     low = normed.astype(BF16)
     low_ref[...] = low
     wait_for(1)
-    wait_for(2)
-    ffn = jnp.zeros((low.shape[0], width), F32)
     for tile in range(ff // FF_TILE):
         cols = slice(tile * FF_TILE, (tile + 1) * FF_TILE)
         gate = dot_nn(low, w_gu[:, cols])
@@ -394,7 +394,8 @@
         hidden_ref[:, cols] = hidden
         gate_grad[:, cols] = up * slope
         up_grad[:, cols] = gelu
-        ffn = ffn + dot_nn(hidden, w_down[cols, :])
+    wait_for(2)
+    ffn = dot_nn(hidden_ref[...], w_down[...])
     unit_two, scale_two = norm_parts(normed + ffn + vec_ref[5:6, :])
     result_ref[...] = (unit_two * gain_two + shift_two).astype(BF16)
     grad = cot_ref[...].astype(F32)
@@ -437,7 +438,7 @@
 def middle_call(ctx, tokens, cotangent, vectors, pieces, plans_of, slot_of, counts):
     rows, width = tokens.shape
     ff = 4 * width
-    tile = 256
+    tile = 384
     by_rows = lambda cols: pl.BlockSpec((tile, cols), lambda i: (i, 0))
     paired = lambda cols: pl.BlockSpec((2, tile, cols), lambda i: (0, i, 0))
     shaped = lambda cols, dtype: jax.ShapeDtypeStruct((rows, cols), dtype)
@@ -479,6 +480,33 @@
     )(ctx, tokens, cotangent, vectors, *pieces)
 
 
+def group_grad_kernel(tokens_ref, dq_ref, dk_ref, dv_ref, mine_ref, away_ref):
+    own_rows = tokens_ref.shape[0]
+    lower = lax.axis_index("head") % 2 == 0
+    for third, ref in enumerate((dq_ref, dk_ref, dv_ref)):
+        skip = HALO if third == 0 else 0
+        cols = slice(third * ref.shape[1], (third + 1) * ref.shape[1])
+        values = dot_tn(tokens_ref[...], ref[skip : skip + own_rows, :]).astype(BF16)
+        halves = values.reshape(8, 2, values.shape[0] // 16, values.shape[1])
+        mine_ref[:, :, cols] = jnp.where(lower, halves[:, 0], halves[:, 1])
+        away_ref[:, :, cols] = jnp.where(lower, halves[:, 1], halves[:, 0])
+
+
+def group_grad_call(tokens, back):
+    width = tokens.shape[1]
+    half = jax.ShapeDtypeStruct((8, width // 16, 3 * back[1].shape[1]), BF16)
+    vmem = pl.BlockSpec(memory_space=pltpu.VMEM)
+    return pl.pallas_call(
+        group_grad_kernel,
+        in_specs=[vmem] * 4,
+        out_specs=[vmem] * 2,
+        out_shape=[half] * 2,
+        compiler_params=pltpu.CompilerParams(vmem_limit_bytes=VMEM_GRANT),
+        cost_estimate=SHORT,
+        name="group_grad",
+    )(tokens, *back)
+
+
 def collect_kernel(plan_of, n_parts, *refs):
     parts, wholes = refs[:n_parts], refs[n_parts : n_parts + 5]
     total_ref, sems = refs[n_parts + 5 :]
@@ -855,10 +883,6 @@
             total = total + other.astype(F32)
         return total.astype(BF16)
 
-    def qkv_grad(back):
-        joined = jnp.concatenate((back[0][HALO:-HALO], back[1], back[2]), axis=1)
-        return core_rows(dot_tn(tokens, joined).astype(BF16))
-
     cut = ff // 2
     one, one_away = split(sum_one, x, 1)
     two, two_away = split_y(core_keep(normed_low, dgu[0, 1], two_theirs).reshape(8, shard, cut), y)
@@ -872,21 +896,26 @@
     vec_cols = jnp.pad(sums.astype(BF16).T, ((0, 0), (0, BLOCK - 8)))
     sum_ov = core_rows(jnp.concatenate((dot_tn(ctx, dattn).astype(BF16), vec_cols), axis=1))
     back_a = attend_back_call(ids, slopes, pairs, stats, dctx_window, own_rows, 0, 1)
-    one_their, two_their, dctx_window, sum_ov, *back_a = together(
-        one_their, two_their, dctx_window, sum_ov, *back_a
-    )
+    grad_a, grad_away = group_grad_call(tokens, back_a)
+    one_their, two_their, dctx_window, sum_ov, grad_a, grad_away, *back_a = together(
+        one_their, two_their, dctx_window, sum_ov, grad_a, grad_away, *back_a
+    )
+    grad_a = slab_sum(grad_a, swap(grad_away, SWAP_CORE))
     two = slab_sum(two, two_their)
     two_their = z_send(two)
-    one = jnp.concatenate((slab_sum(one, one_their), qkv_grad(back_a), sum_ov), axis=2)
+    one = jnp.concatenate((slab_sum(one, one_their), grad_a, sum_ov), axis=2)
     one, one_away = split_y(one, y)
     one_their = swap(one_away, SWAP_Y)
     back_b = attend_back_call(ids, slopes, pairs, stats, dctx_window, own_rows, 1, 1)
-    one_their, share_down, *rest = together(one_their, share_down, *two_their, *back_b)
+    grad_b, grad_away = group_grad_call(tokens, back_b)
+    one_their, share_down, grad_b, grad_away, *rest = together(
+        one_their, share_down, grad_b, grad_away, *two_their, *back_b
+    )
     two_their, back_b = rest[:3], rest[3:]
 
     one = slab_sum(one, one_their)
     one_their = z_send(one)
-    grad_b = trade(qkv_grad(back_b), "dp")
+    grad_b = trade(slab_sum(grad_b, swap(grad_away, SWAP_CORE)), "dp")
     two_mine = z_sum(two, two_their)
     two_other = swap(two_mine, SWAP_X)
     down_other = swap(share_down, SWAP_X)

time: 461 us -> 449 us (0.974)
  Pallas kernels: 114 us -> 127 us
  starting transfers between devices: 75 us -> 66.1 us
  waiting for transfers between devices: 147 us -> 139 us
  matrix products: 42.9 us -> 36.3 us
    pallas_call x0 -> x2, Pallas kernels: none -> 10.5 us  [group_grad_call(): pl.pallas_call(group_grad_kernel, in_specs=[vmem] * 4, out_specs=[vmem] *...]
    ppermute x61, starting transfers between devices: 60.6 us -> 52.6 us  [swap(): return lax.ppermute(values, *how)]
    dot_general x9 -> x7, matrix products: 37.8 us -> 31.2 us  [dot_tn(): lax.dot_general(left, right, (((0,), (0,)), ((), ())), preferred_element_...]
    ppermute x61, waiting for transfers between devices: 114 us -> 108 us  [swap(): return lax.ppermute(values, *how)]
    pallas_call x1, Pallas kernels: 16.3 us -> 21.6 us  [attend_call(): pl.pallas_call(functools.partial(attend_kernel, HALO // BLOCK, own_rows /...]
    unnamed x133 -> x139, local copies, waits for them, and re-layouts: 13.6 us -> 13.9 us
  transfers between devices with their start and end apart: 69 -> 69, of which waited for: 28 -> 28; matrix products, arithmetic and copies ran while one was open for 15% -> 15% of each run, Pallas kernels for 12% -> 15%
where the time goes in v4:
time: 449 us; the launch traced here: 441 us
  waiting for transfers between devices  139 us (31%)
  Pallas kernels  127 us (28%)
  starting transfers between devices  66.1 us (15%)
  matrix products  36.3 us (8%)
  local copies, waits for them, and re-layouts  34.3 us (8%)
  other arithmetic  21.3 us (5%)
  between operations  17.5 us (4%)
    ppermute x61, waiting for transfers between devices, swap(): return lax.ppermute(values, *how)  108 us
    ppermute x61, starting transfers between devices, swap(): return lax.ppermute(values, *how)  52.6 us
    pallas_call x1, Pallas kernels, middle_call(): pl.pallas_call(functools.partial(middle_kernel, plans_of, slot_of, counts...  43.3 us
    dot_general x7, matrix products, dot_tn(): lax.dot_general(left, right, (((0,), (0,)), ((), ())), preferred_element_...  31.2 us
    all_to_all x1, waiting for transfers between devices, trade(): return lax.all_to_all(values, axis, split_axis=0, concat_axis=0, tiled=True)  25.4 us
    pallas_call x2, Pallas kernels, attend_back_call(): pl.pallas_call(functools.partial(attend_back_kernel, HALO // BLOCK, own_r...  23.4 us
    pallas_call x1, Pallas kernels, attend_call(): pl.pallas_call(functools.partial(attend_kernel, HALO // BLOCK, own_rows /...  21.6 us
    unnamed x139, local copies, waits for them, and re-layouts  13.9 us
  transfers between devices with their start and end apart: 69, of which 28 were waited for; matrix products, arithmetic and copies ran while one was open for 15% of the time, Pallas kernels for 15%

profile of v4, /device:TPU:0, one launch (start us, length us, event | category | flops | bytes accessed | tf_op | source)
XLA Modules:
  0.0 441.3 jit_solution(15411506138361438718)
XLA Ops:
  21.2 5.7 %collective-permute-done = bf16[96,1152]{1,0:T(8,128)(2,1)} collective-permute-done((bf16[96,1152]{1,0:T(8,128)(2,1)}, bf16[96,1152]{1,0:T(8,128)(2,1)}, u32[]{:S(2)}, u32[]{:S(2)}) %collective-permute-start) | collective-permute-done | bytes 221216 | tf_op jit(solution)/shard_map/ppermute | solution.py:690
  38.2 6.1 %collective-permute-done.4 = bf16[48,3072]{1,0:T(8,128)(2,1)S(1)} collective-permute-done((bf16[48,3072]{1,0:T(8,128)(2,1)S(1)}, bf16[48,3072]{1,0:T(8,128)(2,1)S(1)}, u32[]{:S(2)}, u32[]{:S(2)}) %collective-permute-start.4) | collective-permute-done | bytes 294944 | tf_op jit(solution)/shard_map/ppermute | solution.py:690
  49.1 14.4 %collective-permute-done.7 = bf16[2,96,1152]{2,1,0:T(8,128)(2,1)S(1)} collective-permute-done((bf16[2,96,1152]{2,1,0:T(8,128)(2,1)S(1)}, bf16[2,96,1152]{2,1,0:T(8,128)(2,1)S(1)}, u32[]{:S(2)}, u32[]{:S(2)}) %collective-permute-start.7) | collective-permute-done | bytes 442400 | tf_op jit(solution)/shard_map/ppermute | solution.py:690
  67.2 10.8 %collective-permute-done.13.refs_3_ = bf16[2,96,1152]{2,1,0:T(8,128)(2,1)S(1)} collective-permute-done((bf16[2,96,1152]{2,1,0:T(8,128)(2,1)S(1)}, bf16[2,96,1152]{2,1,0:T(8,128)(2,1)S(1)}, u32[]{:S(2)}, u32[]{:S(2)}) %collective-permute-start.13) | collective-permute-done | bytes 442400 | tf_op jit(solution)/shard_map/ppermute | solution.py:690
  86.4 12.6 %collective-permute-done.19.refs_3_ = bf16[2,48,3072]{2,1,0:T(8,128)(2,1)S(1)} collective-permute-done((bf16[2,48,3072]{2,1,0:T(8,128)(2,1)S(1)}, bf16[2,48,3072]{2,1,0:T(8,128)(2,1)S(1)}, u32[]{:S(2)}, u32[]{:S(2)}) %collective-permute-start.19) | collective-permute-done | bytes 589856 | tf_op jit(solution)/shard_map/ppermute | solution.py:690
  101.6 11.8 %qkv.1 = (bf16[18,1536,128]{2,1,0:T(8,128)(2,1)}, bf16[768,2304]{1,0:T(8,128)(2,1)}) custom-call(bf16[1536,768]{1,0:T(8,128)(2,1)} %pad_maximum_fusion.1.window_ref, bf16[2,96,1152]{2,1,0:T(8,128)(2,1)} %copy-done.16, bf16[2,96,1152]{2,1,0:T(8,128)(2,1)} %copy-done.38, bf16[2,96,1152]{2,1,0:T(8,128)(2,1)} %copy-done.17, bf16[2,96,1152]{2,1,0:T(8,128)(2,1)} %copy-done.41, ...), custom_call_target="tpu_custom_call" | custom-call | flops 1000 | bytes 1000 | tf_op jit(solution)/shard_map/qkv/pallas_call | solution.py:90
  118.0 21.6 %attend.1 = (bf16[768,768]{1,0:T(8,128)(2,1)}, f32[6,2,768]{2,1,0:T(2,128)}) custom-call(s32[12]{0:T(128)} %pad_dynamic-slice_fusion.ids_ref, f32[12]{0:T(128)} %constant.169.clone.slopes_ref, bf16[18,1536,128]{2,1,0:T(8,128)(2,1)} %get-tuple-element.179.q_ref.k_ref.v_ref, bf16[18,1536,128]{2,1,0:T(8,128)(2,1)} %get-tuple-element.179.q_ref.k_ref.v_ref, ...), custom_call_target="tpu_custom_call" | custom-call | flops 1000 | bytes 1000 | tf_op jit(solution)/shard_map/attend/pallas_call | solution.py:207
  146.8 43.3 %middle.1 = (bf16[768,768]{1,0:T(8,128)(2,1)}, bf16[768,3072]{1,0:T(8,128)(2,1)}, bf16[2,2,768,1536]{3,2,1,0:T(8,128)(2,1)}, bf16[2,768,384]{2,1,0:T(8,128)(2,1)...) custom-call(bf16[768,768]{1,0:T(8,128)(2,1)} %get-tuple-element.189., ...), custom_call_target="tpu_custom_call" | custom-call | flops 1000 | bytes 1000 | tf_op jit(solution)/shard_map/middle/pallas_call | solution.py:445
  190.1 5.6 %convolution_convert_fusion.2 = bf16[768,1536]{1,0:T(8,128)(2,1)} fusion(bf16[768,768]{1,0:T(8,128)(2,1)} %get-tuple-element.215, bf16[2,2,768,1536]{3,2,1,0:T(8,128)(2,1)} %get-tuple-element.208), kind=kOutput, calls=%fused_computation.6 | convolution fusion | flops 1813118976 | bytes 5898240 | tf_op jit(solution)/shard_map/dot_general | solution.py:45
  203.8 5.5 %convolution_convert_fusion.1 = bf16[768,1536]{1,0:T(8,128)(2,1)} fusion(bf16[768,768]{1,0:T(8,128)(2,1)} %get-tuple-element.215, bf16[2,2,768,1536]{3,2,1,0:T(8,128)(2,1)} %get-tuple-element.208), kind=kOutput, calls=%fused_computation.5 | convolution fusion | flops 1813118976 | bytes 5898240 | tf_op jit(solution)/shard_map/dot_general | solution.py:45
  223.8 5.4 %add_convert_fusion.2 = bf16[3072,384]{1,0:T(8,128)(2,1)} fusion(bf16[3072,384]{1,0:T(8,128)(2,1)} %collective-permute-done.37, bf16[768,3072]{1,0:T(8,128)(2,1)S(1)} %bitcast.114, bf16[2,768,384]{2,1,0:T(8,128)(2,1)S(1)} %copy-done.63), kind=kOutput, calls=%fused_computation.3 | convolution fusion | flops 1815478272 | bytes 10027008 | tf_op jit(solution)/shard_map/dot_general | solution.py:45
  237.1 6.6 %collective-permute-start.44 = (bf16[8,48,1536]{2,1,0:T(8,128)(2,1)}, bf16[8,48,1536]{2,1,0:T(8,128)(2,1)}, u32[]{:S(2)}, u32[]{:S(2)}) collective-permute-start(bf16[8,48,1536]{2,1,0:T(8,128)(2,1)} %get-tuple-element.221), channel_id=1, source_target_pairs={{0,2},{1,3},{2,0},{3,1},{4,6},{5,7},{6,4},{7,5},{8,10},{9,11},{10,... | collective-permute-start | bytes 3538952 | tf_op jit(solution)/shard_map/ppermute | solution.py:690
  248.4 11.5 %attend_back.2 = (bf16[1536,384]{1,0:T(8,128)(2,1)}, bf16[768,384]{1,0:T(8,128)(2,1)}, bf16[768,384]{1,0:T(8,128)(2,1)}) custom-call(s32[12]{0:T(128)} %pad_dynamic-slice_fusion.ids_ref, f32[12]{0:T(128)} %constant.169.clone.slopes_ref, bf16[18,1536,128]{2,1,0:T(8,128)(2,1)} %get-tuple-element.179.q_ref.k_ref.v_ref, ...), custom_call_target="tpu_custom_call" | custom-call | flops 1000 | bytes 1000 | tf_op jit(solution)/shard_map/attend_back/pallas_call | solution.py:304
  259.9 5.3 %group_grad.2 = (bf16[8,48,1152]{2,1,0:T(8,128)(2,1)}, bf16[8,48,1152]{2,1,0:T(8,128)(2,1)}) custom-call(bf16[768,768]{1,0:T(8,128)(2,1)} %tokens_ref.3, bf16[1536,384]{1,0:T(8,128)(2,1)} %get-tuple-element.252.dq_ref, bf16[768,384]{1,0:T(8,128)(2,1)} %get-tuple-element.254.dk_ref, bf16[768,384]{1,0:T(8,128)(2,1)} %get-tuple-element.256.dv_ref), custom_call_target="tpu_custom_call" | custom-call | flops 1000 | bytes 1000 | tf_op jit(solution)/shard_map/group_grad/pallas_call | solution.py:499
  265.2 4.8 %collective-permute-done.44 = bf16[8,48,1536]{2,1,0:T(8,128)(2,1)} collective-permute-done((bf16[8,48,1536]{2,1,0:T(8,128)(2,1)}, bf16[8,48,1536]{2,1,0:T(8,128)(2,1)}, u32[]{:S(2)}, u32[]{:S(2)}) %collective-permute-start.44) | collective-permute-done | bytes 1179680 | tf_op jit(solution)/shard_map/ppermute | solution.py:690
  270.0 8.5 %collective-permute-done.45 = bf16[4,96,1536]{2,1,0:T(8,128)(2,1)} collective-permute-done((bf16[4,96,1536]{2,1,0:T(8,128)(2,1)}, bf16[4,96,1536]{2,1,0:T(8,128)(2,1)}, u32[]{:S(2)}, u32[]{:S(2)}) %collective-permute-start.45) | collective-permute-done | bytes 1179680 | tf_op jit(solution)/shard_map/ppermute | solution.py:690
  292.7 11.8 %attend_back.3 = (bf16[1536,384]{1,0:T(8,128)(2,1)}, bf16[768,384]{1,0:T(8,128)(2,1)}, bf16[768,384]{1,0:T(8,128)(2,1)}) custom-call(s32[12]{0:T(128)} %pad_dynamic-slice_fusion.ids_ref, f32[12]{0:T(128)} %constant.169.clone.slopes_ref, bf16[18,1536,128]{2,1,0:T(8,128)(2,1)} %get-tuple-element.179.q_ref.k_ref.v_ref, ...), custom_call_target="tpu_custom_call" | custom-call | flops 1000 | bytes 1000 | tf_op jit(solution)/shard_map/attend_back/pallas_call | solution.py:304
  304.6 5.2 %group_grad.3 = (bf16[8,48,1152]{2,1,0:T(8,128)(2,1)}, bf16[8,48,1152]{2,1,0:T(8,128)(2,1)}) custom-call(bf16[768,768]{1,0:T(8,128)(2,1)} %tokens_ref.3, bf16[1536,384]{1,0:T(8,128)(2,1)} %get-tuple-element.253.dq_ref, bf16[768,384]{1,0:T(8,128)(2,1)} %get-tuple-element.255.dk_ref, bf16[768,384]{1,0:T(8,128)(2,1)} %get-tuple-element.257.dv_ref), custom_call_target="tpu_custom_call" | custom-call | flops 1000 | bytes 1000 | tf_op jit(solution)/shard_map/group_grad/pallas_call | solution.py:499
  314.5 9.2 %collective-permute-done.48 = bf16[4,48,3584]{2,1,0:T(8,128)(2,1)} collective-permute-done((bf16[4,48,3584]{2,1,0:T(8,128)(2,1)}, bf16[4,48,3584]{2,1,0:T(8,128)(2,1)}, u32[]{:S(2)}, u32[]{:S(2)}) %collective-permute-start.48) | collective-permute-done | bytes 1376288 | tf_op jit(solution)/shard_map/ppermute | solution.py:690
  323.7 5.1 %reduce-scatter.2.cloned.1.call-done = bf16[384,384]{1,0:T(8,128)(2,1)} async-done(((bf16[3072,384]{1,0:T(8,128)(2,1)}), bf16[384,384]{1,0:T(8,128)(2,1)}) %reduce-scatter.2.cloned.1.call-update) | async-done | bytes 294928 | tf_op jit(solution)/shard_map/reduce_scatter | solution.py:867
  350.1 5.1 %fusion.30 = f32[768,768]{1,0:T(8,128)S(1)} fusion(bf16[768,2304]{1,0:T(8,128)(2,1)} %constant_dynamic-update-slice_fusion, bf16[768,2304]{1,0:T(8,128)(2,1)S(1)} %copy-done.58), kind=kOutput, calls=%fused_computation.93 | convolution fusion | flops 2717908992 | bytes 9437184 | tf_op jit(solution)/shard_map/dot_general | solution.py:41
  359.9 25.4 %all-to-all-done = bf16[8,48,1152]{2,1,0:T(8,128)(2,1)S(1)} async-done(((bf16[8,48,1152]{2,1,0:T(8,128)(2,1)}), bf16[8,48,1152]{2,1,0:T(8,128)(2,1)S(1)}, u32[]{:S(2)}, u32[]{:S(2)}) %all-to-all-start) | async-done | bytes 884768 | tf_op jit(solution)/shard_map/all_to_all | solution.py:723
  389.2 9.5 %collective-permute-done.58.refs_1_ = bf16[48,4736]{1,0:T(8,128)(2,1)S(1)} collective-permute-done((bf16[48,4736]{1,0:T(8,128)(2,1)S(1)}, bf16[48,4736]{1,0:T(8,128)(2,1)S(1)}, u32[]{:S(2)}, u32[]{:S(2)}) %collective-permute-start.58) | collective-permute-done | bytes 454688 | tf_op jit(solution)/shard_map/ppermute | solution.py:690
  419.6 13.3 %adam.1 = (f32[96,2304]{1,0:T(8,128)}, f32[96,2304]{1,0:T(8,128)}, f32[96,2304]{1,0:T(8,128)}, bf16[96,2304]{1,0:T(8,128)(2,1)}, f32[96,768]{1,0:T(8,128)}, /*in...) custom-call(f32[1]{0:T(128)S(6)} %min.3.factor_ref, ...), custom_call_target="tpu_custom_call" | custom-call | flops 1000 | bytes 1000 | tf_op jit(solution)/shard_map/adam/pallas_call | solution.py:579
  (336 shorter events, 159.4 us)
Async XLA Ops:
  7.2 321.6 %reduce-scatter.2.cloned.1.call-start = ((), (), s32[]{:S(2)}) async-start(), calls=%async_computation.2 | async-start | bytes 2654208 | tf_op jit(solution)/shard_map/reduce_scatter | solution.py:867
  10.2 17.8 %collective-permute-start.1 = (bf16[496,384]{1,0:T(8,128)(2,1)S(1)}, bf16[496,384]{1,0:T(8,128)(2,1)S(1)}, u32[]{:S(2)}, u32[]{:S(2)}) collective-permute-start(bf16[496,384]{1,0:T(8,128)(2,1)S(1)} %get-tuple-element.308), channel_id=1, source_target_pairs={{0,8},{4,12},{8,0},{12,4},{16,24},{20,28},{24,16},{28,20},{1,9},{5... | collective-permute-start | bytes 1142792 | tf_op jit(solution)/shard_map/ppermute | solution.py:690
  17.6 19.1 %collective-permute-start.6 = (bf16[384,768]{1,0:T(8,128)(2,1)}, bf16[384,768]{1,0:T(8,128)(2,1)S(1)}, u32[]{:S(2)}, u32[]{:S(2)}) collective-permute-start(bf16[384,768]{1,0:T(8,128)(2,1)} %get-tuple-element.306), channel_id=1, source_target_pairs={{1,0},{2,1},{3,2},{5,4},{6,5},{7,6},{9,8},{10,9},{11,10},{13,12},{... | collective-permute-start | bytes 1769480 | tf_op jit(solution)/shard_map/ppermute | solution.py:599
  44.5 19.0 %collective-permute-start.10 = (bf16[2,48,3072]{2,1,0:T(8,128)(2,1)S(1)}, bf16[2,48,3072]{2,1,0:T(8,128)(2,1)S(1)}, u32[]{:S(2)}, u32[]{:S(2)}) collective-permute-start(bf16[2,48,3072]{2,1,0:T(8,128)(2,1)S(1)} %pad_maximum_fusion.4.refs_0_), channel_id=1, source_target_pairs={{0,2},{1,3},{2,0},{3,1},{4,6},{5,7},{6,4},{7,5},{8,10},{9,11},{10,... | collective-permute-start | bytes 1769480 | tf_op jit(solution)/shard_map/ppermute | solution.py:690
  81.3 19.4 %collective-permute-start.20 = (bf16[2,496,384]{2,1,0:T(8,128)(2,1)S(1)}, bf16[2,496,384]{2,1,0:T(8,128)(2,1)S(1)}, u32[]{:S(2)}, u32[]{:S(2)}) collective-permute-start(bf16[2,496,384]{2,1,0:T(8,128)(2,1)S(1)} %collective-permute-done.16), channel_id=1, source_target_pairs={{8,0},{12,4},{16,24},{20,28},{9,1},{13,5},{17,25},{21,29},{10,2},{... | collective-permute-start | bytes 2285576 | tf_op jit(solution)/shard_map/ppermute | solution.py:690
  84.6 32.1 %collective-permute-start.23 = (bf16[2,496,384]{2,1,0:T(8,128)(2,1)S(1)}, bf16[2,496,384]{2,1,0:T(8,128)(2,1)S(1)}, u32[]{:S(2)}, u32[]{:S(2)}) collective-permute-start(bf16[2,496,384]{2,1,0:T(8,128)(2,1)S(1)} %pad_maximum_fusion.3.refs_16_), channel_id=1, source_target_pairs={{0,4},{4,0},{8,12},{12,8},{16,20},{20,16},{24,28},{28,24},{1,5},{5... | collective-permute-start | bytes 2285576 | tf_op jit(solution)/shard_map/ppermute | solution.py:690
  85.5 29.5 %collective-permute-start.31 = (bf16[2,48,3072]{2,1,0:T(8,128)(2,1)S(1)}, bf16[2,48,3072]{2,1,0:T(8,128)(2,1)}, u32[]{:S(2)}, u32[]{:S(2)}) collective-permute-start(bf16[2,48,3072]{2,1,0:T(8,128)(2,1)S(1)} %collective-permute-done.10.refs_4_), channel_id=1, source_target_pairs={{0,1},{1,0},{2,3},{3,2},{4,5},{5,4},{6,7},{7,6},{8,9},{9,8},{10,11... | collective-permute-start | bytes 1769480 | tf_op jit(solution)/shard_map/ppermute | solution.py:690
  86.2 30.7 %collective-permute-start.25 = (bf16[2,496,384]{2,1,0:T(8,128)(2,1)S(1)}, bf16[2,496,384]{2,1,0:T(8,128)(2,1)}, u32[]{:S(2)}, u32[]{:S(2)}) collective-permute-start(bf16[2,496,384]{2,1,0:T(8,128)(2,1)S(1)} %pad_maximum_fusion.3.refs_16_), channel_id=1, source_target_pairs={{0,1},{1,0},{2,3},{3,2},{4,5},{5,4},{6,7},{7,6},{8,9},{9,8},{10,11... | collective-permute-start | bytes 2285576 | tf_op jit(solution)/shard_map/ppermute | solution.py:690
  115.1 24.7 %collective-permute-start.24 = (bf16[2,496,384]{2,1,0:T(8,128)(2,1)S(1)}, bf16[2,496,384]{2,1,0:T(8,128)(2,1)}, u32[]{:S(2)}, u32[]{:S(2)}) collective-permute-start(bf16[2,496,384]{2,1,0:T(8,128)(2,1)S(1)} %add.217.refs_18_), channel_id=1, source_target_pairs={{0,4},{4,0},{8,12},{12,8},{16,20},{20,16},{24,28},{28,24},{1,5},{5... | collective-permute-start | bytes 2285576 | tf_op jit(solution)/shard_map/ppermute | solution.py:690
  116.0 23.7 %collective-permute-start.26 = (bf16[2,496,384]{2,1,0:T(8,128)(2,1)S(1)}, bf16[2,496,384]{2,1,0:T(8,128)(2,1)}, u32[]{:S(2)}, u32[]{:S(2)}) collective-permute-start(bf16[2,496,384]{2,1,0:T(8,128)(2,1)S(1)} %add.217.refs_18_), channel_id=1, source_target_pairs={{0,1},{1,0},{2,3},{3,2},{4,5},{5,4},{6,7},{7,6},{8,9},{9,8},{10,11... | collective-permute-start | bytes 2285576 | tf_op jit(solution)/shard_map/ppermute | solution.py:690
  116.2 23.5 %collective-permute-start.22 = (bf16[2,48,3072]{2,1,0:T(8,128)(2,1)}, bf16[2,48,3072]{2,1,0:T(8,128)(2,1)S(1)}, u32[]{:S(2)}, u32[]{:S(2)}) collective-permute-start(bf16[2,48,3072]{2,1,0:T(8,128)(2,1)} %copy-done.34), channel_id=1, source_target_pairs={{0,2},{1,3},{2,0},{3,1},{4,6},{5,7},{6,4},{7,5},{8,10},{9,11},{10,... | collective-permute-start | bytes 1769480 | tf_op jit(solution)/shard_map/ppermute | solution.py:690
  116.8 22.9 %collective-permute-start.29 = (bf16[2,48,3072]{2,1,0:T(8,128)(2,1)S(1)}, bf16[2,48,3072]{2,1,0:T(8,128)(2,1)}, u32[]{:S(2)}, u32[]{:S(2)}) collective-permute-start(bf16[2,48,3072]{2,1,0:T(8,128)(2,1)S(1)} %add.216.refs_2_), channel_id=1, source_target_pairs={{0,1},{1,0},{2,3},{3,2},{4,5},{5,4},{6,7},{7,6},{8,9},{9,8},{10,11... | collective-permute-start | bytes 1769480 | tf_op jit(solution)/shard_map/ppermute | solution.py:690
  116.9 22.9 %collective-permute-start.30 = (bf16[2,48,3072]{2,1,0:T(8,128)(2,1)}, bf16[2,48,3072]{2,1,0:T(8,128)(2,1)}, u32[]{:S(2)}, u32[]{:S(2)}) collective-permute-start(bf16[2,48,3072]{2,1,0:T(8,128)(2,1)} %copy-done.34), channel_id=1, source_target_pairs={{0,1},{1,0},{2,3},{3,2},{4,5},{5,4},{6,7},{7,6},{8,9},{9,8},{10,11... | collective-permute-start | bytes 1769480 | tf_op jit(solution)/shard_map/ppermute | solution.py:690
  209.3 19.9 %collective-permute-start.39 = (bf16[768,1536]{1,0:T(8,128)(2,1)}, bf16[768,1536]{1,0:T(8,128)(2,1)}, u32[]{:S(2)}, u32[]{:S(2)}) collective-permute-start(bf16[768,1536]{1,0:T(8,128)(2,1)} %convolution_convert_fusion.1), channel_id=1, source_target_pairs={{0,1},{1,0},{2,3},{3,2},{4,5},{5,4},{6,7},{7,6},{8,9},{9,8},{10,11... | collective-permute-start | bytes 7077896 | tf_op jit(solution)/shard_map/ppermute | solution.py:690
  237.1 32.9 %collective-permute-start.44 = (bf16[8,48,1536]{2,1,0:T(8,128)(2,1)}, bf16[8,48,1536]{2,1,0:T(8,128)(2,1)}, u32[]{:S(2)}, u32[]{:S(2)}) collective-permute-start(bf16[8,48,1536]{2,1,0:T(8,128)(2,1)} %get-tuple-element.221), channel_id=1, source_target_pairs={{0,2},{1,3},{2,0},{3,1},{4,6},{5,7},{6,4},{7,5},{8,10},{9,11},{10,... | collective-permute-start | bytes 3538952 | tf_op jit(solution)/shard_map/ppermute | solution.py:690
  243.8 34.8 %collective-permute-start.45 = (bf16[4,96,1536]{2,1,0:T(8,128)(2,1)}, bf16[4,96,1536]{2,1,0:T(8,128)(2,1)}, u32[]{:S(2)}, u32[]{:S(2)}) collective-permute-start(bf16[4,96,1536]{2,1,0:T(8,128)(2,1)} %get-tuple-element.222), channel_id=1, source_target_pairs={{0,4},{4,0},{8,12},{12,8},{16,20},{20,16},{24,28},{28,24},{1,5},{5... | collective-permute-start | bytes 3538952 | tf_op jit(solution)/shard_map/ppermute | solution.py:690
  282.8 40.8 %collective-permute-start.48 = (bf16[4,48,3584]{2,1,0:T(8,128)(2,1)}, bf16[4,48,3584]{2,1,0:T(8,128)(2,1)}, u32[]{:S(2)}, u32[]{:S(2)}) collective-permute-start(bf16[4,48,3584]{2,1,0:T(8,128)(2,1)} %dynamic-slice_bitcast_fusion), channel_id=1, source_target_pairs={{0,4},{4,0},{8,12},{12,8},{16,20},{20,16},{24,28},{28,24},{1,5},{5... | collective-permute-start | bytes 4128776 | tf_op jit(solution)/shard_map/ppermute | solution.py:690
  287.8 24.0 %collective-permute-start.49 = (bf16[96,1536]{1,0:T(8,128)(2,1)}, bf16[96,1536]{1,0:T(8,128)(2,1)}, u32[]{:S(2)}, u32[]{:S(2)}) collective-permute-start(bf16[96,1536]{1,0:T(8,128)(2,1)} %get-tuple-element.302), channel_id=1, source_target_pairs={{0,8},{4,12},{8,0},{12,4},{16,24},{20,28},{24,16},{28,20},{1,9},{5... | collective-permute-start | bytes 884744 | tf_op jit(solution)/shard_map/ppermute | solution.py:690
  290.2 24.2 %collective-permute-start.50 = (bf16[96,1536]{1,0:T(8,128)(2,1)S(1)}, bf16[96,1536]{1,0:T(8,128)(2,1)}, u32[]{:S(2)}, u32[]{:S(2)}) collective-permute-start(bf16[96,1536]{1,0:T(8,128)(2,1)S(1)} %get-tuple-element.301), channel_id=1, source_target_pairs={{0,16},{4,20},{8,24},{12,28},{16,0},{20,4},{24,8},{28,12},{1,17},{... | collective-permute-start | bytes 884744 | tf_op jit(solution)/shard_map/ppermute | solution.py:690
  291.9 22.6 %collective-permute-start.51 = (bf16[96,1536]{1,0:T(8,128)(2,1)S(1)}, bf16[96,1536]{1,0:T(8,128)(2,1)}, u32[]{:S(2)}, u32[]{:S(2)}) collective-permute-start(bf16[96,1536]{1,0:T(8,128)(2,1)S(1)} %get-tuple-element.300), channel_id=1, source_target_pairs={{0,24},{4,28},{8,16},{12,20},{16,8},{20,12},{24,0},{28,4},{1,25},{... | collective-permute-start | bytes 884744 | tf_op jit(solution)/shard_map/ppermute | solution.py:690
  332.6 25.6 %collective-permute-start.55 = (bf16[48,3584]{1,0:T(8,128)(2,1)}, bf16[48,3584]{1,0:T(8,128)(2,1)S(1)}, u32[]{:S(2)}, u32[]{:S(2)}) collective-permute-start(bf16[48,3584]{1,0:T(8,128)(2,1)} %get-tuple-element.299), channel_id=1, source_target_pairs={{0,8},{4,12},{8,0},{12,4},{16,24},{20,28},{24,16},{28,20},{1,9},{5... | collective-permute-start | bytes 1032200 | tf_op jit(solution)/shard_map/ppermute | solution.py:690
  332.9 27.0 %collective-permute-start.56 = (bf16[48,3584]{1,0:T(8,128)(2,1)}, bf16[48,3584]{1,0:T(8,128)(2,1)}, u32[]{:S(2)}, u32[]{:S(2)}) collective-permute-start(bf16[48,3584]{1,0:T(8,128)(2,1)} %get-tuple-element.298), channel_id=1, source_target_pairs={{0,16},{4,20},{8,24},{12,28},{16,0},{20,4},{24,8},{28,12},{1,17},{... | collective-permute-start | bytes 1032200 | tf_op jit(solution)/shard_map/ppermute | solution.py:690
  335.0 24.9 %collective-permute-start.57 = (bf16[48,3584]{1,0:T(8,128)(2,1)}, bf16[48,3584]{1,0:T(8,128)(2,1)}, u32[]{:S(2)}, u32[]{:S(2)}) collective-permute-start(bf16[48,3584]{1,0:T(8,128)(2,1)} %get-tuple-element.297), channel_id=1, source_target_pairs={{0,24},{4,28},{8,16},{12,20},{16,8},{20,12},{24,0},{28,4},{1,25},{... | collective-permute-start | bytes 1032200 | tf_op jit(solution)/shard_map/ppermute | solution.py:690
  338.1 47.2 %all-to-all-start = ((bf16[8,48,1152]{2,1,0:T(8,128)(2,1)}), bf16[8,48,1152]{2,1,0:T(8,128)(2,1)S(1)}, u32[]{:S(2)}, u32[]{:S(2)}) async-start(bf16[8,48,1152]{2,1,0:T(8,128)(2,1)} %add_convert_fusion.5), calls=%async_computation.1 | async-start | bytes 1769472 | tf_op jit(solution)/shard_map/all_to_all | solution.py:723
  (112 other events, 1409.0 us)
Sparse Core Ops, SparseCore 0:
  246.2 82.5 reduce-scatter.1

commit v5 on v4

--- a/solution.py
+++ b/solution.py
@@ -679,6 +679,7 @@
 SWAP_CORE = ("head", [(i, i ^ 1) for i in range(4)])
 SWAP_X = ("head", [(i, i ^ 2) for i in range(4)])
 SWAP_Y = ("dp", [(i, i ^ 1) for i in range(8)])
+LINES_Z = [[0, 2, 4, 6], [1, 3, 5, 7]]
 SWAP_Z = [None] + [("dp", [(i, i ^ (2 * step)) for i in range(8)]) for step in (1, 2, 3)]
 
 
@@ -719,8 +720,10 @@
     return split(values.reshape(4, 2, *values.shape[1:]), y, 1)
 
 
-def trade(values, axis):
-    return lax.all_to_all(values, axis, split_axis=0, concat_axis=0, tiled=True)
+def trade_z(values):
+    return lax.all_to_all(
+        values, "dp", split_axis=0, concat_axis=0, tiled=True, axis_index_groups=LINES_Z
+    )
 
 
 def cube_body(tokens, segment_ids, cotangent, clip_norm, *state):
@@ -915,7 +918,8 @@
 
     one = slab_sum(one, one_their)
     one_their = z_send(one)
-    grad_b = trade(slab_sum(grad_b, swap(grad_away, SWAP_CORE)), "dp")
+    b_y, b_away = split_y(slab_sum(grad_b, swap(grad_away, SWAP_CORE)), y)
+    grad_b = trade_z(slab_sum(b_y, swap(b_away, SWAP_Y)))
     two_mine = z_sum(two, two_their)
     two_other = swap(two_mine, SWAP_X)
     down_other = swap(share_down, SWAP_X)

time: 449 us -> 438 us (0.976)
  local copies, waits for them, and re-layouts: 34.3 us -> 27.1 us
  Pallas kernels: 127 us -> 120 us
    all_to_all x1, waiting for transfers between devices: 25.4 us -> 11.5 us  [trade_z(): lax.all_to_all(values, 'dp', split_axis=0, concat_axis=0, tiled=True, axi...]
    ppermute x61 -> x62, waiting for transfers between devices: 108 us -> 119 us  [swap(): return lax.ppermute(values, *how)]
    unnamed x139 -> x135, local copies, waits for them, and re-layouts: 13.9 us -> 8.45 us
    pallas_call x1, Pallas kernels: 21.6 us -> 16.2 us  [attend_call(): pl.pallas_call(functools.partial(attend_kernel, HALO // BLOCK, own_rows /...]
    ppermute x61 -> x62, starting transfers between devices: 52.6 us -> 56.5 us  [swap(): return lax.ppermute(values, *how)]
  transfers between devices with their start and end apart: 69 -> 70, of which waited for: 28 -> 28; matrix products, arithmetic and copies ran while one was open for 15% -> 14% of each run, Pallas kernels for 15% -> 14%
where the time goes in v5:
time: 438 us; the launch traced here: 430 us
  waiting for transfers between devices  137 us (31%)
  Pallas kernels  120 us (27%)
  starting transfers between devices  70 us (16%)
  matrix products  37.4 us (9%)
  local copies, waits for them, and re-layouts  27.1 us (6%)
  other arithmetic  21.9 us (5%)
  between operations  17.6 us (4%)
    ppermute x62, waiting for transfers between devices, swap(): return lax.ppermute(values, *how)  119 us
    ppermute x62, starting transfers between devices, swap(): return lax.ppermute(values, *how)  56.5 us
    pallas_call x1, Pallas kernels, middle_call(): pl.pallas_call(functools.partial(middle_kernel, plans_of, slot_of, counts...  43.3 us
    dot_general x7, matrix products, dot_tn(): lax.dot_general(left, right, (((0,), (0,)), ((), ())), preferred_element_...  31.2 us
    pallas_call x2, Pallas kernels, attend_back_call(): pl.pallas_call(functools.partial(attend_back_kernel, HALO // BLOCK, own_r...  21.1 us
    pallas_call x1, Pallas kernels, attend_call(): pl.pallas_call(functools.partial(attend_kernel, HALO // BLOCK, own_rows /...  16.2 us
    pallas_call x1, Pallas kernels, adam_call(): pl.pallas_call(adam_kernel, grid=(steps,), in_specs=[pl.BlockSpec(memory_...  13.3 us
    pallas_call x1, Pallas kernels, qkv_call(): pl.pallas_call(functools.partial(qkv_kernel, plan_of, len(pieces)), grid=...  11.9 us
  transfers between devices with their start and end apart: 70, of which 28 were waited for; matrix products, arithmetic and copies ran while one was open for 14% of the time, Pallas kernels for 14%

profile of v5, /device:TPU:0, one launch (start us, length us, event | category | flops | bytes accessed | tf_op | source)
XLA Modules:
  0.0 430.3 jit_solution(2122713196249402915)
XLA Ops:
  21.2 5.7 %collective-permute-done = bf16[96,1152]{1,0:T(8,128)(2,1)} collective-permute-done((bf16[96,1152]{1,0:T(8,128)(2,1)}, bf16[96,1152]{1,0:T(8,128)(2,1)}, u32[]{:S(2)}, u32[]{:S(2)}) %collective-permute-start) | collective-permute-done | bytes 221216 | tf_op jit(solution)/shard_map/ppermute | solution.py:691
  38.2 6.1 %collective-permute-done.4 = bf16[48,3072]{1,0:T(8,128)(2,1)S(1)} collective-permute-done((bf16[48,3072]{1,0:T(8,128)(2,1)S(1)}, bf16[48,3072]{1,0:T(8,128)(2,1)S(1)}, u32[]{:S(2)}, u32[]{:S(2)}) %collective-permute-start.4) | collective-permute-done | bytes 294944 | tf_op jit(solution)/shard_map/ppermute | solution.py:691
  49.1 14.4 %collective-permute-done.7 = bf16[2,96,1152]{2,1,0:T(8,128)(2,1)S(1)} collective-permute-done((bf16[2,96,1152]{2,1,0:T(8,128)(2,1)S(1)}, bf16[2,96,1152]{2,1,0:T(8,128)(2,1)S(1)}, u32[]{:S(2)}, u32[]{:S(2)}) %collective-permute-start.7) | collective-permute-done | bytes 442400 | tf_op jit(solution)/shard_map/ppermute | solution.py:691
  67.2 10.8 %collective-permute-done.13.refs_3_ = bf16[2,96,1152]{2,1,0:T(8,128)(2,1)S(1)} collective-permute-done((bf16[2,96,1152]{2,1,0:T(8,128)(2,1)S(1)}, bf16[2,96,1152]{2,1,0:T(8,128)(2,1)S(1)}, u32[]{:S(2)}, u32[]{:S(2)}) %collective-permute-start.13) | collective-permute-done | bytes 442400 | tf_op jit(solution)/shard_map/ppermute | solution.py:691
  86.4 12.6 %collective-permute-done.19.refs_3_ = bf16[2,48,3072]{2,1,0:T(8,128)(2,1)S(1)} collective-permute-done((bf16[2,48,3072]{2,1,0:T(8,128)(2,1)S(1)}, bf16[2,48,3072]{2,1,0:T(8,128)(2,1)S(1)}, u32[]{:S(2)}, u32[]{:S(2)}) %collective-permute-start.19) | collective-permute-done | bytes 589856 | tf_op jit(solution)/shard_map/ppermute | solution.py:691
  101.6 11.9 %qkv.1 = (bf16[18,1536,128]{2,1,0:T(8,128)(2,1)}, bf16[768,2304]{1,0:T(8,128)(2,1)}) custom-call(bf16[1536,768]{1,0:T(8,128)(2,1)} %pad_maximum_fusion.1.window_ref, bf16[2,96,1152]{2,1,0:T(8,128)(2,1)} %copy-done.16, bf16[2,96,1152]{2,1,0:T(8,128)(2,1)} %copy-done.38, bf16[2,96,1152]{2,1,0:T(8,128)(2,1)} %copy-done.17, bf16[2,96,1152]{2,1,0:T(8,128)(2,1)} %copy-done.41, ...), custom_call_target="tpu_custom_call" | custom-call | flops 1000 | bytes 1000 | tf_op jit(solution)/shard_map/qkv/pallas_call | solution.py:90
  118.1 16.2 %attend.1 = (bf16[768,768]{1,0:T(8,128)(2,1)}, f32[6,2,768]{2,1,0:T(2,128)}) custom-call(s32[12]{0:T(128)} %pad_dynamic-slice_fusion.ids_ref, f32[12]{0:T(128)} %constant.175.clone.slopes_ref, bf16[18,1536,128]{2,1,0:T(8,128)(2,1)} %get-tuple-element.179.q_ref.k_ref.v_ref, bf16[18,1536,128]{2,1,0:T(8,128)(2,1)} %get-tuple-element.179.q_ref.k_ref.v_ref, ...), custom_call_target="tpu_custom_call" | custom-call | flops 1000 | bytes 1000 | tf_op jit(solution)/shard_map/attend/pallas_call | solution.py:207
  144.7 43.3 %middle.1 = (bf16[768,768]{1,0:T(8,128)(2,1)}, bf16[768,3072]{1,0:T(8,128)(2,1)}, bf16[2,2,768,1536]{3,2,1,0:T(8,128)(2,1)}, bf16[2,768,384]{2,1,0:T(8,128)(2,1)...) custom-call(bf16[768,768]{1,0:T(8,128)(2,1)} %get-tuple-element.189., ...), custom_call_target="tpu_custom_call" | custom-call | flops 1000 | bytes 1000 | tf_op jit(solution)/shard_map/middle/pallas_call | solution.py:445
  188.1 5.6 %convolution_convert_fusion.2 = bf16[768,1536]{1,0:T(8,128)(2,1)} fusion(bf16[768,768]{1,0:T(8,128)(2,1)} %get-tuple-element.215, bf16[2,2,768,1536]{3,2,1,0:T(8,128)(2,1)} %get-tuple-element.208), kind=kOutput, calls=%fused_computation.6 | convolution fusion | flops 1813118976 | bytes 5898240 | tf_op jit(solution)/shard_map/dot_general | solution.py:45
  202.0 5.5 %convolution_convert_fusion.1 = bf16[768,1536]{1,0:T(8,128)(2,1)} fusion(bf16[768,768]{1,0:T(8,128)(2,1)} %get-tuple-element.215, bf16[2,2,768,1536]{3,2,1,0:T(8,128)(2,1)} %get-tuple-element.208), kind=kOutput, calls=%fused_computation.5 | convolution fusion | flops 1813118976 | bytes 5898240 | tf_op jit(solution)/shard_map/dot_general | solution.py:45
  224.1 5.4 %add_convert_fusion.2 = bf16[3072,384]{1,0:T(8,128)(2,1)} fusion(bf16[3072,384]{1,0:T(8,128)(2,1)} %collective-permute-done.37, bf16[768,3072]{1,0:T(8,128)(2,1)S(1)} %bitcast.122, bf16[2,768,384]{2,1,0:T(8,128)(2,1)S(1)} %copy-done.60), kind=kOutput, calls=%fused_computation.3 | convolution fusion | flops 1815478272 | bytes 10027008 | tf_op jit(solution)/shard_map/dot_general | solution.py:45
  237.4 7.5 %collective-permute-start.44 = (bf16[8,48,1536]{2,1,0:T(8,128)(2,1)}, bf16[8,48,1536]{2,1,0:T(8,128)(2,1)}, u32[]{:S(2)}, u32[]{:S(2)}) collective-permute-start(bf16[8,48,1536]{2,1,0:T(8,128)(2,1)} %get-tuple-element.221), channel_id=1, source_target_pairs={{0,2},{1,3},{2,0},{3,1},{4,6},{5,7},{6,4},{7,5},{8,10},{9,11},{10,... | collective-permute-start | bytes 3538952 | tf_op jit(solution)/shard_map/ppermute | solution.py:691
  248.4 10.4 %attend_back.2 = (bf16[1536,384]{1,0:T(8,128)(2,1)}, bf16[768,384]{1,0:T(8,128)(2,1)}, bf16[768,384]{1,0:T(8,128)(2,1)}) custom-call(s32[12]{0:T(128)} %pad_dynamic-slice_fusion.ids_ref, f32[12]{0:T(128)} %constant.175.clone.slopes_ref, bf16[18,1536,128]{2,1,0:T(8,128)(2,1)} %get-tuple-element.179.q_ref.k_ref.v_ref, ...), custom_call_target="tpu_custom_call" | custom-call | flops 1000 | bytes 1000 | tf_op jit(solution)/shard_map/attend_back/pallas_call | solution.py:304
  258.8 5.3 %group_grad.2 = (bf16[8,48,1152]{2,1,0:T(8,128)(2,1)}, bf16[8,48,1152]{2,1,0:T(8,128)(2,1)}) custom-call(bf16[768,768]{1,0:T(8,128)(2,1)} %tokens_ref.3, bf16[1536,384]{1,0:T(8,128)(2,1)} %get-tuple-element.252.dq_ref, bf16[768,384]{1,0:T(8,128)(2,1)} %get-tuple-element.254.dk_ref, bf16[768,384]{1,0:T(8,128)(2,1)} %get-tuple-element.256.dv_ref), custom_call_target="tpu_custom_call" | custom-call | flops 1000 | bytes 1000 | tf_op jit(solution)/shard_map/group_grad/pallas_call | solution.py:499
  264.1 7.2 %collective-permute-done.44 = bf16[8,48,1536]{2,1,0:T(8,128)(2,1)} collective-permute-done((bf16[8,48,1536]{2,1,0:T(8,128)(2,1)}, bf16[8,48,1536]{2,1,0:T(8,128)(2,1)}, u32[]{:S(2)}, u32[]{:S(2)}) %collective-permute-start.44) | collective-permute-done | bytes 1179680 | tf_op jit(solution)/shard_map/ppermute | solution.py:691
  271.2 8.5 %collective-permute-done.45 = bf16[4,96,1536]{2,1,0:T(8,128)(2,1)} collective-permute-done((bf16[4,96,1536]{2,1,0:T(8,128)(2,1)}, bf16[4,96,1536]{2,1,0:T(8,128)(2,1)}, u32[]{:S(2)}, u32[]{:S(2)}) %collective-permute-start.45) | collective-permute-done | bytes 1179680 | tf_op jit(solution)/shard_map/ppermute | solution.py:691
  292.6 10.7 %attend_back.3 = (bf16[1536,384]{1,0:T(8,128)(2,1)}, bf16[768,384]{1,0:T(8,128)(2,1)}, bf16[768,384]{1,0:T(8,128)(2,1)}) custom-call(s32[12]{0:T(128)} %pad_dynamic-slice_fusion.ids_ref, f32[12]{0:T(128)} %constant.175.clone.slopes_ref, bf16[18,1536,128]{2,1,0:T(8,128)(2,1)} %get-tuple-element.179.q_ref.k_ref.v_ref, ...), custom_call_target="tpu_custom_call" | custom-call | flops 1000 | bytes 1000 | tf_op jit(solution)/shard_map/attend_back/pallas_call | solution.py:304
  303.3 5.2 %group_grad.3 = (bf16[8,48,1152]{2,1,0:T(8,128)(2,1)}, bf16[8,48,1152]{2,1,0:T(8,128)(2,1)}) custom-call(bf16[768,768]{1,0:T(8,128)(2,1)} %tokens_ref.3, bf16[1536,384]{1,0:T(8,128)(2,1)} %get-tuple-element.253.dq_ref, bf16[768,384]{1,0:T(8,128)(2,1)} %get-tuple-element.255.dk_ref, bf16[768,384]{1,0:T(8,128)(2,1)} %get-tuple-element.257.dv_ref), custom_call_target="tpu_custom_call" | custom-call | flops 1000 | bytes 1000 | tf_op jit(solution)/shard_map/group_grad/pallas_call | solution.py:499
  313.8 10.2 %collective-permute-done.48 = bf16[4,48,3584]{2,1,0:T(8,128)(2,1)} collective-permute-done((bf16[4,48,3584]{2,1,0:T(8,128)(2,1)}, bf16[4,48,3584]{2,1,0:T(8,128)(2,1)}, u32[]{:S(2)}, u32[]{:S(2)}) %collective-permute-start.48) | collective-permute-done | bytes 1376288 | tf_op jit(solution)/shard_map/ppermute | solution.py:691
  339.8 10.2 %collective-permute-done.53 = bf16[4,48,1152]{2,1,0:T(8,128)(2,1)S(1)} collective-permute-done((bf16[4,48,1152]{2,1,0:T(8,128)(2,1)S(1)}, bf16[4,48,1152]{2,1,0:T(8,128)(2,1)S(1)}, u32[]{:S(2)}, u32[]{:S(2)}) %collective-permute-start.53) | collective-permute-done | bytes 442400 | tf_op jit(solution)/shard_map/ppermute | solution.py:691
  355.2 6.1 %fusion.31 = f32[768,768]{1,0:T(8,128)S(1)} fusion(bf16[768,2304]{1,0:T(8,128)(2,1)} %copy-done.51, bf16[768,2304]{1,0:T(8,128)(2,1)} %get-tuple-element.258), kind=kOutput, calls=%fused_computation.96 | convolution fusion | flops 2717908992 | bytes 9437184 | tf_op jit(solution)/shard_map/dot_general | solution.py:41
  363.1 11.5 %all-to-all-done = bf16[4,48,1152]{2,1,0:T(8,128)(2,1)S(1)} async-done(((bf16[4,48,1152]{2,1,0:T(8,128)(2,1)}), bf16[4,48,1152]{2,1,0:T(8,128)(2,1)S(1)}, u32[]{:S(2)}, u32[]{:S(2)}) %all-to-all-start) | async-done | bytes 442400 | tf_op jit(solution)/shard_map/all_to_all | solution.py:724
  378.8 8.8 %collective-permute-done.59.refs_1_ = bf16[48,4736]{1,0:T(8,128)(2,1)S(1)} collective-permute-done((bf16[48,4736]{1,0:T(8,128)(2,1)S(1)}, bf16[48,4736]{1,0:T(8,128)(2,1)S(1)}, u32[]{:S(2)}, u32[]{:S(2)}) %collective-permute-start.59) | collective-permute-done | bytes 454688 | tf_op jit(solution)/shard_map/ppermute | solution.py:691
  408.5 13.3 %adam.1 = (f32[96,2304]{1,0:T(8,128)}, f32[96,2304]{1,0:T(8,128)}, f32[96,2304]{1,0:T(8,128)}, bf16[96,2304]{1,0:T(8,128)(2,1)}, f32[96,768]{1,0:T(8,128)}, /*in...) custom-call(f32[1]{0:T(128)S(6)} %min.3.factor_ref, ...), custom_call_target="tpu_custom_call" | custom-call | flops 1000 | bytes 1000 | tf_op jit(solution)/shard_map/adam/pallas_call | solution.py:579
  (336 shorter events, 160.2 us)
Async XLA Ops:
  7.2 321.7 %reduce-scatter.2.cloned.1.call-start = ((), (), s32[]{:S(2)}) async-start(), calls=%async_computation.2 | async-start | bytes 2654208 | tf_op jit(solution)/shard_map/reduce_scatter | solution.py:870
  10.2 17.8 %collective-permute-start.1 = (bf16[496,384]{1,0:T(8,128)(2,1)S(1)}, bf16[496,384]{1,0:T(8,128)(2,1)S(1)}, u32[]{:S(2)}, u32[]{:S(2)}) collective-permute-start(bf16[496,384]{1,0:T(8,128)(2,1)S(1)} %get-tuple-element.308), channel_id=1, source_target_pairs={{0,8},{4,12},{8,0},{12,4},{16,24},{20,28},{24,16},{28,20},{1,9},{5... | collective-permute-start | bytes 1142792 | tf_op jit(solution)/shard_map/ppermute | solution.py:691
  17.6 19.1 %collective-permute-start.6 = (bf16[384,768]{1,0:T(8,128)(2,1)}, bf16[384,768]{1,0:T(8,128)(2,1)S(1)}, u32[]{:S(2)}, u32[]{:S(2)}) collective-permute-start(bf16[384,768]{1,0:T(8,128)(2,1)} %get-tuple-element.306), channel_id=1, source_target_pairs={{1,0},{2,1},{3,2},{5,4},{6,5},{7,6},{9,8},{10,9},{11,10},{13,12},{... | collective-permute-start | bytes 1769480 | tf_op jit(solution)/shard_map/ppermute | solution.py:599
  44.5 19.0 %collective-permute-start.10 = (bf16[2,48,3072]{2,1,0:T(8,128)(2,1)S(1)}, bf16[2,48,3072]{2,1,0:T(8,128)(2,1)S(1)}, u32[]{:S(2)}, u32[]{:S(2)}) collective-permute-start(bf16[2,48,3072]{2,1,0:T(8,128)(2,1)S(1)} %pad_maximum_fusion.4.refs_0_), channel_id=1, source_target_pairs={{0,2},{1,3},{2,0},{3,1},{4,6},{5,7},{6,4},{7,5},{8,10},{9,11},{10,... | collective-permute-start | bytes 1769480 | tf_op jit(solution)/shard_map/ppermute | solution.py:691
  81.3 19.4 %collective-permute-start.20 = (bf16[2,496,384]{2,1,0:T(8,128)(2,1)S(1)}, bf16[2,496,384]{2,1,0:T(8,128)(2,1)S(1)}, u32[]{:S(2)}, u32[]{:S(2)}) collective-permute-start(bf16[2,496,384]{2,1,0:T(8,128)(2,1)S(1)} %collective-permute-done.16), channel_id=1, source_target_pairs={{8,0},{12,4},{16,24},{20,28},{9,1},{13,5},{17,25},{21,29},{10,2},{... | collective-permute-start | bytes 2285576 | tf_op jit(solution)/shard_map/ppermute | solution.py:691
  84.6 32.2 %collective-permute-start.23 = (bf16[2,496,384]{2,1,0:T(8,128)(2,1)S(1)}, bf16[2,496,384]{2,1,0:T(8,128)(2,1)S(1)}, u32[]{:S(2)}, u32[]{:S(2)}) collective-permute-start(bf16[2,496,384]{2,1,0:T(8,128)(2,1)S(1)} %pad_maximum_fusion.3.refs_16_), channel_id=1, source_target_pairs={{0,4},{4,0},{8,12},{12,8},{16,20},{20,16},{24,28},{28,24},{1,5},{5... | collective-permute-start | bytes 2285576 | tf_op jit(solution)/shard_map/ppermute | solution.py:691
  85.5 29.6 %collective-permute-start.31 = (bf16[2,48,3072]{2,1,0:T(8,128)(2,1)S(1)}, bf16[2,48,3072]{2,1,0:T(8,128)(2,1)}, u32[]{:S(2)}, u32[]{:S(2)}) collective-permute-start(bf16[2,48,3072]{2,1,0:T(8,128)(2,1)S(1)} %collective-permute-done.10.refs_4_), channel_id=1, source_target_pairs={{0,1},{1,0},{2,3},{3,2},{4,5},{5,4},{6,7},{7,6},{8,9},{9,8},{10,11... | collective-permute-start | bytes 1769480 | tf_op jit(solution)/shard_map/ppermute | solution.py:691
  86.2 30.7 %collective-permute-start.25 = (bf16[2,496,384]{2,1,0:T(8,128)(2,1)S(1)}, bf16[2,496,384]{2,1,0:T(8,128)(2,1)}, u32[]{:S(2)}, u32[]{:S(2)}) collective-permute-start(bf16[2,496,384]{2,1,0:T(8,128)(2,1)S(1)} %pad_maximum_fusion.3.refs_16_), channel_id=1, source_target_pairs={{0,1},{1,0},{2,3},{3,2},{4,5},{5,4},{6,7},{7,6},{8,9},{9,8},{10,11... | collective-permute-start | bytes 2285576 | tf_op jit(solution)/shard_map/ppermute | solution.py:691
  115.1 19.6 %collective-permute-start.24 = (bf16[2,496,384]{2,1,0:T(8,128)(2,1)S(1)}, bf16[2,496,384]{2,1,0:T(8,128)(2,1)}, u32[]{:S(2)}, u32[]{:S(2)}) collective-permute-start(bf16[2,496,384]{2,1,0:T(8,128)(2,1)S(1)} %add.223.refs_18_), channel_id=1, source_target_pairs={{0,4},{4,0},{8,12},{12,8},{16,20},{20,16},{24,28},{28,24},{1,5},{5... | collective-permute-start | bytes 2285576 | tf_op jit(solution)/shard_map/ppermute | solution.py:691
  116.0 18.7 %collective-permute-start.26 = (bf16[2,496,384]{2,1,0:T(8,128)(2,1)S(1)}, bf16[2,496,384]{2,1,0:T(8,128)(2,1)}, u32[]{:S(2)}, u32[]{:S(2)}) collective-permute-start(bf16[2,496,384]{2,1,0:T(8,128)(2,1)S(1)} %add.223.refs_18_), channel_id=1, source_target_pairs={{0,1},{1,0},{2,3},{3,2},{4,5},{5,4},{6,7},{7,6},{8,9},{9,8},{10,11... | collective-permute-start | bytes 2285576 | tf_op jit(solution)/shard_map/ppermute | solution.py:691
  116.3 18.1 %collective-permute-start.22 = (bf16[2,48,3072]{2,1,0:T(8,128)(2,1)}, bf16[2,48,3072]{2,1,0:T(8,128)(2,1)S(1)}, u32[]{:S(2)}, u32[]{:S(2)}) collective-permute-start(bf16[2,48,3072]{2,1,0:T(8,128)(2,1)} %copy-done.34), channel_id=1, source_target_pairs={{0,2},{1,3},{2,0},{3,1},{4,6},{5,7},{6,4},{7,5},{8,10},{9,11},{10,... | collective-permute-start | bytes 1769480 | tf_op jit(solution)/shard_map/ppermute | solution.py:691
  198.3 18.8 %collective-permute-start.42 = (f32[6,4,384]{2,1,0:T(4,128)S(1)}, f32[6,4,384]{2,1,0:T(4,128)S(1)}, u32[]{:S(2)}, u32[]{:S(2)}) collective-permute-start(f32[6,4,384]{2,1,0:T(4,128)S(1)} %get-tuple-element.309), channel_id=1, source_target_pairs={{0,1},{1,2},{2,3},{4,5},{5,6},{6,7},{8,9},{9,10},{10,11},{12,13},{... | collective-permute-start | bytes 110600 | tf_op jit(solution)/shard_map/ppermute | solution.py:605
  207.5 22.0 %collective-permute-start.39 = (bf16[768,1536]{1,0:T(8,128)(2,1)}, bf16[768,1536]{1,0:T(8,128)(2,1)}, u32[]{:S(2)}, u32[]{:S(2)}) collective-permute-start(bf16[768,1536]{1,0:T(8,128)(2,1)} %convolution_convert_fusion.1), channel_id=1, source_target_pairs={{0,1},{1,0},{2,3},{3,2},{4,5},{5,4},{6,7},{7,6},{8,9},{9,8},{10,11... | collective-permute-start | bytes 7077896 | tf_op jit(solution)/shard_map/ppermute | solution.py:691
  237.4 33.8 %collective-permute-start.44 = (bf16[8,48,1536]{2,1,0:T(8,128)(2,1)}, bf16[8,48,1536]{2,1,0:T(8,128)(2,1)}, u32[]{:S(2)}, u32[]{:S(2)}) collective-permute-start(bf16[8,48,1536]{2,1,0:T(8,128)(2,1)} %get-tuple-element.221), channel_id=1, source_target_pairs={{0,2},{1,3},{2,0},{3,1},{4,6},{5,7},{6,4},{7,5},{8,10},{9,11},{10,... | collective-permute-start | bytes 3538952 | tf_op jit(solution)/shard_map/ppermute | solution.py:691
  245.0 34.8 %collective-permute-start.45 = (bf16[4,96,1536]{2,1,0:T(8,128)(2,1)}, bf16[4,96,1536]{2,1,0:T(8,128)(2,1)}, u32[]{:S(2)}, u32[]{:S(2)}) collective-permute-start(bf16[4,96,1536]{2,1,0:T(8,128)(2,1)} %get-tuple-element.222), channel_id=1, source_target_pairs={{0,4},{4,0},{8,12},{12,8},{16,20},{20,16},{24,28},{28,24},{1,5},{5... | collective-permute-start | bytes 3538952 | tf_op jit(solution)/shard_map/ppermute | solution.py:691
  284.0 40.0 %collective-permute-start.48 = (bf16[4,48,3584]{2,1,0:T(8,128)(2,1)}, bf16[4,48,3584]{2,1,0:T(8,128)(2,1)}, u32[]{:S(2)}, u32[]{:S(2)}) collective-permute-start(bf16[4,48,3584]{2,1,0:T(8,128)(2,1)} %dynamic-slice_bitcast_fusion), channel_id=1, source_target_pairs={{0,4},{4,0},{8,12},{12,8},{16,20},{20,16},{24,28},{28,24},{1,5},{5... | collective-permute-start | bytes 4128776 | tf_op jit(solution)/shard_map/ppermute | solution.py:691
  288.1 22.4 %collective-permute-start.49 = (bf16[96,1536]{1,0:T(8,128)(2,1)}, bf16[96,1536]{1,0:T(8,128)(2,1)}, u32[]{:S(2)}, u32[]{:S(2)}) collective-permute-start(bf16[96,1536]{1,0:T(8,128)(2,1)} %get-tuple-element.302), channel_id=1, source_target_pairs={{0,8},{4,12},{8,0},{12,4},{16,24},{20,28},{24,16},{28,20},{1,9},{5... | collective-permute-start | bytes 884744 | tf_op jit(solution)/shard_map/ppermute | solution.py:691
  290.3 23.6 %collective-permute-start.50 = (bf16[96,1536]{1,0:T(8,128)(2,1)S(1)}, bf16[96,1536]{1,0:T(8,128)(2,1)}, u32[]{:S(2)}, u32[]{:S(2)}) collective-permute-start(bf16[96,1536]{1,0:T(8,128)(2,1)S(1)} %get-tuple-element.301), channel_id=1, source_target_pairs={{0,16},{4,20},{8,24},{12,28},{16,0},{20,4},{24,8},{28,12},{1,17},{... | collective-permute-start | bytes 884744 | tf_op jit(solution)/shard_map/ppermute | solution.py:691
  291.3 22.6 %collective-permute-start.51 = (bf16[96,1536]{1,0:T(8,128)(2,1)S(1)}, bf16[96,1536]{1,0:T(8,128)(2,1)}, u32[]{:S(2)}, u32[]{:S(2)}) collective-permute-start(bf16[96,1536]{1,0:T(8,128)(2,1)S(1)} %get-tuple-element.300), channel_id=1, source_target_pairs={{0,24},{4,28},{8,16},{12,20},{16,8},{20,12},{24,0},{28,4},{1,25},{... | collective-permute-start | bytes 884744 | tf_op jit(solution)/shard_map/ppermute | solution.py:691
  330.9 32.1 %collective-permute-start.56 = (bf16[48,3584]{1,0:T(8,128)(2,1)S(1)}, bf16[48,3584]{1,0:T(8,128)(2,1)S(1)}, u32[]{:S(2)}, u32[]{:S(2)}) collective-permute-start(bf16[48,3584]{1,0:T(8,128)(2,1)S(1)} %get-tuple-element.299), channel_id=1, source_target_pairs={{0,8},{4,12},{8,0},{12,4},{16,24},{20,28},{24,16},{28,20},{1,9},{5... | collective-permute-start | bytes 1032200 | tf_op jit(solution)/shard_map/ppermute | solution.py:691
  331.9 31.2 %collective-permute-start.57 = (bf16[48,3584]{1,0:T(8,128)(2,1)S(1)}, bf16[48,3584]{1,0:T(8,128)(2,1)S(1)}, u32[]{:S(2)}, u32[]{:S(2)}) collective-permute-start(bf16[48,3584]{1,0:T(8,128)(2,1)S(1)} %get-tuple-element.298), channel_id=1, source_target_pairs={{0,16},{4,20},{8,24},{12,28},{16,0},{20,4},{24,8},{28,12},{1,17},{... | collective-permute-start | bytes 1032200 | tf_op jit(solution)/shard_map/ppermute | solution.py:691
  333.6 29.5 %collective-permute-start.58 = (bf16[48,3584]{1,0:T(8,128)(2,1)S(1)}, bf16[48,3584]{1,0:T(8,128)(2,1)S(1)}, u32[]{:S(2)}, u32[]{:S(2)}) collective-permute-start(bf16[48,3584]{1,0:T(8,128)(2,1)S(1)} %get-tuple-element.297), channel_id=1, source_target_pairs={{0,24},{4,28},{8,16},{12,20},{16,8},{20,12},{24,0},{28,4},{1,25},{... | collective-permute-start | bytes 1032200 | tf_op jit(solution)/shard_map/ppermute | solution.py:691
  336.8 26.3 %collective-permute-start.54 = (bf16[96,1536]{1,0:T(8,128)(2,1)S(1)}, bf16[96,1536]{1,0:T(8,128)(2,1)S(1)}, u32[]{:S(2)}, u32[]{:S(2)}) collective-permute-start(bf16[96,1536]{1,0:T(8,128)(2,1)S(1)} %fusion.19), channel_id=1, source_target_pairs={{0,2},{1,3},{2,0},{3,1},{4,6},{5,7},{6,4},{7,5},{8,10},{9,11},{10,... | collective-permute-start | bytes 884744 | tf_op jit(solution)/shard_map/ppermute | solution.py:691
  351.7 22.9 %all-to-all-start = ((bf16[4,48,1152]{2,1,0:T(8,128)(2,1)}), bf16[4,48,1152]{2,1,0:T(8,128)(2,1)S(1)}, u32[]{:S(2)}, u32[]{:S(2)}) async-start(bf16[4,48,1152]{2,1,0:T(8,128)(2,1)} %fusion.12), calls=%async_computation.1 | async-start | bytes 884736 | tf_op jit(solution)/shard_map/all_to_all | solution.py:724
  (111 other events, 1370.1 us)
Sparse Core Ops, SparseCore 0:
  246.6 82.2 reduce-scatter.1
